TPU v7x, 128 devices: a whole 4x4x4 slice. The times are simulated.
128 devices in a mesh: gx: 16 (over x, y), yz: 8 (over z, core).
Axes of the slice: x: 4, y: 4, z: 4, core: 2. Of those that a mesh axis runs over, the one named last changes fastest.
Arguments:
- populations: bfloat16 [19, 256, 256, 128], P(None, 'gx', 'yz'), may hold values from -0.29882812 to 0.29882812
- levels: int32 [2048], replicated, may hold values from 0 to 1
- refine_flags: int32 [2048], replicated, may hold values from 0 to 2, as said below
- new_owner: int32 [2048], replicated, may hold values from 0 to 127, as said below
Outputs:
- migrated: bfloat16 [3072, 19, 4096], P(('gx', 'yz'))
Inputs may be any that keep to these rules, and one draw needn't show every extreme that they name: On every device exactly 8 of the blocks it holds have refine_flags 1 or 2; all other blocks have 0. `new_owner`: A block with refine_flags 0 keeps the device that holds it. No device receives more than one flagged block from any one device, itself included. After migration a quarter of the devices hold exactly 24 blocks, a quarter exactly 16, and the rest exactly 16 minus half of 8.
All inputs are finite; a program needn't handle non-finite values.
Results may differ from a plain program's by a relative error of at most 0.0049.
Values may be sent and summed in bfloat16 or wider, within the bound.
No kernel may reach another device: no remote copies, remote signals or barrier semaphores. Data moves between devices by JAX's collectives and lax.ppermute only.
A program may use at most 192 MiB of HBM per device.

v0:
```python
import jax
import jax.numpy as jnp
from jax import lax
from jax.sharding import PartitionSpec as P

BS = 16
HALF = 8
BX = 1
BY = 2
BZ = 8
MIG = 8
STEPS = 2
BLK = 16
CAP = 24


VELOCITY_LIST = [
    [0, 0, 0],
    [1, 0, 0],
    [-1, 0, 0],
    [0, 1, 0],
    [0, -1, 0],
    [0, 0, 1],
    [0, 0, -1],
    [1, 1, 0],
    [-1, -1, 0],
    [1, -1, 0],
    [-1, 1, 0],
    [1, 0, 1],
    [-1, 0, -1],
    [1, 0, -1],
    [-1, 0, 1],
    [0, 1, 1],
    [0, -1, -1],
    [0, 1, -1],
    [0, -1, 1],
]
WEIGHT_LIST = [1.0 / 3.0] + [1.0 / 18.0] * 6 + [1.0 / 36.0] * 12
OPPOSITE_LIST = [0, 2, 1, 4, 3, 6, 5, 8, 7, 10, 9, 12, 11, 14, 13, 16, 15, 18, 17]


def padded(block, sides, width):
    for axis, dim in sides:
        count = lax.axis_size(axis)
        forward = [(i, i + 1) for i in range(count - 1)]
        forward.append((count - 1, 0))
        backward = [(target, source) for source, target in forward]
        low = lax.ppermute(
            lax.slice_in_dim(block, block.shape[dim] - width, None, axis=dim), axis, forward
        )
        high = lax.ppermute(lax.slice_in_dim(block, 0, width, axis=dim), axis, backward)
        block = jnp.concatenate([low, block, high], axis=dim)
    return block


def relax_rates(levels):
    return 1.0 / (0.5 + jnp.power(0.5, levels.astype(jnp.float32)))


def collide(current, relax_field):
    values = current.astype(jnp.float32)
    weights = jnp.asarray(WEIGHT_LIST, jnp.float32).reshape((19,) + (1,) * (values.ndim - 1))
    speeds = jnp.asarray(VELOCITY_LIST, jnp.float32)
    weighted = values * weights
    density = 1.0 + jnp.sum(weighted, axis=0)
    momentum = jnp.einsum("ic,i...->c...", speeds, weighted, precision=lax.Precision.HIGHEST)
    velocity = momentum / density
    speed_square = jnp.sum(velocity * velocity, axis=0)
    project = jnp.einsum("ic,c...->i...", speeds, velocity, precision=lax.Precision.HIGHEST)
    balance = density * (1.0 + 3.0 * project + 4.5 * project * project - 1.5 * speed_square) - 1.0
    return values - relax_field * (values - balance)


def propagate(collided):
    cells_pipe = collided.shape[1] - 2
    cells_cross = collided.shape[2] - 2
    interior = collided[:, 1:-1, 1:-1, :]
    results = []
    for direction in range(19):
        delta_first, delta_second, delta_third = VELOCITY_LIST[direction]
        shifted = collided[
            direction,
            1 - delta_first : 1 - delta_first + cells_pipe,
            1 - delta_second : 1 - delta_second + cells_cross,
            :,
        ]
        mirror = interior[OPPOSITE_LIST[direction]]
        if delta_third == 1:
            shifted = jnp.concatenate([mirror[:, :, :1], shifted[:, :, :-1]], axis=2)
        elif delta_third == -1:
            shifted = jnp.concatenate([shifted[:, :, 1:], mirror[:, :, -1:]], axis=2)
        results.append(shifted)
    return jnp.stack(results)


def restrict(blocks):
    count = blocks.shape[0]
    values = blocks.astype(jnp.float32).reshape(count, 19, HALF, 2, HALF, 2, HALF, 2)
    return (
        (jnp.sum(values, axis=(3, 5, 7)) * 0.125)
        .reshape(count, 19, HALF * HALF * HALF)
        .astype(jnp.bfloat16)
    )


def prolong(coarse, flag_kinds):
    count = coarse.shape[0]
    fine_index = jnp.arange(BS, dtype=jnp.int32)
    parent = fine_index // 2
    neighbor_index = jnp.clip(jnp.where(fine_index % 2 == 0, parent - 1, parent + 1), 0, HALF - 1)
    coarse_index = jnp.arange(HALF, dtype=jnp.int32)
    inject = (parent[:, None] == coarse_index[None, :]).astype(jnp.float32)
    linear = 0.75 * inject + 0.25 * (neighbor_index[:, None] == coarse_index[None, :]).astype(
        jnp.float32
    )
    matrices = jnp.where((flag_kinds == 2)[:, None, None], linear[None], inject[None])
    values = coarse.astype(jnp.float32).reshape(count, 19, HALF, HALF, HALF)
    values = jnp.einsum("nah,nphij->npaij", matrices, values, precision=lax.Precision.HIGHEST)
    values = jnp.einsum("nbi,npaij->npabj", matrices, values, precision=lax.Precision.HIGHEST)
    values = jnp.einsum("ncj,npabj->npabc", matrices, values, precision=lax.Precision.HIGHEST)
    return values.reshape(count, 19, BS * BS * BS).astype(jnp.bfloat16)


def body(populations, levels, refine_flags, new_owner):
    slab_count = lax.axis_size("gx")
    column_count = lax.axis_size("yz")
    slab_index = lax.axis_index("gx")
    column_index = lax.axis_index("yz")
    myself = slab_index * column_count + column_index
    device_total = slab_count * column_count
    block_total = new_owner.shape[0]
    cells_pipe = populations.shape[1]
    cells_cross = populations.shape[2]
    blocks_pipe = BX * slab_count
    blocks_cross = BY * column_count
    grid_pipe = (slab_index * BX + jnp.arange(-1, BX + 1, dtype=jnp.int32)) % blocks_pipe
    grid_cross = (column_index * BY + jnp.arange(-1, BY + 1, dtype=jnp.int32)) % blocks_cross
    grid_ids = (grid_pipe[:, None, None] * blocks_cross + grid_cross[None, :, None]) * BZ
    grid_ids = grid_ids + jnp.arange(BZ, dtype=jnp.int32)[None, None, :]
    block_rates = relax_rates(jnp.take(levels, grid_ids))
    cell_rates = jnp.repeat(jnp.repeat(jnp.repeat(block_rates, BS, 0), BS, 1), BS, 2)
    padded_rates = cell_rates[BS - 1 : BS + cells_pipe + 1, BS - 1 : BS + cells_cross + 1, :]
    interior_rates = padded_rates[1:-1, 1:-1, :]
    current = populations
    for sweep_number in range(STEPS):
        collided_inner = collide(current, interior_rates).astype(jnp.bfloat16)
        collided = padded(collided_inner, (("gx", 1), ("yz", 2)), 1)
        current = propagate(collided)
    local_blocks = current.reshape(19, BX, BS, BY, BS, BZ, BS)
    local_blocks = jnp.transpose(local_blocks, (1, 3, 5, 0, 2, 4, 6)).reshape(BLK, 19, BS * BS * BS)
    local_pipe = slab_index * BX + jnp.arange(BX, dtype=jnp.int32)
    local_cross = column_index * BY + jnp.arange(BY, dtype=jnp.int32)
    local_global = (local_pipe[:, None, None] * blocks_cross + local_cross[None, :, None]) * BZ
    local_global = (local_global + jnp.arange(BZ, dtype=jnp.int32)[None, None, :]).reshape(BLK)
    flag_local = jnp.take(refine_flags, local_global)
    chosen = jnp.nonzero(flag_local != 0, size=MIG, fill_value=0)[0].astype(jnp.int32)
    chosen_kinds = jnp.take(flag_local, chosen)
    targets = jnp.take(new_owner, jnp.take(local_global, chosen))
    coarse = restrict(jnp.take(local_blocks, chosen, axis=0))
    device_range = jnp.arange(device_total, dtype=jnp.int32)
    matches = targets[None, :] == device_range[:, None]
    chosen_slot = jnp.sum(jnp.where(matches, jnp.arange(MIG, dtype=jnp.int32)[None, :], 0), axis=1)
    present = jnp.any(matches, axis=1)
    arriving = (refine_flags != 0) & (new_owner == myself)
    arrival_ids = jnp.nonzero(arriving, size=2 * MIG, fill_value=0)[0].astype(jnp.int32)
    arrival_pipe = arrival_ids // (blocks_cross * BZ)
    arrival_cross = arrival_ids // BZ % blocks_cross
    arrival_source = arrival_pipe // BX * column_count + arrival_cross // BY
    empty_value = jnp.zeros((), jnp.bfloat16)
    refined = prolong(coarse, chosen_kinds)
    outgoing = jnp.where(
        present[:, None, None], jnp.take(refined, chosen_slot, axis=0), empty_value
    )
    incoming = lax.all_to_all(outgoing, ("gx", "yz"), split_axis=0, concat_axis=0, tiled=True)
    arrivals = jnp.take(incoming, arrival_source, axis=0)
    owned_ids = jnp.nonzero(new_owner == myself, size=CAP, fill_value=block_total)[0].astype(
        jnp.int32
    )
    occupied = owned_ids < block_total
    safe_ids = jnp.where(occupied, owned_ids, 0)
    owned_flagged = (jnp.take(refine_flags, safe_ids) != 0) & occupied
    arrival_rank = jnp.cumsum(owned_flagged.astype(jnp.int32)) - 1
    owned_pipe = safe_ids // (blocks_cross * BZ)
    owned_cross = safe_ids // BZ % blocks_cross
    local_index = (owned_pipe % BX * BY + owned_cross % BY) * BZ + safe_ids % BZ
    source = jnp.where(owned_flagged, BLK + arrival_rank, local_index)
    block_pool = jnp.concatenate([local_blocks, arrivals], axis=0)
    migrated = jnp.where(occupied[:, None, None], jnp.take(block_pool, source, axis=0), empty_value)
    return migrated


def solution(mesh):
    placed = (P(None, "gx", "yz", None), P(), P(), P())
    return jax.shard_map(
        body, mesh=mesh, in_specs=placed, out_specs=P(("gx", "yz"), None, None), check_vma=False
    )
```

profile of v0, /device:TPU:2, one launch (start us, length us, event | category | flops | bytes accessed | tf_op | source)
XLA Modules:
  0.0 829.9 jit_solution(6901249111036378466)
XLA Ops:
  8.2 4.0 fusion.3
  12.2 8.2 fusion.32
  20.5 9.2 %fusion.10 = bf16[19,16,32,128]{3,0,2,1:T(8,128)(2,1)S(1)} fusion(f32[16,32,128]{2,1,0:T(8,128)S(1)} %broadcast_multiply_fusion.1, f32[16,32,128]{2,1,0:T(8,128)S(1)} %broadcast_add_fusion.1, f32[16,32,128]{2,1,0:T(8,128)S(1)} %copy.384, bf16[19,16,32,128]{3,2,1,0:T(8,128)(2,1)S(1)} %copy-done.22, f32[19,3,1,1]{0,1,3,2:T(4,128)S(1)} %copy-done.53, ...), kind=kOutput, calls=%fused_computation.31 | convolution fusion | flops 61014016 | bytes 6553828 | tf_op jit(solution)/shard_map/ic,c...->i.../dot_general | solution.py:69
  32.3 2.6 collective-permute-start.1
  34.9 2.8 fusion.108
  48.6 15.2 %scatter_custom_fusion = s32[24]{0:T(128)S(1)} fusion(s32[2048]{0:T(1024)S(1)} %bitcast.270, s32[2048]{0:T(1024)S(1)} %broadcast.1928, s32[]{:T(128)} %constant.398.clone.1), kind=kCustom, calls=%fused_computation.404 | custom fusion | flops 2048 | bytes 100 | tf_op jit(solution)/shard_map/scatter-add | solution.py:176
  78.7 2.9 collective-permute-start.3
  84.0 4.6 pad_maximum_fusion.13
  88.6 5.3 pad_maximum_fusion.21
  95.2 4.4 pad_maximum_fusion.16
  107.9 15.3 %stack.94 = bf16[19,16,32,128]{3,0,2,1:T(8,128)(2,1)S(1)} concatenate(bf16[1,16,32,128]{3,0,2,1:T(2,128)(2,1)S(1)} %copy-done.24, bf16[1,16,32,128]{3,0,2,1:T(2,128)(2,1)} %get-tuple-element.62, bf16[1,16,32,128]{3,0,2,1:T(2,128)(2,1)} %get-tuple-element.63, bf16[1,16,32,128]{3,0,2,1:T(2,128)(2,1)} %get-tuple-element.60, bf16[1,16,32,128]{3,0,2,1:T(2,128)(2,1)} %get-tuple-element.61, ...), dimensions={0} | concatenate | bytes 4980736 | tf_op jit(solution)/shard_map/stack | solution.py:93
  123.2 2.6 fusion.5
  125.9 5.8 fusion.30
  131.7 9.7 %fusion.16 = bf16[19,16,32,128]{3,0,2,1:T(8,128)(2,1)S(1)} fusion(bf16[19,16,32,128]{3,0,2,1:T(8,128)(2,1)} %copy-done.6, f32[16,32,128]{2,1,0:T(8,128)S(1)} %broadcast_multiply_fusion, f32[16,32,128]{2,1,0:T(8,128)S(1)} %broadcast_add_fusion, f32[16,32,128]{2,1,0:T(8,128)S(1)} %copy-done.38, f32[19,3,1,1]{0,1,3,2:T(4,128)S(1)} %copy-done.54, ...), kind=kOutput, calls=%fused_computation.37 | convolution fusion | flops 61014016 | bytes 6553828 | tf_op jit(solution)/shard_map/ic,c...->i.../dot_general | solution.py:69
  142.2 4.5 collective-permute-start.5
  146.8 2.7 fusion.106
  151.8 2.6 stack.100
  155.1 2.5 collective-permute-start.7
  159.3 2.5 stack.101
  168.6 8.2 maximum_reduce_fusion.1
  176.7 2.6 stack.99
  179.3 9.9 %maximum_reduce_fusion = (bf16[16,32,128]{2,1,0:T(8,128)(2,1)}, bf16[16,32,128]{2,1,0:T(8,128)(2,1)}, bf16[16,32,128]{2,1,0:T(8,128)(2,1)}, bf16[16,32,128]{2,1,...) fusion(bf16[19,18,1,128]{3,0,2,1:T(8,128)(2,1)} %collective-per, ...), kind=kLoop, calls=%fused_computation.74 | loop fusion | flops 2097152 | bytes 5461504 | tf_op jit(solution)/shard_map/slice | solution.py:81
  194.0 2.5 stack.96
  196.6 2.6 stack.97
  199.2 2.5 stack.98
  201.7 2.5 stack.102
  204.3 2.8 stack.103
  207.1 2.5 stack.104
  209.6 2.6 stack.105
  212.2 4.7 pad_maximum_fusion.1
  260.4 17.9 %copy.410 = bf16[1,2,8,19,16,16,16]{6,5,4,3,2,1,0:T(8,128)(2,1)} copy(bf16[1,2,8,19,16,16,16]{6,2,5,1,4,0,3:T(8,128)(2,1)} %bitcast.225) | data formatting | bytes 4980736 | tf_op jit(solution)/shard_map/reshape | solution.py:150
  278.4 34.1 %reshape.1238 = bf16[16,19,4096]{2,1,0:T(8,128)(2,1)S(1)} reshape(bf16[1,2,8,19,16,16,16]{6,5,4,3,2,1,0:T(8,128)(2,1)} %copy.410) | data formatting | bytes 4980736 | tf_op jit(solution)/shard_map/reshape | solution.py:150
  314.6 8.9 %copy.401 = bf16[8,19,4096]{1,0,2:T(8,128)(2,1)} copy(bf16[8,19,4096]{2,1,0:T(8,128)(2,1)} %gather_fusion.4) | data formatting | bytes 2490368 | tf_op jit(solution)/shard_map/jit(_take)/gather | solution.py:159
  323.6 6.0 convert_reduce_fusion
  329.8 2.7 convolution_bitcast_fusion
  332.5 9.7 %fusion.23 = f32[8,19,16,16,8]{1,3,4,2,0:T(8,128)S(1)} fusion(f32[8,19,16,8,8]{1,2,4,3,0:T(8,128)S(1)} %convolution_bitcast_fusion, f32[16,8]{0,1:T(8,128)S(1)} %fusion.78, f32[16,8]{0,1:T(8,128)S(1)} %select_add_fusion, pred[8]{0:T(512)(128)(4,1)S(1)} %copy-done.41), kind=kOutput, calls=%fused_computation.46 | convolution fusion | flops 29885440 | bytes 1868808 | tf_op jit(solution)/shard_map/nbi,npaij->npabj/dot_general | solution.py:119
  342.2 15.9 %fusion.6 = bf16[8,19,16,16,16]{1,4,3,2,0:T(8,128)(2,1)} fusion(f32[8,19,16,16,8]{1,3,4,2,0:T(8,128)S(1)} %fusion.23, f32[16,8]{0,1:T(8,128)S(1)} %fusion.78, f32[16,8]{0,1:T(8,128)S(1)} %select_add_fusion, pred[8]{0:T(512)(128)(4,1)S(1)} %copy-done.41), kind=kOutput, calls=%fused_computation.29 | convolution fusion | flops 60392448 | bytes 2491400 | tf_op jit(solution)/shard_map/ncj,npabj->npabc/dot_general | solution.py:120
  358.1 7.1 copy.405
  365.3 10.7 %gather_fusion.5 = bf16[128,19,4096]{2,1,0:T(8,128)(2,1)} fusion(bf16[8,19,4096]{2,1,0:T(8,128)(2,1)S(1)} %copy.405, s32[1024]{0:T(1024)} %get-tuple-element.95), kind=kCustom, calls=%fused_computation.7 | custom fusion | bytes 39846400 | tf_op jit(solution)/shard_map/jit(_take)/gather | solution.py:172
  375.9 21.9 %select_select_fusion = bf16[128,19,4096]{2,1,0:T(8,128)(2,1)} fusion(bf16[128,19,4096]{2,1,0:T(8,128)(2,1)} %gather_fusion.5, pred[128]{0:T(512)(128)(4,1)S(1)} %copy-done.51, pred[128]{0:T(512)(128)(4,1)S(1)} %copy-done.52), kind=kLoop, calls=%fused_computation.13 | loop fusion | flops 19922944 | bytes 39846144 | tf_op jit(solution)/shard_map/jit(_where)/select_n | solution.py:171
  397.8 8.4 %all-to-all-start = ((bf16[128,19,4096]{2,1,0:T(8,128)(2,1)}), bf16[128,19,4096]{2,1,0:T(8,128)(2,1)}, u32[]{:S(2)}, u32[]{:S(2)}) async-start(bf16[128,19,4096]{2,1,0:T(8,128)(2,1)} %select_select_fusion), calls=%async_computation | async-start | bytes 50331648 | tf_op jit(solution)/shard_map/all_to_all | solution.py:174
  407.5 15.0 %scatter_custom_fusion.1 = s32[16]{0:T(128)S(1)} fusion(s32[2048]{0:T(1024)S(1)} %bitcast.271, s32[2048]{0:T(1024)} %copy-done.42, s32[]{:T(128)} %constant.398.clone.1), kind=kCustom, calls=%fused_computation.402 | custom fusion | flops 2048 | bytes 576 | tf_op jit(solution)/shard_map/scatter-add | solution.py:165
  424.9 375.5 %all-to-all-done = bf16[128,19,4096]{2,1,0:T(8,128)(2,1)} async-done(((bf16[128,19,4096]{2,1,0:T(8,128)(2,1)}), bf16[128,19,4096]{2,1,0:T(8,128)(2,1)}, u32[]{:S(2)}, u32[]{:S(2)}) %all-to-all-start) | async-done | bytes 19922976 | tf_op jit(solution)/shard_map/all_to_all | solution.py:174
  800.4 10.6 %gather_fusion.6 = bf16[16,19,4096]{2,1,0:T(8,128)(2,1)} fusion(bf16[128,19,4096]{2,1,0:T(8,128)(2,1)} %all-to-all-done, s32[1024]{0:T(1024)S(1)} %pad_clamp_fusion.1), kind=kCustom, calls=%fused_computation.8 | custom fusion | bytes 4980800 | tf_op jit(solution)/shard_map/jit(_take)/gather | solution.py:175
  813.3 3.4 pad_maximum_fusion
  816.7 6.1 gather_fusion.7
  822.8 2.9 select_select_fusion.1
  825.7 4.0 copy.407
  (338 shorter events, 117.0 us)
Async XLA Ops:
  8.2 12.3 %copy-start.37 = (f32[16,32,128]{2,1,0:T(8,128)}, f32[16,32,128]{2,1,0:T(8,128)S(1)}, u32[]{:S(2)}) copy-start(f32[16,32,128]{2,1,0:T(8,128)S(1)} %copy.384) | copy-start | bytes 786436
  12.2 8.2 copy-start.22
  20.5 19.0 %copy-start.3 = (s32[2048]{0:T(1024)S(1)}, s32[2048]{0:T(1024)}, u32[]{:S(2)}) copy-start(s32[2048]{0:T(1024)} %param.13) | copy-start | bytes 24580
  29.7 35.0 %copy-start.2 = (s32[2048]{0:T(1024)S(1)}, s32[2048]{0:T(1024)}, u32[]{:S(2)}) copy-start(s32[2048]{0:T(1024)} %param.12) | copy-start | bytes 24580
  30.5 47.5 %collective-permute-start = (bf16[19,1,32,128]{3,0,2,1:T(8,128)(2,1)}, bf16[19,1,32,128]{3,0,2,1:T(8,128)(2,1)S(1)}, u32[]{:S(2)}, u32[]{:S(2)}) collective-permute-start(bf16[19,1,32,128]{3,0,2,1:T(8,128)(2,1)} %get-tuple-element.88), channel_id=1, source_target_pairs={{0,8},{8,16},{16,24},{24,32},{32,40},{40,48},{48,56},{56,64},{64,7... | collective-permute-start | bytes 466952 | tf_op jit(solution)/shard_map/ppermute | solution.py:48
  32.3 45.7 %collective-permute-start.1 = (bf16[19,1,32,128]{3,0,2,1:T(8,128)(2,1)}, bf16[19,1,32,128]{3,0,2,1:T(8,128)(2,1)}, u32[]{:S(2)}, u32[]{:S(2)}) collective-permute-start(bf16[19,1,32,128]{3,0,2,1:T(8,128)(2,1)} %get-tuple-element.87), channel_id=1, source_target_pairs={{8,0},{16,8},{24,16},{32,24},{40,32},{48,40},{56,48},{64,56},{72,6... | collective-permute-start | bytes 466952 | tf_op jit(solution)/shard_map/ppermute | solution.py:51
  48.6 15.2 %copy-start.42 = (s32[2048]{0:T(1024)}, s32[2048]{0:T(1024)S(1)}, u32[]{:S(2)}) copy-start(s32[2048]{0:T(1024)S(1)} %broadcast.1928) | copy-start | bytes 24580
  65.4 7.5 copy-start.43
  68.9 12.7 %copy-start.50 = (s32[128]{0:T(128)S(1)}, s32[128]{0:T(128)}, u32[]{:S(2)}) copy-start(s32[128]{0:T(128)} %fusion.95) | copy-start | bytes 1540
  78.7 5.3 collective-permute-start.3
  82.3 6.3 collective-permute-start.2
  95.2 9.4 %copy-start.36 = (bf16[16,32,1]{2,1,0:T(8,128)(2,1)S(1)}, bf16[16,32,1]{2,1,0:T(8,128)(2,1)}, u32[]{:S(2)}) copy-start(bf16[16,32,1]{2,1,0:T(8,128)(2,1)} %slice.508) | copy-start | bytes 3076
  95.2 10.6 %copy-start.35 = (bf16[16,32,1]{2,1,0:T(8,128)(2,1)S(1)}, bf16[16,32,1]{2,1,0:T(8,128)(2,1)}, u32[]{:S(2)}) copy-start(bf16[16,32,1]{2,1,0:T(8,128)(2,1)} %slice.505) | copy-start | bytes 3076
  99.6 8.3 %copy-start.24 = (bf16[1,16,32,128]{3,0,2,1:T(2,128)(2,1)S(1)}, bf16[1,16,32,128]{3,0,2,1:T(2,128)(2,1)}, u32[]{:S(2)}) copy-start(bf16[1,16,32,128]{3,0,2,1:T(2,128)(2,1)} %get-tuple-element.86) | copy-start | bytes 393220
  107.0 18.9 %copy-start.46 = (f32[19]{0:T(128)S(1)}, f32[19]{0:T(128)}, u32[]{:S(2)}) copy-start(f32[19]{0:T(128)} %constant.427.clone) | copy-start | bytes 232
  107.0 18.9 %copy-start.54 = (f32[19,3,1,1]{0,1,3,2:T(4,128)S(1)}, f32[19,3,1,1]{0,1,3,2:T(4,128)}, u32[]{:S(2)}) copy-start(f32[19,3,1,1]{0,1,3,2:T(4,128)} %constant.429) | copy-start | bytes 688
  123.2 8.5 %copy-start.6 = (bf16[19,16,32,128]{3,0,2,1:T(8,128)(2,1)}, bf16[19,16,32,128]{3,0,2,1:T(8,128)(2,1)S(1)}, u32[]{:S(2)}) copy-start(bf16[19,16,32,128]{3,0,2,1:T(8,128)(2,1)S(1)} %stack.94) | copy-start | bytes 7471108
  142.2 12.1 %collective-permute-start.4 = (bf16[19,1,32,128]{3,0,2,1:T(8,128)(2,1)}, bf16[19,1,32,128]{3,0,2,1:T(8,128)(2,1)S(1)}, u32[]{:S(2)}, u32[]{:S(2)}) collective-permute-start(bf16[19,1,32,128]{3,0,2,1:T(8,128)(2,1)} %get-tuple-element.74), channel_id=1, source_target_pairs={{0,8},{8,16},{16,24},{24,32},{32,40},{40,48},{48,56},{56,64},{64,7... | collective-permute-start | bytes 466952 | tf_op jit(solution)/shard_map/ppermute | solution.py:48
  142.2 12.1 %collective-permute-start.5 = (bf16[19,1,32,128]{3,0,2,1:T(8,128)(2,1)}, bf16[19,1,32,128]{3,0,2,1:T(8,128)(2,1)S(1)}, u32[]{:S(2)}, u32[]{:S(2)}) collective-permute-start(bf16[19,1,32,128]{3,0,2,1:T(8,128)(2,1)} %get-tuple-element.75), channel_id=1, source_target_pairs={{8,0},{16,8},{24,16},{32,24},{40,32},{48,40},{56,48},{64,56},{72,6... | collective-permute-start | bytes 466952 | tf_op jit(solution)/shard_map/ppermute | solution.py:51
  155.1 13.5 %collective-permute-start.7 = (bf16[19,18,1,128]{3,0,2,1:T(8,128)(2,1)}, bf16[19,18,1,128]{3,0,2,1:T(8,128)(2,1)}, u32[]{:S(2)}, u32[]{:S(2)}) collective-permute-start(bf16[19,18,1,128]{3,0,2,1:T(8,128)(2,1)} %get-tuple-element.46), channel_id=1, source_target_pairs={{1,0},{2,1},{3,2},{4,3},{5,4},{6,5},{7,6},{0,7},{9,8},{10,9},{11,1... | collective-permute-start | bytes 262664 | tf_op jit(solution)/shard_map/ppermute | solution.py:51
  168.6 10.7 %collective-permute-start.6 = (bf16[19,18,1,128]{3,0,2,1:T(8,128)(2,1)}, bf16[19,18,1,128]{3,0,2,1:T(8,128)(2,1)}, u32[]{:S(2)}, u32[]{:S(2)}) collective-permute-start(bf16[19,18,1,128]{3,0,2,1:T(8,128)(2,1)} %get-tuple-element.47), channel_id=1, source_target_pairs={{0,1},{1,2},{2,3},{3,4},{4,5},{5,6},{6,7},{7,0},{8,9},{9,10},{10,1... | collective-permute-start | bytes 262664 | tf_op jit(solution)/shard_map/ppermute | solution.py:48
  216.9 10.5 %copy-start.28 = (bf16[1,16,32,128]{3,0,2,1:T(2,128)(2,1)S(1)}, bf16[1,16,32,128]{3,0,2,1:T(2,128)(2,1)}, u32[]{:S(2)}) copy-start(bf16[1,16,32,128]{3,0,2,1:T(2,128)(2,1)} %get-tuple-element.53) | copy-start | bytes 393220
  216.9 10.5 %copy-start.34 = (bf16[1,16,32,128]{3,2,0,1:T(8,128)(2,1)S(1)}, bf16[1,16,32,128]{3,2,0,1:T(8,128)(2,1)}, u32[]{:S(2)}) copy-start(bf16[1,16,32,128]{3,2,0,1:T(8,128)(2,1)} %copy.513) | copy-start | bytes 393220
  216.9 12.3 %copy-start.33 = (bf16[1,16,32,128]{3,0,2,1:T(2,128)(2,1)S(1)}, bf16[1,16,32,128]{3,0,2,1:T(2,128)(2,1)}, u32[]{:S(2)}) copy-start(bf16[1,16,32,128]{3,0,2,1:T(2,128)(2,1)} %get-tuple-element.44) | copy-start | bytes 393220
  216.9 12.3 %copy-start.29 = (bf16[1,16,32,128]{3,0,2,1:T(2,128)(2,1)S(1)}, bf16[1,16,32,128]{3,0,2,1:T(2,128)(2,1)}, u32[]{:S(2)}) copy-start(bf16[1,16,32,128]{3,0,2,1:T(2,128)(2,1)} %get-tuple-element.67) | copy-start | bytes 393220
  216.9 14.1 %copy-start.32 = (bf16[1,16,32,128]{3,0,2,1:T(2,128)(2,1)S(1)}, bf16[1,16,32,128]{3,0,2,1:T(2,128)(2,1)}, u32[]{:S(2)}) copy-start(bf16[1,16,32,128]{3,0,2,1:T(2,128)(2,1)} %get-tuple-element.33) | copy-start | bytes 393220
  216.9 14.2 %copy-start.26 = (bf16[1,16,32,128]{3,0,2,1:T(2,128)(2,1)S(1)}, bf16[1,16,32,128]{3,0,2,1:T(2,128)(2,1)}, u32[]{:S(2)}) copy-start(bf16[1,16,32,128]{3,0,2,1:T(2,128)(2,1)} %get-tuple-element.66) | copy-start | bytes 393220
  218.1 15.0 %copy-start.31 = (bf16[1,16,32,128]{3,0,2,1:T(2,128)(2,1)S(1)}, bf16[1,16,32,128]{3,0,2,1:T(2,128)(2,1)}, u32[]{:S(2)}) copy-start(bf16[1,16,32,128]{3,0,2,1:T(2,128)(2,1)} %get-tuple-element.45) | copy-start | bytes 393220
  219.7 13.5 %copy-start.30 = (bf16[1,16,32,128]{3,0,2,1:T(2,128)(2,1)S(1)}, bf16[1,16,32,128]{3,0,2,1:T(2,128)(2,1)}, u32[]{:S(2)}) copy-start(bf16[1,16,32,128]{3,0,2,1:T(2,128)(2,1)} %get-tuple-element.65) | copy-start | bytes 393220
  223.5 11.7 %copy-start.27 = (bf16[1,16,32,128]{3,0,2,1:T(2,128)(2,1)S(1)}, bf16[1,16,32,128]{3,0,2,1:T(2,128)(2,1)}, u32[]{:S(2)}) copy-start(bf16[1,16,32,128]{3,0,2,1:T(2,128)(2,1)} %get-tuple-element.32) | copy-start | bytes 393220
  223.5 11.7 %copy-start.25 = (bf16[1,16,32,128]{3,0,2,1:T(2,128)(2,1)S(1)}, bf16[1,16,32,128]{3,0,2,1:T(2,128)(2,1)}, u32[]{:S(2)}) copy-start(bf16[1,16,32,128]{3,0,2,1:T(2,128)(2,1)} %get-tuple-element.64) | copy-start | bytes 393220
  231.4 12.9 %copy-start.9 = (bf16[1,1,16,2,16,8,16]{6,5,4,3,2,1,0:T(8,128)(2,1)S(1)}, bf16[1,1,16,2,16,8,16]{6,5,4,3,2,1,0:T(8,128)(2,1)}, u32[]{:S(2)}) copy-start(bf16[1,1,16,2,16,8,16]{6,5,4,3,2,1,0:T(8,128)(2,1)} %stack.99) | copy-start | bytes 393220
  233.3 12.1 %copy-start.7 = (bf16[1,1,16,2,16,8,16]{6,5,4,3,2,1,0:T(8,128)(2,1)S(1)}, bf16[1,1,16,2,16,8,16]{6,5,4,3,2,1,0:T(8,128)(2,1)}, u32[]{:S(2)}) copy-start(bf16[1,1,16,2,16,8,16]{6,5,4,3,2,1,0:T(8,128)(2,1)} %stack.100) | copy-start | bytes 393220
  235.2 11.3 %copy-start.8 = (bf16[1,1,16,2,16,8,16]{6,5,4,3,2,1,0:T(8,128)(2,1)S(1)}, bf16[1,1,16,2,16,8,16]{6,5,4,3,2,1,0:T(8,128)(2,1)}, u32[]{:S(2)}) copy-start(bf16[1,1,16,2,16,8,16]{6,5,4,3,2,1,0:T(8,128)(2,1)} %stack.101) | copy-start | bytes 393220
  237.0 10.5 %copy-start.13 = (bf16[1,1,16,2,16,8,16]{6,5,4,3,2,1,0:T(8,128)(2,1)S(1)}, bf16[1,1,16,2,16,8,16]{6,5,4,3,2,1,0:T(8,128)(2,1)}, u32[]{:S(2)}) copy-start(bf16[1,1,16,2,16,8,16]{6,5,4,3,2,1,0:T(8,128)(2,1)} %stack.102) | copy-start | bytes 393220
  239.5 9.1 %copy-start.12 = (bf16[1,1,16,2,16,8,16]{6,5,4,3,2,1,0:T(8,128)(2,1)S(1)}, bf16[1,1,16,2,16,8,16]{6,5,4,3,2,1,0:T(8,128)(2,1)}, u32[]{:S(2)}) copy-start(bf16[1,1,16,2,16,8,16]{6,5,4,3,2,1,0:T(8,128)(2,1)} %stack.103) | copy-start | bytes 393220
  241.9 7.8 copy-start.11
  312.4 11.1 %copy-start.4 = (bf16[16,19,4096]{2,1,0:T(8,128)(2,1)}, bf16[16,19,4096]{2,1,0:T(8,128)(2,1)S(1)}, u32[]{:S(2)}) copy-start(bf16[16,19,4096]{2,1,0:T(8,128)(2,1)S(1)} %reshape.1238) | copy-start | bytes 7471108
  312.5 11.1 %copy-start.49 = (pred[8]{0:T(512)(128)(4,1)S(1)}, pred[8]{0:T(512)(128)(4,1)}, u32[]{:S(2)}) copy-start(pred[8]{0:T(512)(128)(4,1)} %get-tuple-element.30) | copy-start | bytes 28
  365.2 10.7 %copy-start.51 = (pred[128]{0:T(512)(128)(4,1)S(1)}, pred[128]{0:T(512)(128)(4,1)}, u32[]{:S(2)}) copy-start(pred[128]{0:T(512)(128)(4,1)} %compare_and_fusion.3) | copy-start | bytes 388
  365.3 10.7 %copy-start.52 = (pred[128]{0:T(512)(128)(4,1)S(1)}, pred[128]{0:T(512)(128)(4,1)}, u32[]{:S(2)}) copy-start(pred[128]{0:T(512)(128)(4,1)} %fusion.79) | copy-start | bytes 388
  397.8 8.4 %copy-start.40 = (pred[2048]{0:T(1024)(128)(4,1)S(1)}, pred[2048]{0:T(1024)(128)(4,1)}, u32[]{:S(2)}) copy-start(pred[2048]{0:T(1024)(128)(4,1)} %copy-done.39) | copy-start | bytes 6148
  397.8 26.3 %copy-start.48 = (s32[24]{0:T(128)S(1)}, s32[24]{0:T(128)}, u32[]{:S(2)}) copy-start(s32[24]{0:T(128)} %get-tuple-element.15) | copy-start | bytes 292
  397.8 27.0 %copy-start.44 = (s32[24]{0:T(128)S(1)}, s32[24]{0:T(128)}, u32[]{:S(2)}) copy-start(s32[24]{0:T(128)} %copy-done.43) | copy-start | bytes 292
  397.8 27.0 %copy-start.47 = (s32[24]{0:T(128)S(1)}, s32[24]{0:T(128)}, u32[]{:S(2)}) copy-start(s32[24]{0:T(128)} %get-tuple-element.17) | copy-start | bytes 292
  397.8 402.6 %all-to-all-start = ((bf16[128,19,4096]{2,1,0:T(8,128)(2,1)}), bf16[128,19,4096]{2,1,0:T(8,128)(2,1)}, u32[]{:S(2)}, u32[]{:S(2)}) async-start(bf16[128,19,4096]{2,1,0:T(8,128)(2,1)} %select_select_fusion), calls=%async_computation | async-start | bytes 50331648 | tf_op jit(solution)/shard_map/all_to_all | solution.py:174
  424.9 388.4 %copy-start.5 = (bf16[16,19,4096]{2,1,0:T(8,128)(2,1)S(1)}, bf16[16,19,4096]{2,1,0:T(8,128)(2,1)}, u32[]{:S(2)}) copy-start(bf16[16,19,4096]{2,1,0:T(8,128)(2,1)} %copy-done.4) | copy-start | bytes 7471108
  822.8 6.9 copy-start.1
  (16 other events, 85.1 us)
where the time goes:
time: 842 us; the launch traced here: 830 us
  waiting for transfers between devices  377 us (45%)
  local copies, waits for them, and re-layouts  230 us (27%)
  other arithmetic  137 us (16%)
  matrix products  61.1 us (7%)
  starting transfers between devices  22.8 us (3%)
    all_to_all x1, waiting for transfers between devices, body(): lax.all_to_all(outgoing, ('gx', 'yz'), split_axis=0, concat_axis=0, tiled...  376 us
    another operation x31, local copies, waits for them, and re-layouts, propagate(): return jnp.stack(results)  67.5 us
    reshape x2, local copies, waits for them, and re-layouts, body(): jnp.transpose(local_blocks, (1, 3, 5, 0, 2, 4, 6))  52 us
    unnamed x164, local copies, waits for them, and re-layouts  38.6 us
    select_n x1, other arithmetic, body(): jnp.where(present[:, None, None], jnp.take(refined, chosen_slot, axis=0),...  21.9 us
    concatenate x6, other arithmetic, padded(): block = jnp.concatenate([low, block, high], axis=dim)  20.5 us
    dot_general x2, matrix products, collide(): jnp.einsum('ic,c...->i...', speeds, velocity, precision=lax.Precision.HIG...  18.9 us
    slice x2, other arithmetic, propagate(): collided[direction, 1 - delta_first:1 - delta_first + cells_pipe, 1 - del...  18 us
  transfers between devices with their start and end apart: 9, of which 2 were waited for; matrix products, arithmetic and copies ran while one was open for 11% of the time, Pallas kernels for 0%

commit v1 on v0

v1 whole, which is shorter than its diff:
```python
import functools

import jax
import jax.numpy as jnp
import numpy as np
from jax import lax
from jax.experimental import pallas as pl
from jax.experimental.pallas import tpu as pltpu
from jax.sharding import PartitionSpec as P

BS = 16
BZ = 8
CAP = 24
BLK = 16
ROWS = 48
MAXIN = 16
F32 = jnp.float32
BF16 = jnp.bfloat16

VEL = [
    (0, 0, 0),
    (1, 0, 0), (-1, 0, 0), (0, 1, 0), (0, -1, 0), (0, 0, 1), (0, 0, -1),
    (1, 1, 0), (-1, -1, 0), (1, -1, 0), (-1, 1, 0),
    (1, 0, 1), (-1, 0, -1), (1, 0, -1), (-1, 0, 1),
    (0, 1, 1), (0, -1, -1), (0, 1, -1), (0, -1, 1),
]
OPP = [0, 2, 1, 4, 3, 6, 5, 8, 7, 10, 9, 12, 11, 14, 13, 16, 15, 18, 17]
PLUS = [i for i in range(19) if VEL[i][0] == 1]
MINUS = [i for i in range(19) if VEL[i][0] == -1]
FLAT = [i for i in range(19) if VEL[i][0] == 0]
RIGHTWARD = [(i, 2) for i in PLUS] + [(i, 1) for i in PLUS + FLAT + [12, 14]]
LEFTWARD = [(i, 2) for i in MINUS] + [(i, 1) for i in MINUS + FLAT + [11, 13]]
FACES = len(RIGHTWARD)
FROWS = 40
HALO_Y = ((0, 32), (1, 33), (6, -2), (7, -1))


def collide(h, r):
    p = {}
    d = {}
    for a in range(1, 19, 2):
        p[a] = h[a] + h[a + 1]
        d[a] = h[a] - h[a + 1]
    axis = p[1] + p[3] + p[5]
    diag = (p[7] + p[9]) + (p[11] + p[13]) + (p[15] + p[17])
    rho = 1.0 + (h[0] * (1.0 / 3.0) + axis * (1.0 / 18.0) + diag * (1.0 / 36.0))
    mx = (2.0 * d[1] + (d[7] + d[9]) + (d[11] + d[13])) * (1.0 / 36.0)
    my = (2.0 * d[3] + (d[7] - d[9]) + (d[15] + d[17])) * (1.0 / 36.0)
    mz = (2.0 * d[5] + (d[11] - d[13]) + (d[15] - d[17])) * (1.0 / 36.0)
    inv = 1.0 / rho
    ux, uy, uz = mx * inv, my * inv, mz * inv
    square = ux * ux + uy * uy + uz * uz
    keep = 1.0 - r
    base = r * (rho * (1.0 - 1.5 * square) - 1.0)
    quad = (4.5 * r) * rho
    lin = (3.0 * r) * rho
    proj = {
        1: ux, 3: uy, 5: uz, 7: ux + uy, 9: ux - uy, 11: ux + uz, 13: ux - uz, 15: uy + uz, 17: uy - uz,
    }
    out = [keep * h[0] + base] + [None] * 18
    for a in range(1, 19, 2):
        even = base + quad * (proj[a] * proj[a])
        odd = lin * proj[a]
        out[a] = keep * h[a] + (even + odd)
        out[a + 1] = keep * h[a + 1] + (even - odd)
    return out


def plan_kernel(owner_ref, owned_ref, part):
    me = lax.axis_index("gx") * lax.axis_size("yz") + lax.axis_index("yz")
    rows = owner_ref.shape[0]
    mine = owner_ref[...] == me
    mask = jnp.where(mine, 1.0, 0.0)
    upper = lax.broadcasted_iota(jnp.int32, (128, 128), 0) <= lax.broadcasted_iota(jnp.int32, (128, 128), 1)
    before = lax.broadcasted_iota(jnp.int32, (rows, rows), 1) < lax.broadcasted_iota(jnp.int32, (rows, rows), 0)
    prefix = jnp.dot(mask.astype(BF16), jnp.where(upper, 1.0, 0.0).astype(BF16), preferred_element_type=F32)
    total = jnp.sum(mask, axis=1, keepdims=True)
    total = jnp.broadcast_to(total, (rows, 128))
    offset = jnp.dot(jnp.where(before, 1.0, 0.0).astype(BF16), total.astype(BF16), preferred_element_type=F32)
    rank = prefix + offset
    ids = lax.broadcasted_iota(jnp.int32, (rows, 128), 0) * 128 + lax.broadcasted_iota(jnp.int32, (rows, 128), 1)
    marked = jnp.where(mine, ids.astype(F32) + 1.0, 0.0)
    part[...] = jnp.zeros_like(part)
    for slot in range(CAP):
        hit = jnp.where(rank == float(slot + 1), marked, 0.0)
        part[slot : slot + 1, :] = jnp.sum(hit, axis=0, keepdims=True)
    found = jnp.sum(part[...], axis=1, keepdims=True) - 1.0
    owned_ref[...] = jnp.broadcast_to(found, part.shape).astype(jnp.int32)


def collide_kernel(pop_ref, low_ref, high_ref, rate_ref, c1_ref, cy_ref, right_ref, left_ref, edge):
    @pl.loop(0, 16)
    def _(x):
        for t in range(4):
            rows = slice(8 * t, 8 * t + 8)
            h = [pop_ref[i, x, rows, :].astype(F32) for i in range(19)]
            out = collide(h, rate_ref[1, 8 + 8 * t : 16 + 8 * t, :])
            for i in range(19):
                c1_ref[i, x, rows, :] = out[i].astype(BF16)

    for slot, y in HALO_Y:
        source = low_ref if y < 0 else high_ref
        row = y + 2 if y < 0 else y - 32
        rate = jnp.broadcast_to(rate_ref[1, y + 8 : y + 9, :], (8, 128))

        @pl.loop(0, 2)
        def _(half):
            start = pl.multiple_of(half * 8, 8)
            h = [source[i, row, pl.ds(start, 8), :].astype(F32) for i in range(19)]
            out = collide(h, rate)
            for i in range(19):
                edge[pl.ds(pl.multiple_of((i * 8 + slot) * 16 + start, 8), 8), :] = out[i]
                cy_ref[i, slot, pl.ds(start, 8), :] = out[i].astype(BF16)

    for ref, faces, planes in ((right_ref, RIGHTWARD, (None, 15, 14)), (left_ref, LEFTWARD, (None, 0, 1))):
        for n, (i, depth) in enumerate(faces):
            plane = planes[depth]
            ref[n, 0:32, :] = c1_ref[i, plane, :, :]
            ref[n, 32:40, :] = edge[pl.ds(i * 128 + plane, 8, stride=16), :].astype(BF16)


def shifted(ref, at, lane):
    out = []
    for i in range(19):
        dx, dy, dz = VEL[i]
        v = ref[i, pl.ds(at(-dx, -dy), 8), :]
        if dz == 1:
            v = jnp.where(lane == 0, ref[OPP[i], pl.ds(at(0, 0), 8), :], pltpu.roll(v, 1, axis=1))
        elif dz == -1:
            v = jnp.where(lane == 127, ref[OPP[i], pl.ds(at(0, 0), 8), :], pltpu.roll(v, 127, axis=1))
        out.append(v)
    return out


def step_kernel(
    flags_ref, owner_ref, owned_ref, c1_ref, cy_ref, gl_ref, gr_ref, rate_ref, reduce_ref,
    out_ref, send_ref,
    first, second, mix, blk, padded, coarse, pack, stage, zero, out_sem, send_sem,
):
    me = lax.axis_index("gx") * lax.axis_size("yz") + lax.axis_index("yz")
    lane = lax.broadcasted_iota(jnp.int32, (8, 128), 1)

    zero[...] = jnp.zeros_like(zero)

    @pl.loop(0, CAP)
    def _(s):
        @pl.when(owned_ref[s, 0] < 0)
        def _():
            pltpu.make_async_copy(zero, out_ref.at[s], out_sem.at[s]).start()

    @pl.loop(0, 16)
    def _(x):
        for i in range(19):
            start = pl.multiple_of((x + 2) * ROWS + 8, 8)
            first[i, pl.ds(start, 32), :] = c1_ref[i, x, :, :].astype(F32)

    for slot, y in HALO_Y:
        for i in range(19):
            for half in range(2):
                first[i, pl.ds((8 * half + 2) * ROWS + y + 8, 8, stride=ROWS), :] = cy_ref[
                    i, slot, 8 * half : 8 * half + 8, :
                ].astype(F32)
    for ref, faces, planes in ((gl_ref, RIGHTWARD, (None, -1, -2)), (gr_ref, LEFTWARD, (None, 16, 17))):
        for n, (i, depth) in enumerate(faces):
            base = (planes[depth] + 2) * ROWS
            first[i, base + 8 : base + 40, :] = ref[n, 0:32, :].astype(F32)
            edge = ref[n, 32:40, :].astype(F32)
            first[i, base + 40 : base + 48, :] = edge
            first[i, base : base + 8, :] = edge

    @pl.loop(0, 18)
    def _(p):
        which = (p + 15) // 16
        for t in range(5):
            def at(dx, dy, t=t):
                return pl.multiple_of(p * ROWS, 8) + ((dx + 1) * ROWS + 7 + 8 * t + dy)

            h = shifted(first, at, lane)
            out = collide([v.astype(BF16).astype(F32) for v in h], rate_ref[which, 7 + 8 * t : 15 + 8 * t, :])
            for i in range(19):
                second[i, pl.ds(pl.multiple_of(p * ROWS, 8) + (7 + 8 * t), 8), :] = out[i].astype(BF16).astype(F32)

    @pl.loop(0, 16)
    def _(x):
        for yh in range(4):
            def at(dx, dy, yh=yh):
                return pl.multiple_of(x * ROWS, 8) + ((dx + 1) * ROWS + 8 + 8 * yh + dy)

            h = shifted(second, at, lane)
            for i in range(19):
                mix[yh, 8 * i : 8 * i + 8, :] = h[i]
            groups = []
            for g in range(3):
                a = [mix[yh, pl.ds(64 * g + y, 8, stride=8), :] for y in range(8)]
                for bit in range(3):
                    width = 16 << bit
                    low = (lane & width) == 0
                    b = list(a)
                    for j in range(8):
                        if j & (1 << bit):
                            continue
                        k = j | (1 << bit)
                        b[j] = jnp.where(low, a[j], pltpu.roll(a[k], width, axis=1))
                        b[k] = jnp.where(low, pltpu.roll(a[j], 128 - width, axis=1), a[k])
                    a = b
                groups.append(a)
            lanes = pl.ds(pl.multiple_of(x * 256 + (yh % 2) * 128, 128), 128)
            for z in range(8):
                k = (yh // 2) * 8 + z
                head = jnp.concatenate([groups[0][z], groups[1][z]], axis=0).astype(BF16)
                tail = groups[2][z].astype(BF16)
                padded[k, 0:16, lanes] = head
                padded[k, 16:24, lanes] = tail
                blk[k, 0:16, lanes] = head
                blk[k, 16:19, lanes] = tail[0:3, :]

    @pl.loop(0, CAP)
    def _(s):
        b = owned_ref[s, 0]

        @pl.when((b >= 0) & (flags_ref[jnp.maximum(b, 0)] == 0))
        def _():
            pltpu.make_async_copy(blk.at[b - me * BLK], out_ref.at[s], out_sem.at[s]).start()

    for q in range(4):
        part = padded[:, :, q * 1024 : (q + 1) * 1024].reshape(BLK * 24, 1024)
        mean = jnp.dot(part, reduce_ref[...], preferred_element_type=F32)
        coarse[:, q, :, :] = mean.reshape(BLK, 24, 128)

    @pl.loop(0, BLK)
    def _(k):
        @pl.when(flags_ref[me * BLK + k] != 0)
        def _():
            for q in range(4):
                pack[20 * q : 20 * q + 24, :] = coarse[k, q, :, :]
            stage[k, :, :] = pack[0:80, :].astype(BF16)
            pltpu.make_async_copy(stage.at[k], send_ref.at[owner_ref[me * BLK + k]], send_sem.at[k]).start()

    @pl.loop(0, BLK)
    def _(k):
        @pl.when(flags_ref[me * BLK + k] != 0)
        def _():
            pltpu.make_async_copy(stage.at[k], send_ref.at[0], send_sem.at[k]).wait()

    @pl.loop(0, CAP)
    def _(s):
        b = owned_ref[s, 0]

        @pl.when((b < 0) | (flags_ref[jnp.maximum(b, 0)] == 0))
        def _():
            pltpu.make_async_copy(zero, out_ref.at[s], out_sem.at[s]).wait()


def refine_kernel(
    flags_ref, owned_ref, recv_ref, expand_ref, base_ref, out_ref,
    taken, fine, wide, product, result, slots, in_sem, out_sem,
):
    del base_ref

    def fetch(s, count):
        b = owned_ref[s, 0]
        arrives = (b >= 0) & (flags_ref[jnp.maximum(b, 0)] != 0)

        @pl.when(arrives)
        def _():
            slots[0, count] = s
            slots[1, count] = flags_ref[jnp.maximum(b, 0)]
            pltpu.make_async_copy(recv_ref.at[b // BLK], taken.at[count], in_sem.at[count]).start()

        return count + jnp.where(arrives, 1, 0)

    count = lax.fori_loop(0, CAP, fetch, jnp.int32(0))

    @pl.loop(0, count)
    def _(n):
        pltpu.make_async_copy(recv_ref.at[0], taken.at[n], in_sem.at[n]).wait()

    @pl.loop(0, (count + 3) // 4)
    def _(group):
        for m in range(4):
            fine[0:80, :] = taken[group * 4 + m, :, :].astype(F32)
            for q in range(4):
                wide[m * 96 + q * 24 : m * 96 + q * 24 + 24, :] = fine[20 * q : 20 * q + 24, :].astype(BF16)
        product[...] = jnp.dot(wide[...], expand_ref[...], preferred_element_type=F32)
        for m in range(4):
            n = group * 4 + m

            @pl.when(n < count)
            def _():
                kind = slots[1, n]
                linear = kind == 2
                near = jnp.where(linear, 0.75, 1.0)
                far = jnp.where(linear, 0.25, 0.0)
                offset = pl.multiple_of(jnp.where(linear, 512, 0), 512)

                def plane(c):
                    return product[
                        m * 96 + (c // 2) * 24 : m * 96 + (c // 2) * 24 + 24,
                        pl.ds(pl.multiple_of(offset + (c % 2) * 256, 256), 256),
                    ]

                for c in range(8):
                    mid = plane(c) * near
                    for odd in range(2):
                        other = max(c - 1, 0) if odd == 0 else min(c + 1, 7)
                        x = 2 * c + odd
                        value = (mid + plane(other) * far).astype(BF16)
                        result[n, 0:16, x * 256 : x * 256 + 256] = value[0:16, :]
                        result[n, 16:19, x * 256 : x * 256 + 256] = value[16:19, :]
                pltpu.make_async_copy(result.at[n], out_ref.at[slots[0, n]], out_sem.at[n]).start()

    @pl.loop(0, count)
    def _(n):
        pltpu.make_async_copy(result.at[n], out_ref.at[0], out_sem.at[n]).wait()


def mean_matrix():
    half = np.zeros((16, 8), np.float32)
    half[np.arange(16), np.arange(16) // 2] = 0.5
    pair = np.zeros((4, 2), np.float32)
    pair[np.arange(4), np.arange(4) // 2] = 0.5
    return np.kron(pair, np.kron(half, half))


def expand_matrix():
    inject = np.zeros((8, 16), np.float32)
    linear = np.zeros((8, 16), np.float32)
    for k in range(8):
        for odd, other in ((0, max(k - 1, 0)), (1, min(k + 1, 7))):
            inject[k, 2 * k + odd] = 1.0
            linear[k, 2 * k + odd] += 0.75
            linear[other, 2 * k + odd] += 0.25
    eye = np.eye(2, dtype=np.float32)
    return np.concatenate([np.kron(eye, np.kron(m, m)) for m in (inject, linear)], axis=1)


def ring(count, step):
    return [(i, (i + step) % count) for i in range(count)]


VM = pl.BlockSpec(memory_space=pltpu.VMEM)
SM = pl.BlockSpec(memory_space=pltpu.SMEM)
ANY = pl.BlockSpec(memory_space=pl.ANY)


def struct(shape, dtype):
    return jax.ShapeDtypeStruct(shape, dtype)


def body(populations, levels, refine_flags, new_owner):
    columns = lax.axis_size("yz")
    slabs = lax.axis_size("gx")
    slab = lax.axis_index("gx")
    column = lax.axis_index("yz")
    total = new_owner.shape[0]

    top = jnp.transpose(populations[:, :, 30:32, :], (0, 2, 1, 3))
    bottom = jnp.transpose(populations[:, :, 0:2, :], (0, 2, 1, 3))
    low = lax.ppermute(top, "yz", ring(columns, 1))
    high = lax.ppermute(bottom, "yz", ring(columns, -1))

    grid = levels.reshape(slabs, 2 * columns, BZ)
    grid = jnp.concatenate([grid[-1:], grid, grid[:1]], axis=0)
    grid = jnp.concatenate([grid[:, -1:], grid, grid[:, :1]], axis=1)
    near = lax.dynamic_slice(grid, (slab, 2 * column, 0), (3, 4, BZ)).astype(F32)
    near = 1.0 / (0.5 + jnp.power(0.5, near))
    rate = jnp.repeat(jnp.repeat(near, BS, axis=2), BS, axis=1)[:, 8:56, :]

    owned = pl.pallas_call(
        plan_kernel,
        out_shape=struct((32, 128), jnp.int32),
        in_specs=[VM],
        out_specs=VM,
        scratch_shapes=[pltpu.VMEM((32, 128), F32)],
    )(new_owner.reshape(total // 128, 128))

    c1, cy, right, left = pl.pallas_call(
        collide_kernel,
        out_shape=(
            struct((19, 16, 32, 128), BF16),
            struct((19, 8, 16, 128), BF16),
            struct((FACES, FROWS, 128), BF16),
            struct((FACES, FROWS, 128), BF16),
        ),
        in_specs=[VM] * 4,
        out_specs=(VM,) * 4,
        scratch_shapes=[pltpu.VMEM((19 * 128 + 128, 128), F32)],
    )(populations, low, high, rate)

    from_left = lax.ppermute(right, "gx", ring(slabs, 1))
    from_right = lax.ppermute(left, "gx", ring(slabs, -1))

    half, send = pl.pallas_call(
        step_kernel,
        out_shape=(struct((CAP, 19, 4096), BF16), struct((slabs * columns, 80, 128), BF16)),
        in_specs=[SM, SM, SM] + [VM] * 6,
        out_specs=(ANY, ANY),
        scratch_shapes=[
            pltpu.VMEM((19, 20 * ROWS, 128), F32),
            pltpu.VMEM((19, 18 * ROWS, 128), F32),
            pltpu.VMEM((4, 192, 128), F32),
            pltpu.VMEM((BLK, 19, 4096), BF16),
            pltpu.VMEM((BLK, 24, 4096), BF16),
            pltpu.VMEM((BLK, 4, 24, 128), F32),
            pltpu.VMEM((88, 128), F32),
            pltpu.VMEM((BLK, 80, 128), BF16),
            pltpu.VMEM((19, 4096), BF16),
            pltpu.SemaphoreType.DMA((CAP,)),
            pltpu.SemaphoreType.DMA((BLK,)),
        ],
    )(
        refine_flags, new_owner, owned, c1, cy, from_left, from_right, rate,
        jnp.asarray(mean_matrix(), BF16),
    )

    recv = lax.all_to_all(send, ("gx", "yz"), split_axis=0, concat_axis=0, tiled=True)

    return pl.pallas_call(
        refine_kernel,
        out_shape=struct((CAP, 19, 4096), BF16),
        in_specs=[SM, SM, ANY, VM, ANY],
        out_specs=ANY,
        input_output_aliases={4: 0},
        scratch_shapes=[
            pltpu.VMEM((MAXIN, 80, 128), BF16),
            pltpu.VMEM((88, 128), F32),
            pltpu.VMEM((384, 128), BF16),
            pltpu.VMEM((384, 1024), F32),
            pltpu.VMEM((MAXIN, 19, 4096), BF16),
            pltpu.SMEM((2, MAXIN), jnp.int32),
            pltpu.SemaphoreType.DMA((MAXIN,)),
            pltpu.SemaphoreType.DMA((MAXIN,)),
        ],
    )(refine_flags, owned, recv, jnp.asarray(expand_matrix(), BF16), half)


def solution(mesh):
    placed = (P(None, "gx", "yz", None), P(), P(), P())
    return jax.shard_map(
        body, mesh=mesh, in_specs=placed, out_specs=P(("gx", "yz"), None, None), check_vma=False
    )
```

time: 842 us -> 101 us (0.12)
  the two profiles are of different devices: /device:TPU:2 before, /device:TPU:1 now
where the time goes in v1:
time: 101 us; the launch traced here: 99.9 us
  blocking collectives  46.9 us (46%)
  Pallas kernels  28 us (28%)
  local copies, waits for them, and re-layouts  12.5 us (12%)
  starting transfers between devices  7.98 us (8%)
  waiting for transfers between devices  4.29 us (4%)
    all_to_all x1, blocking collectives, body(): lax.all_to_all(send, ('gx', 'yz'), split_axis=0, concat_axis=0, tiled=True)  46.9 us
    pallas_call x1, Pallas kernels, body(): pl.pallas_call(step_kernel, out_shape=(struct((CAP, 19, 4096), BF16), str...  16.7 us
    pallas_call x1, local copies, waits for them, and re-layouts, body(): pl.pallas_call(refine_kernel, out_shape=struct((CAP, 19, 4096), BF16), in...  6.34 us
    pallas_call x1, Pallas kernels, body(): pl.pallas_call(collide_kernel, out_shape=(struct((19, 16, 32, 128), BF16)...  6.11 us
    ppermute x1, starting transfers between devices, body(): from_right = lax.ppermute(left, 'gx', ring(slabs, -1))  3.64 us
    pallas_call x1, Pallas kernels, body(): pl.pallas_call(refine_kernel, out_shape=struct((CAP, 19, 4096), BF16), in...  3.59 us
    ppermute x1, starting transfers between devices, body(): low = lax.ppermute(top, 'yz', ring(columns, 1))  3.03 us
    ppermute x1, waiting for transfers between devices, body(): from_left = lax.ppermute(right, 'gx', ring(slabs, 1))  2.89 us
  transfers between devices with their start and end apart: 4, of which 2 were waited for; matrix products, arithmetic and copies ran while one was open for 3% of the time, Pallas kernels for 2%

profile of v1, /device:TPU:1, one launch (start us, length us, event | category | flops | bytes accessed | tf_op | source)
XLA Modules:
  0.0 99.9 jit_solution(6851662709875042894)
XLA Ops:
  0.0 1.5 %fusion.6 = (bf16[19,16,2,128]{3,2,1,0:T(2,128)(2,1)S(1)}, bf16[19,16,2,128]{3,2,1,0:T(2,128)(2,1)S(1)}) fusion(bf16[19,16,32,128]{3,2,1,0:T(8,128)(2,1)} %pop_ref.1), kind=kLoop, calls=%fused_computation.14 | loop fusion | bytes 622592 | tf_op jit(solution)/shard_map/slice | solution.py:358
  1.6 3.0 %collective-permute-start = (bf16[19,2,16,128]{3,2,1,0:T(8,128)(2,1)S(1)}, bf16[19,2,16,128]{3,2,1,0:T(8,128)(2,1)S(1)}, u32[]{:S(2)}, u32[]{:S(2)}) collective-permute-start(bf16[19,2,16,128]{3,2,1,0:T(8,128)(2,1)S(1)} %bitcast.11), channel_id=1, source_target_pairs={{0,1},{1,2},{2,3},{3,4},{4,5},{5,6},{6,7},{7,0},{8,9},{9,10},{10,1... | collective-permute-start | bytes 466952 | tf_op jit(solution)/shard_map/ppermute | solution.py:359
  4.6 0.0 collective-permute-start.1
  4.6 0.7 fusion.8
  5.4 0.8 reshape.31
  6.2 0.1 slice.48
  6.2 0.1 slice.46
  6.4 0.1 copy.27
  6.5 0.2 copy.28
  6.7 0.2 copy.26
  6.8 0.1 fusion.5
  7.0 0.1 copy.29
  7.1 0.1 broadcast_in_dim.6
  7.1 0.1 reshape.32
  7.3 0.6 slice.54.rate_ref
  7.9 0.0 collective-permute-done.low_ref
  7.9 0.0 copy-start.2
  7.9 1.4 %collective-permute-done.1.high_ref = bf16[19,2,16,128]{3,2,1,0:T(8,128)(2,1)S(1)} collective-permute-done((bf16[19,2,16,128]{3,2,1,0:T(8,128)(2,1)S(1)}, bf16[19,2,16,128]{3,2,1,0:T(8,128)(2,1)S(1)}, u32[]{:S(2)}, u32[]{:S(2)}) %collective-permute-start.1) | collective-permute-done | bytes 155680 | tf_op jit(solution)/shard_map/ppermute | solution.py:360
  9.3 0.0 copy-done.2
  9.3 0.0 copy-start.3
  9.3 0.7 copy-done.3
  10.0 6.1 %shard_map.65 = (bf16[19,16,32,128]{3,2,1,0:T(8,128)(2,1)}, bf16[19,8,16,128]{3,2,1,0:T(8,128)(2,1)}, bf16[21,40,128]{2,1,0:T(8,128)(2,1)}, bf16[21,40,128]{2,1,0:T(8,128)(2,1)}) custom-call(bf16[19,16,32,128]{3,2,1,0:T(8,128)(2,1)} %pop_ref.1, bf16[19,2,16,128]{3,2,1,0:T(8,128)(2,1)} %copy-done.2, bf16[19,2,16,128]{3,2,1,0:T(8,128)(2,1)} %copy-done.3, ...), custom_call_target="tpu_custom_call" | custom-call | tf_op jit(solution)/shard_map/pallas_call | solution.py:377
  16.1 1.3 %collective-permute-start.2 = (bf16[21,40,128]{2,1,0:T(8,128)(2,1)}, bf16[21,40,128]{2,1,0:T(8,128)(2,1)S(1)}, u32[]{:S(2)}, u32[]{:S(2)}) collective-permute-start(bf16[21,40,128]{2,1,0:T(8,128)(2,1)} %get-tuple-element.13), channel_id=1, source_target_pairs={{0,8},{8,16},{16,24},{24,32},{32,40},{40,48},{48,56},{56,64},{64,7... | collective-permute-start | bytes 645128 | tf_op jit(solution)/shard_map/ppermute | solution.py:390
  17.4 3.6 %collective-permute-start.3 = (bf16[21,40,128]{2,1,0:T(8,128)(2,1)}, bf16[21,40,128]{2,1,0:T(8,128)(2,1)S(1)}, u32[]{:S(2)}, u32[]{:S(2)}) collective-permute-start(bf16[21,40,128]{2,1,0:T(8,128)(2,1)} %get-tuple-element.14), channel_id=1, source_target_pairs={{0,120},{8,0},{16,8},{24,16},{32,24},{40,32},{48,40},{56,48},{64,5... | collective-permute-start | bytes 645128 | tf_op jit(solution)/shard_map/ppermute | solution.py:391
  21.0 1.6 %shard_map.64.owned_ref = s32[32,128]{1,0:T(8,128)} custom-call(s32[16,128]{1,0:T(8,128)} %bitcast.13), custom_call_target="tpu_custom_call" | custom-call | tf_op jit(solution)/shard_map/pallas_call | solution.py:369
  22.6 2.9 %collective-permute-done.2.gl_ref = bf16[21,40,128]{2,1,0:T(8,128)(2,1)S(1)} collective-permute-done((bf16[21,40,128]{2,1,0:T(8,128)(2,1)}, bf16[21,40,128]{2,1,0:T(8,128)(2,1)S(1)}, u32[]{:S(2)}, u32[]{:S(2)}) %collective-permute-start.2) | collective-permute-done | bytes 215072 | tf_op jit(solution)/shard_map/ppermute | solution.py:390
  25.5 0.0 copy-start
  25.5 0.0 collective-permute-done.3.gr_ref
  25.5 0.0 copy-start.1
  25.5 0.7 copy-done
  26.2 0.1 copy-done.1
  26.3 16.7 %shard_map.66 = (bf16[24,19,4096]{2,1,0:T(8,128)(2,1)}, bf16[128,80,128]{2,1,0:T(8,128)(2,1)}) custom-call(s32[2048]{0:T(1024)} %flags_ref.3, s32[2048]{0:T(1024)} %owner_ref.1, s32[32,128]{1,0:T(8,128)} %shard_map.64.owned_ref, bf16[19,16,32,128]{3,2,1,0:T(8,128)(2,1)} %get-tuple-element.11.c1_ref, bf16[19,8,16,128]{3,2,1,0:T(8,128)(2,1)} %get-tuple-element.12.cy_ref, ...), custom_call_target="tpu_custom_call" | custom-call | tf_op jit(solution)/shard_map/pallas_call | solution.py:393
  43.0 46.9 %all_to_all.5.recv_ref = bf16[128,80,128]{2,1,0:T(8,128)(2,1)} all-to-all(bf16[128,80,128]{2,1,0:T(8,128)(2,1)} %get-tuple-element.15), channel_id=1, replica_groups=mesh['gx'=16,'yz'=8] {'gx','yz'}, dimensions={0} | all-to-all | bytes 5242880 | tf_op jit(solution)/shard_map/all_to_all | solution.py:416
  89.9 3.6 %shard_map.67 = bf16[24,19,4096]{2,1,0:T(8,128)(2,1)} custom-call(s32[2048]{0:T(1024)} %flags_ref.3, s32[32,128]{1,0:T(8,128)} %shard_map.64.owned_ref, bf16[128,80,128]{2,1,0:T(8,128)(2,1)} %all_to_all.5.recv_ref, bf16[128,1024]{1,0:T(8,128)(2,1)} %constant.24.clone.expand_ref, ...), custom_call_target="tpu_custom_call", output_to_operand_aliasing={{}: (4, {})} | custom-call | tf_op jit(solution)/shard_map/pallas_call | solution.py:418
  93.5 6.3 %copy.30 = bf16[24,19,4096]{2,0,1:T(8,128)(2,1)} copy(bf16[24,19,4096]{2,1,0:T(8,128)(2,1)} %shard_map.67) | data formatting | bytes 7471104 | tf_op jit(solution)/shard_map/pallas_call | solution.py:418
  (7 shorter events, 0.1 us)
Async XLA Ops:
  1.6 6.3 %collective-permute-start = (bf16[19,2,16,128]{3,2,1,0:T(8,128)(2,1)S(1)}, bf16[19,2,16,128]{3,2,1,0:T(8,128)(2,1)S(1)}, u32[]{:S(2)}, u32[]{:S(2)}) collective-permute-start(bf16[19,2,16,128]{3,2,1,0:T(8,128)(2,1)S(1)} %bitcast.11), channel_id=1, source_target_pairs={{0,1},{1,2},{2,3},{3,4},{4,5},{5,6},{6,7},{7,0},{8,9},{9,10},{10,1... | collective-permute-start | bytes 466952 | tf_op jit(solution)/shard_map/ppermute | solution.py:359
  4.6 4.7 %collective-permute-start.1 = (bf16[19,2,16,128]{3,2,1,0:T(8,128)(2,1)S(1)}, bf16[19,2,16,128]{3,2,1,0:T(8,128)(2,1)S(1)}, u32[]{:S(2)}, u32[]{:S(2)}) collective-permute-start(bf16[19,2,16,128]{3,2,1,0:T(8,128)(2,1)S(1)} %bitcast.12), channel_id=1, source_target_pairs={{0,7},{1,0},{2,1},{3,2},{4,3},{5,4},{6,5},{7,6},{8,15},{9,8},{10,9... | collective-permute-start | bytes 466952 | tf_op jit(solution)/shard_map/ppermute | solution.py:360
  7.9 1.4 %copy-start.2 = (bf16[19,2,16,128]{3,2,1,0:T(8,128)(2,1)}, bf16[19,2,16,128]{3,2,1,0:T(8,128)(2,1)S(1)}, u32[]{:S(2)}) copy-start(bf16[19,2,16,128]{3,2,1,0:T(8,128)(2,1)S(1)} %collective-permute-done.low_ref) | copy-start | bytes 466948
  9.3 0.7 copy-start.3
  16.1 9.5 %collective-permute-start.2 = (bf16[21,40,128]{2,1,0:T(8,128)(2,1)}, bf16[21,40,128]{2,1,0:T(8,128)(2,1)S(1)}, u32[]{:S(2)}, u32[]{:S(2)}) collective-permute-start(bf16[21,40,128]{2,1,0:T(8,128)(2,1)} %get-tuple-element.13), channel_id=1, source_target_pairs={{0,8},{8,16},{16,24},{24,32},{32,40},{40,48},{48,56},{56,64},{64,7... | collective-permute-start | bytes 645128 | tf_op jit(solution)/shard_map/ppermute | solution.py:390
  17.4 8.2 %collective-permute-start.3 = (bf16[21,40,128]{2,1,0:T(8,128)(2,1)}, bf16[21,40,128]{2,1,0:T(8,128)(2,1)S(1)}, u32[]{:S(2)}, u32[]{:S(2)}) collective-permute-start(bf16[21,40,128]{2,1,0:T(8,128)(2,1)} %get-tuple-element.14), channel_id=1, source_target_pairs={{0,120},{8,0},{16,8},{24,16},{32,24},{40,32},{48,40},{56,48},{64,5... | collective-permute-start | bytes 645128 | tf_op jit(solution)/shard_map/ppermute | solution.py:391
  25.5 0.7 copy-start
  25.5 0.8 copy-start.1

commit v2 on v1

v2 whole, which is shorter than its diff:
```python
import jax
import jax.numpy as jnp
import numpy as np
from jax import lax
from jax.experimental import pallas as pl
from jax.experimental.pallas import tpu as pltpu
from jax.sharding import PartitionSpec as P

BS = 16
BZ = 8
CAP = 24
BLK = 16
ROWS = 48
F32 = jnp.float32
BF16 = jnp.bfloat16

VEL = [
    (0, 0, 0),
    (1, 0, 0), (-1, 0, 0), (0, 1, 0), (0, -1, 0), (0, 0, 1), (0, 0, -1),
    (1, 1, 0), (-1, -1, 0), (1, -1, 0), (-1, 1, 0),
    (1, 0, 1), (-1, 0, -1), (1, 0, -1), (-1, 0, 1),
    (0, 1, 1), (0, -1, -1), (0, 1, -1), (0, -1, 1),
]
OPP = [0, 2, 1, 4, 3, 6, 5, 8, 7, 10, 9, 12, 11, 14, 13, 16, 15, 18, 17]
PLUS = [i for i in range(19) if VEL[i][0] == 1]
MINUS = [i for i in range(19) if VEL[i][0] == -1]
FLAT = [i for i in range(19) if VEL[i][0] == 0]
RIGHTWARD = [(i, 2) for i in PLUS] + [(i, 1) for i in PLUS + FLAT + [12, 14]]
LEFTWARD = [(i, 2) for i in MINUS] + [(i, 1) for i in MINUS + FLAT + [11, 13]]
FACES = len(RIGHTWARD)
FROWS = 40
HALO_Y = ((0, 32), (1, 33), (6, -2), (7, -1))


def collide(h, r):
    p = {}
    d = {}
    for a in range(1, 19, 2):
        p[a] = h[a] + h[a + 1]
        d[a] = h[a] - h[a + 1]
    axis = p[1] + p[3] + p[5]
    diag = (p[7] + p[9]) + (p[11] + p[13]) + (p[15] + p[17])
    rho = 1.0 + (h[0] * (1.0 / 3.0) + axis * (1.0 / 18.0) + diag * (1.0 / 36.0))
    mx = (2.0 * d[1] + (d[7] + d[9]) + (d[11] + d[13])) * (1.0 / 36.0)
    my = (2.0 * d[3] + (d[7] - d[9]) + (d[15] + d[17])) * (1.0 / 36.0)
    mz = (2.0 * d[5] + (d[11] - d[13]) + (d[15] - d[17])) * (1.0 / 36.0)
    inv = 1.0 / rho
    ux, uy, uz = mx * inv, my * inv, mz * inv
    square = ux * ux + uy * uy + uz * uz
    keep = 1.0 - r
    base = r * (rho * (1.0 - 1.5 * square) - 1.0)
    quad = (4.5 * r) * rho
    lin = (3.0 * r) * rho
    proj = {
        1: ux, 3: uy, 5: uz, 7: ux + uy, 9: ux - uy, 11: ux + uz, 13: ux - uz, 15: uy + uz, 17: uy - uz,
    }
    out = [keep * h[0] + base] + [None] * 18
    for a in range(1, 19, 2):
        even = base + quad * (proj[a] * proj[a])
        odd = lin * proj[a]
        out[a] = keep * h[a] + (even + odd)
        out[a + 1] = keep * h[a + 1] + (even - odd)
    return out


def plan_kernel(levels_ref, flags_ref, owner_ref, rate_ref, owned_ref, kind_ref, part, kinds):
    slab, column = lax.axis_index("gx"), lax.axis_index("yz")
    slabs, columns = lax.axis_size("gx"), lax.axis_size("yz")
    me = slab * columns + column

    group = lax.broadcasted_iota(jnp.int32, (8, 128), 1) // BS
    for plane in range(3):
        row = lax.rem(slab + (plane + slabs - 1), slabs) * (2 * columns)
        for band, (first, last) in enumerate(((0, 8), (8, 24), (24, 40), (40, 48))):
            start = (row + lax.rem(2 * column + (band + 2 * columns - 1), 2 * columns)) * BZ
            level = jnp.zeros((8, 128), F32)
            for z in range(BZ):
                level = jnp.where(group == z, levels_ref[start + z].astype(F32), level)
            rate = 1.0 / (0.5 + jnp.exp2(-level))
            for at in range(first, last, 8):
                rate_ref[plane, at : at + 8, :] = rate

    rows = owner_ref.shape[0]
    mine = owner_ref[...] == me
    mask = jnp.where(mine, 1.0, 0.0)
    upper = lax.broadcasted_iota(jnp.int32, (128, 128), 0) <= lax.broadcasted_iota(jnp.int32, (128, 128), 1)
    before = lax.broadcasted_iota(jnp.int32, (rows, rows), 1) < lax.broadcasted_iota(jnp.int32, (rows, rows), 0)
    prefix = jnp.dot(mask.astype(BF16), jnp.where(upper, 1.0, 0.0).astype(BF16), preferred_element_type=F32)
    total = jnp.broadcast_to(jnp.sum(mask, axis=1, keepdims=True), (rows, 128))
    offset = jnp.dot(jnp.where(before, 1.0, 0.0).astype(BF16), total.astype(BF16), preferred_element_type=F32)
    rank = prefix + offset
    ids = lax.broadcasted_iota(jnp.int32, (rows, 128), 0) * 128 + lax.broadcasted_iota(jnp.int32, (rows, 128), 1)
    marked = jnp.where(mine, ids.astype(F32) + 1.0, 0.0)
    flagged = jnp.where(mine, flags_ref[...].astype(F32), 0.0)
    part[...] = jnp.zeros_like(part)
    kinds[...] = jnp.zeros_like(kinds)
    for slot in range(CAP):
        hit = rank == float(slot + 1)
        part[slot : slot + 1, :] = jnp.sum(jnp.where(hit, marked, 0.0), axis=0, keepdims=True)
        kinds[slot : slot + 1, :] = jnp.sum(jnp.where(hit, flagged, 0.0), axis=0, keepdims=True)
    found = jnp.sum(part[...], axis=1, keepdims=True) - 1.0
    owned_ref[...] = jnp.broadcast_to(found, part.shape).astype(jnp.int32)
    kind_ref[...] = jnp.broadcast_to(jnp.sum(kinds[...], axis=1, keepdims=True), kinds.shape)


def collide_kernel(pop_ref, rate_ref, c1_ref):
    @pl.loop(0, 16)
    def _(x):
        for t in range(4):
            rows = slice(8 * t, 8 * t + 8)
            h = [pop_ref[i, x, rows, :].astype(F32) for i in range(19)]
            out = collide(h, rate_ref[1, 8 + 8 * t : 16 + 8 * t, :])
            for i in range(19):
                c1_ref[i, x, rows, :] = out[i].astype(BF16)


def face_kernel(c1_ref, low_ref, high_ref, rate_ref, cy_ref, rim_ref, right_ref, left_ref, planes, edge, sem):
    copies = [
        pltpu.make_async_copy(c1_ref.at[:, a : a + 2], planes.at[:, b : b + 2], sem.at[n])
        for n, (a, b) in enumerate(((0, 0), (14, 2)))
    ]
    for copy in copies:
        copy.start()

    for slot, y in HALO_Y:
        source = low_ref if y < 0 else high_ref
        row = y + 2 if y < 0 else y - 32
        rate = jnp.broadcast_to(rate_ref[1, y + 8 : y + 9, :], (8, 128))

        @pl.loop(0, 2)
        def _(half):
            start = pl.multiple_of(half * 8, 8)
            h = [source[i, row, pl.ds(start, 8), :].astype(F32) for i in range(19)]
            out = collide(h, rate)
            for i in range(19):
                edge[pl.ds(pl.multiple_of((i * 8 + slot) * 16 + start, 8), 8), :] = out[i]
                cy_ref[i, slot, pl.ds(start, 8), :] = out[i].astype(BF16)

    for copy in copies:
        copy.wait()
    for i in range(19):
        for n, plane in enumerate((0, 1, 14, 15)):
            body_rows = planes[i, n, :, :]
            ends = edge[pl.ds(i * 128 + plane, 8, stride=16), :].astype(BF16)
            rim_ref[i, n, 0:32, :] = body_rows
            rim_ref[i, n, 32:40, :] = ends
            for ref, faces, depth in ((right_ref, RIGHTWARD, 16 - plane), (left_ref, LEFTWARD, plane + 1)):
                if (i, depth) in faces:
                    at = faces.index((i, depth))
                    ref[at, 0:32, :] = body_rows
                    ref[at, 32:40, :] = ends


def shifted(ref, at, lane):
    out = []
    for i in range(19):
        dx, dy, dz = VEL[i]
        v = ref[i, pl.ds(at(-dx, -dy), 8), :]
        if dz == 1:
            v = jnp.where(lane == 0, ref[OPP[i], pl.ds(at(0, 0), 8), :], pltpu.roll(v, 1, axis=1))
        elif dz == -1:
            v = jnp.where(lane == 127, ref[OPP[i], pl.ds(at(0, 0), 8), :], pltpu.roll(v, 127, axis=1))
        out.append(v)
    return out


def advance(source, at, rate, target, row, lane):
    h = shifted(source, at, lane)
    out = collide([v.astype(BF16).astype(F32) for v in h], rate)
    for i in range(19):
        target[i, pl.ds(row, 8), :] = out[i].astype(BF16).astype(F32)


def inner_kernel(c1_ref, cy_ref, rate_ref, c2_ref, first, second, sem):
    lane = lax.broadcasted_iota(jnp.int32, (8, 128), 1)

    @pl.loop(0, 16)
    def _(x):
        for i in range(19):
            first[i, pl.ds(pl.multiple_of(x * ROWS + 8, 8), 32), :] = c1_ref[i, x, :, :].astype(F32)

    for slot, y in HALO_Y:
        for i in range(19):
            for half in range(2):
                first[i, pl.ds(8 * half * ROWS + y + 8, 8, stride=ROWS), :] = cy_ref[
                    i, slot, 8 * half : 8 * half + 8, :
                ].astype(F32)

    @pl.loop(0, 14)
    def _(p):
        base = pl.multiple_of(p * ROWS, 8)
        for t in range(5):
            def at(dx, dy, t=t):
                return base + ((dx + 1) * ROWS + 7 + 8 * t + dy)

            advance(first, at, rate_ref[1, 7 + 8 * t : 15 + 8 * t, :], second, base + (7 + 8 * t), lane)
        pltpu.make_async_copy(second.at[:, pl.ds(base, ROWS)], c2_ref.at[:, pl.ds(base, ROWS)], sem.at[p]).start()

    @pl.loop(0, 14)
    def _(p):
        base = pl.multiple_of(p * ROWS, 8)
        pltpu.make_async_copy(second.at[:, pl.ds(base, ROWS)], c2_ref.at[:, pl.ds(base, ROWS)], sem.at[p]).wait()


def butterfly(a, lane, unit):
    for bit in range(3):
        width = unit << bit
        low = (lane & width) == 0
        b = list(a)
        for j in range(8):
            if j & (1 << bit):
                continue
            k = j | (1 << bit)
            b[j] = jnp.where(low, a[j], pltpu.roll(a[k], width, axis=1))
            b[k] = jnp.where(low, pltpu.roll(a[j], 128 - width, axis=1), a[k])
        a = b
    return a


def step_kernel(
    flags_ref, owner_ref, c2_ref, rim_ref, gl_ref, gr_ref, rate_ref, reduce_ref,
    state_ref, send_ref,
    first, second, state, mean, pack, stage, in_sem, out_sem, send_sem,
):
    me = lax.axis_index("gx") * lax.axis_size("yz") + lax.axis_index("yz")
    lane = lax.broadcasted_iota(jnp.int32, (8, 128), 1)
    inner = pltpu.make_async_copy(c2_ref, second.at[:, 2 * ROWS : 16 * ROWS], in_sem)
    inner.start()

    def place(i, at, rows):
        first[i, at * ROWS + 8 : at * ROWS + 40, :] = rows[0:32, :]
        first[i, at * ROWS + 40 : at * ROWS + 48, :] = rows[32:40, :]
        first[i, at * ROWS : at * ROWS + 8, :] = rows[32:40, :]

    for i in range(19):
        for n, at in enumerate((2, 3, 4, 5)):
            place(i, at, rim_ref[i, n, :, :].astype(F32))
    for ref, faces, places in ((gl_ref, RIGHTWARD, (None, 1, 0)), (gr_ref, LEFTWARD, (None, 6, 7))):
        for n, (i, depth) in enumerate(faces):
            place(i, places[depth], ref[n, :, :].astype(F32))

    @pl.loop(0, 4)
    def _(e):
        above = e // 2
        base = pl.multiple_of((e + 2 * above) * ROWS, 8)
        row = pl.multiple_of((e + 14 * above) * ROWS, 8)
        for t in range(5):
            def at(dx, dy, t=t):
                return base + ((dx + 1) * ROWS + 7 + 8 * t + dy)

            advance(first, at, rate_ref[(e + 1) // 2, 7 + 8 * t : 15 + 8 * t, :], second, row + (7 + 8 * t), lane)

    inner.wait()

    for q in range(4):
        @pl.loop(0, 4)
        def _(part):
            base = pl.multiple_of((4 * q + part) * ROWS, 8)
            for yh in range(4):
                def at(dx, dy, yh=yh):
                    return base + ((dx + 1) * ROWS + 8 + 8 * yh + dy)

                h = shifted(second, at, lane)
                for i in range(19):
                    state[q, 32 * i + 8 * yh : 32 * i + 8 * yh + 8, pl.ds(pl.multiple_of(part * 128, 128), 128)] = h[
                        i
                    ].astype(BF16)

        pltpu.make_async_copy(state.at[q], state_ref.at[q], out_sem.at[q]).start()
        mean[0:608, :] = jnp.dot(state[q, :, :], reduce_ref[...], preferred_element_type=F32)
        for by in range(2):
            for g in range(3):
                rows = [256 * g + 16 * by + 2 * y for y in range(8)]
                a = [mean[pl.ds(r, 8, stride=32), :] + mean[pl.ds(r + 1, 8, stride=32), :] for r in rows]
                a = butterfly(a, lane, 8)
                for z in range(8):
                    pack[8 * by + z, 20 * q + 8 * g : 20 * q + 8 * g + 8, :] = a[z]

    @pl.loop(0, BLK)
    def _(k):
        @pl.when(flags_ref[me * BLK + k] != 0)
        def _():
            stage[k, :, :] = pack[k, 0:80, :].astype(BF16)
            pltpu.make_async_copy(stage.at[k], send_ref.at[owner_ref[me * BLK + k]], send_sem.at[k]).start()

    @pl.loop(0, BLK)
    def _(k):
        @pl.when(flags_ref[me * BLK + k] != 0)
        def _():
            pltpu.make_async_copy(stage.at[k], send_ref.at[0], send_sem.at[k]).wait()

    for q in range(4):
        pltpu.make_async_copy(state.at[q], state_ref.at[q], out_sem.at[q]).wait()


def keep_kernel(flags_ref, owned_ref, state_ref, half_ref, mix, slots, place):
    me = lax.axis_index("gx") * lax.axis_size("yz") + lax.axis_index("yz")
    lane = lax.broadcasted_iota(jnp.int32, (8, 128), 1)

    @pl.loop(0, BLK)
    def _(k):
        place[k] = CAP

    @pl.loop(0, CAP)
    def _(s):
        b = owned_ref[s, 0]

        @pl.when((b >= 0) & (flags_ref[jnp.maximum(b, 0)] == 0))
        def _():
            place[b - me * BLK] = s

    @pl.loop(0, 32)
    def _(c):
        for r in range(CAP * 3):
            slots[c, 8 * r : 8 * r + 8, :] = jnp.zeros((8, 128), F32)

    @pl.loop(0, 16)
    def _(x):
        lanes = pl.ds(pl.multiple_of((x % 4) * 128, 128), 128)
        for yh in range(4):
            for i in range(19):
                mix[yh, 8 * i : 8 * i + 8, :] = state_ref[x // 4, 32 * i + 8 * yh : 32 * i + 8 * yh + 8, lanes].astype(
                    F32
                )
            for g in range(3):
                a = [mix[yh, pl.ds(64 * g + y, 8, stride=8), :] for y in range(8)]
                a = butterfly(a, lane, 16)
                for z in range(8):
                    row = pl.multiple_of(place[(yh // 2) * 8 + z] * 24 + 8 * g, 8)
                    slots[2 * x + yh % 2, pl.ds(row, 8), :] = a[z]

    @pl.loop(0, 32)
    def _(c):
        lanes = pl.ds(pl.multiple_of(c * 128, 128), 128)
        for i in range(19):
            parts = [slots[c, pl.ds(192 * g + i, 8, stride=24), :] for g in range(3)]
            half_ref[i, 0:16, lanes] = jnp.concatenate(parts[:2], axis=0).astype(BF16)
            half_ref[i, 16:24, lanes] = parts[2].astype(BF16)


def refine_kernel(
    flags_ref, owned_ref, recv_ref, kind_ref, expand_ref, half_ref, out_ref,
    taken, rows, wide, product, half, result, in_sem, half_sem, out_sem,
):
    def each_arrival(act):
        @pl.loop(0, CAP)
        def _(s):
            b = owned_ref[s, 0]

            @pl.when((b >= 0) & (flags_ref[jnp.maximum(b, 0)] != 0))
            def _():
                act(s, b // BLK)

    def fetch(s, device):
        pltpu.make_async_copy(recv_ref.at[device], taken.at[s], in_sem.at[s]).start()

    def widen(s, device):
        pltpu.make_async_copy(recv_ref.at[device], taken.at[s], in_sem.at[s]).wait()
        rows[pl.ds(pl.multiple_of(s * 80, 8), 80), :] = taken[s, :, :].astype(F32)

    each_arrival(fetch)

    @pl.loop(0, 19)
    def _(i):
        pltpu.make_async_copy(half_ref.at[i], half.at[i], half_sem.at[i]).start()

    each_arrival(widen)

    kinds = [kind_ref[8 * g : 8 * g + 8, :] for g in range(3)]
    for q in range(4):
        for i in range(19):
            ones, twos = [], []
            for g in range(3):
                v = rows[pl.ds(640 * g + 20 * q + i, 8, stride=80), :]
                ones.append(jnp.where(kinds[g] == 1.0, v, 0.0))
                twos.append(jnp.where(kinds[g] == 2.0, v, 0.0))
            for start, v in ((0, ones), (128, twos)):
                wide[q, 24 * i : 24 * i + 16, start : start + 128] = jnp.concatenate(v[:2], axis=0).astype(BF16)
                wide[q, 24 * i + 16 : 24 * i + 24, start : start + 128] = v[2].astype(BF16)
        product[q, :, :] = jnp.dot(wide[q, :, :], expand_ref[...], preferred_element_type=F32)

    linear = jnp.concatenate([jnp.concatenate([k, k], axis=1) for k in kinds], axis=0) == 2.0
    near = jnp.where(linear, 0.75, 1.0)
    far = jnp.where(linear, 0.25, 0.0)

    @pl.loop(0, 19)
    def _(i):
        pltpu.make_async_copy(half_ref.at[i], half.at[i], half_sem.at[i]).wait()
        start = pl.multiple_of(i * 24, 8)

        def plane(c):
            return product[c // 2, pl.ds(start, 24), (c % 2) * 256 : (c % 2) * 256 + 256]

        for c in range(8):
            mid = plane(c) * near
            for odd in range(2):
                other = max(c - 1, 0) if odd == 0 else min(c + 1, 7)
                x = slice((2 * c + odd) * 256, (2 * c + odd) * 256 + 256)
                value = (mid + plane(other) * far) + half[i, :, x].astype(F32)
                result[i, :, x] = value.astype(BF16)
        pltpu.make_async_copy(result.at[i], out_ref.at[i], out_sem.at[i]).start()

    @pl.loop(0, 19)
    def _(i):
        pltpu.make_async_copy(result.at[i], out_ref.at[i], out_sem.at[i]).wait()


def mean_matrix():
    half = np.zeros((128, 64), np.float32)
    half[np.arange(128), np.arange(128) // 2] = 0.125
    pair = np.zeros((4, 2), np.float32)
    pair[np.arange(4), np.arange(4) // 2] = 1.0
    return np.kron(pair, half)


def expand_matrix():
    inject = np.zeros((8, 16), np.float32)
    linear = np.zeros((8, 16), np.float32)
    for k in range(8):
        for odd, other in ((0, max(k - 1, 0)), (1, min(k + 1, 7))):
            inject[k, 2 * k + odd] = 1.0
            linear[k, 2 * k + odd] += 0.75
            linear[other, 2 * k + odd] += 0.25
    eye = np.eye(2, dtype=np.float32)
    return np.concatenate([np.kron(eye, np.kron(m, m)) for m in (inject, linear)], axis=0)


def ring(count, step):
    return [(i, (i + step) % count) for i in range(count)]


VM = pl.BlockSpec(memory_space=pltpu.VMEM)
SM = pl.BlockSpec(memory_space=pltpu.SMEM)
ANY = pl.BlockSpec(memory_space=pl.ANY)


def struct(shape, dtype):
    return jax.ShapeDtypeStruct(shape, dtype)


def cost(microseconds):
    return pl.CostEstimate(flops=0, bytes_accessed=int(microseconds * 3.0e6), transcendentals=0)


def body(populations, levels, refine_flags, new_owner):
    columns = lax.axis_size("yz")
    slabs = lax.axis_size("gx")
    total = new_owner.shape[0]
    devices = slabs * columns

    top = jnp.transpose(populations[:, :, 30:32, :], (0, 2, 1, 3))
    bottom = jnp.transpose(populations[:, :, 0:2, :], (0, 2, 1, 3))
    low = lax.ppermute(top, "yz", ring(columns, 1))
    high = lax.ppermute(bottom, "yz", ring(columns, -1))

    rate, owned, kind = pl.pallas_call(
        plan_kernel,
        out_shape=(struct((3, ROWS, 128), F32), struct((32, 128), jnp.int32), struct((32, 128), F32)),
        in_specs=[SM, VM, VM],
        out_specs=(VM, VM, VM),
        scratch_shapes=[pltpu.VMEM((32, 128), F32), pltpu.VMEM((32, 128), F32)],
        cost_estimate=cost(2),
        name="plan",
    )(levels, refine_flags.reshape(total // 128, 128), new_owner.reshape(total // 128, 128))

    c1 = pl.pallas_call(
        collide_kernel,
        out_shape=struct((19, 16, 32, 128), BF16),
        in_specs=[VM, VM],
        out_specs=VM,
        cost_estimate=cost(5),
        name="collide",
    )(populations, rate)

    cy, rim, right, left = pl.pallas_call(
        face_kernel,
        out_shape=(
            struct((19, 8, 16, 128), BF16),
            struct((19, 4, FROWS, 128), BF16),
            struct((FACES, FROWS, 128), BF16),
            struct((FACES, FROWS, 128), BF16),
        ),
        in_specs=[ANY, VM, VM, VM],
        out_specs=(VM,) * 4,
        scratch_shapes=[
            pltpu.VMEM((19, 4, 32, 128), BF16),
            pltpu.VMEM((19 * 128 + 128, 128), F32),
            pltpu.SemaphoreType.DMA((2,)),
        ],
        cost_estimate=cost(2),
        name="faces",
    )(c1, low, high, rate)

    from_left = lax.ppermute(right, "gx", ring(slabs, 1))
    from_right = lax.ppermute(left, "gx", ring(slabs, -1))

    c2 = pl.pallas_call(
        inner_kernel,
        out_shape=struct((19, 14 * ROWS, 128), F32),
        in_specs=[VM, VM, VM],
        out_specs=ANY,
        scratch_shapes=[
            pltpu.VMEM((19, 16 * ROWS, 128), F32),
            pltpu.VMEM((19, 14 * ROWS, 128), F32),
            pltpu.SemaphoreType.DMA((14,)),
        ],
        cost_estimate=cost(6),
        name="inner",
    )(c1, cy, rate)

    state, send = pl.pallas_call(
        step_kernel,
        out_shape=(struct((4, 608, 512), BF16), struct((devices, 80, 128), BF16)),
        in_specs=[SM, SM, ANY] + [VM] * 5,
        out_specs=(ANY, ANY),
        scratch_shapes=[
            pltpu.VMEM((19, 8 * ROWS, 128), F32),
            pltpu.VMEM((19, 18 * ROWS, 128), F32),
            pltpu.VMEM((4, 608, 512), BF16),
            pltpu.VMEM((768, 128), F32),
            pltpu.VMEM((BLK, 88, 128), F32),
            pltpu.VMEM((BLK, 80, 128), BF16),
            pltpu.SemaphoreType.DMA,
            pltpu.SemaphoreType.DMA((4,)),
            pltpu.SemaphoreType.DMA((BLK,)),
        ],
        cost_estimate=cost(6),
        name="step",
    )(
        refine_flags, new_owner, c2, rim, from_left, from_right, rate,
        jnp.asarray(mean_matrix(), BF16),
    )

    recv = lax.all_to_all(send, ("gx", "yz"), split_axis=0, concat_axis=0, tiled=True)

    half = pl.pallas_call(
        keep_kernel,
        out_shape=struct((19, CAP, 4096), BF16),
        in_specs=[SM, SM, VM],
        out_specs=VM,
        scratch_shapes=[
            pltpu.VMEM((4, 192, 128), F32),
            pltpu.VMEM((32, (CAP + 1) * 24, 128), F32),
            pltpu.SMEM((BLK,), jnp.int32),
        ],
        cost_estimate=cost(10),
        name="keep",
    )(refine_flags, owned, state)

    migrated = pl.pallas_call(
        refine_kernel,
        out_shape=struct((19, CAP, 4096), BF16),
        in_specs=[SM, SM, ANY, VM, VM, ANY],
        out_specs=ANY,
        scratch_shapes=[
            pltpu.VMEM((CAP, 80, 128), BF16),
            pltpu.VMEM((CAP * 80, 128), F32),
            pltpu.VMEM((4, 456, 256), BF16),
            pltpu.VMEM((4, 456, 512), F32),
            pltpu.VMEM((19, CAP, 4096), BF16),
            pltpu.VMEM((19, CAP, 4096), BF16),
            pltpu.SemaphoreType.DMA((CAP,)),
            pltpu.SemaphoreType.DMA((19,)),
            pltpu.SemaphoreType.DMA((19,)),
        ],
        cost_estimate=cost(5),
        name="refine",
    )(refine_flags, owned, recv, kind, jnp.asarray(expand_matrix(), BF16), half)
    return jnp.transpose(migrated, (1, 0, 2))


def solution(mesh):
    placed = (P(None, "gx", "yz", None), P(), P(), P())
    return jax.shard_map(
        body, mesh=mesh, in_specs=placed, out_specs=P(("gx", "yz"), None, None), check_vma=False
    )
```

time: 101 us -> 91.2 us (0.903)
  blocking collectives: 46.9 us -> 0 us
  Pallas kernels: 28 us -> 50.1 us
  waiting for transfers between devices: 4.29 us -> 18.9 us
  starting transfers between devices: 7.98 us -> 16.4 us
  local copies, waits for them, and re-layouts: 12.5 us -> 5.13 us
    all_to_all x1 -> x0, blocking collectives: 46.9 us -> none  [body(): lax.all_to_all(send, ('gx', 'yz'), split_axis=0, concat_axis=0, tiled=True)]
    pallas_call x4 -> x7, Pallas kernels: 28 us -> 50.1 us  [the longest x1 17.1 us: body(): pl.pallas_call(keep_kernel, out_shape=struct((19, CAP, 4096), BF16), in_s...]
    all_to_all x0 -> x1, waiting for transfers between devices: none -> 18.9 us  [body(): lax.all_to_all(send, ('gx', 'yz'), split_axis=0, concat_axis=0, tiled=True)]
    all_to_all x0 -> x1, starting transfers between devices: none -> 8.32 us  [body(): lax.all_to_all(send, ('gx', 'yz'), split_axis=0, concat_axis=0, tiled=True)]
    pallas_call x1 -> x0, local copies, waits for them, and re-layouts: 6.34 us -> none  [body(): pl.pallas_call(refine_kernel, out_shape=struct((CAP, 19, 4096), BF16), in...]
    ppermute x1, waiting for transfers between devices: 2.89 us -> 0.01 us  [body(): from_left = lax.ppermute(right, 'gx', ring(slabs, 1))]
    unnamed x12, local copies, waits for them, and re-layouts: 1.54 us -> 3.6 us
    slice x7 -> x0, local copies, waits for them, and re-layouts: 1.89 us -> none  [the longest x3 0.87 us: body(): grid = jnp.concatenate([grid[-1:], grid, grid[:1]], axis=0)]
  transfers between devices with their start and end apart: 4 -> 5, of which waited for: 2 -> 1; matrix products, arithmetic and copies ran while one was open for 3% -> 0% of each run, Pallas kernels for 2% -> 35%
where the time goes in v2:
time: 91.2 us; the launch traced here: 90.7 us
  Pallas kernels  50.1 us (55%)
  waiting for transfers between devices  18.9 us (21%)
  starting transfers between devices  16.4 us (18%)
  local copies, waits for them, and re-layouts  5.13 us (6%)
    all_to_all x1, waiting for transfers between devices, body(): lax.all_to_all(send, ('gx', 'yz'), split_axis=0, concat_axis=0, tiled=True)  18.9 us
    pallas_call x1, Pallas kernels, body(): pl.pallas_call(keep_kernel, out_shape=struct((19, CAP, 4096), BF16), in_s...  17.1 us
    pallas_call x1, Pallas kernels, body(): pl.pallas_call(step_kernel, out_shape=(struct((4, 608, 512), BF16), struc...  9.83 us
    all_to_all x1, starting transfers between devices, body(): lax.all_to_all(send, ('gx', 'yz'), split_axis=0, concat_axis=0, tiled=True)  8.32 us
    pallas_call x1, Pallas kernels, body(): pl.pallas_call(inner_kernel, out_shape=struct((19, 14 * ROWS, 128), F32),...  7.04 us
    pallas_call x1, Pallas kernels, body(): pl.pallas_call(refine_kernel, out_shape=struct((19, CAP, 4096), BF16), in...  5.43 us
    pallas_call x1, Pallas kernels, body(): pl.pallas_call(collide_kernel, out_shape=struct((19, 16, 32, 128), BF16),...  5.36 us
    ppermute x1, starting transfers between devices, body(): from_right = lax.ppermute(left, 'gx', ring(slabs, -1))  3.71 us
  transfers between devices with their start and end apart: 5, of which 1 were waited for; matrix products, arithmetic and copies ran while one was open for 0% of the time, Pallas kernels for 35%

profile of v2, /device:TPU:1, one launch (start us, length us, event | category | flops | bytes accessed | tf_op | source)
XLA Modules:
  0.0 90.7 jit_solution(8660686950437933383)
XLA Ops:
  0.0 1.5 %fusion = (bf16[19,16,2,128]{3,2,1,0:T(2,128)(2,1)S(1)}, bf16[19,16,2,128]{3,2,1,0:T(2,128)(2,1)S(1)}) fusion(bf16[19,16,32,128]{3,2,1,0:T(8,128)(2,1)} %pop_ref.1), kind=kLoop, calls=%fused_computation.2 | loop fusion | bytes 622592 | tf_op jit(solution)/shard_map/slice | solution.py:452
  1.6 3.0 %collective-permute-start = (bf16[19,2,16,128]{3,2,1,0:T(8,128)(2,1)S(1)}, bf16[19,2,16,128]{3,2,1,0:T(8,128)(2,1)S(1)}, u32[]{:S(2)}, u32[]{:S(2)}) collective-permute-start(bf16[19,2,16,128]{3,2,1,0:T(8,128)(2,1)S(1)} %bitcast.9), channel_id=1, source_target_pairs={{0,1},{1,2},{2,3},{3,4},{4,5},{5,6},{6,7},{7,0},{8,9},{9,10},{10,1... | collective-permute-start | bytes 466952 | tf_op jit(solution)/shard_map/ppermute | solution.py:453
  4.6 0.0 collective-permute-start.1
  4.6 1.8 %plan.1 = (f32[3,48,128]{2,1,0:T(8,128)}, s32[32,128]{1,0:T(8,128)}, f32[32,128]{1,0:T(8,128)}) custom-call(s32[2048]{0:T(1024)} %levels_ref.1, s32[16,128]{1,0:T(8,128)} %bitcast.11, s32[16,128]{1,0:T(8,128)} %bitcast.12), custom_call_target="tpu_custom_call" | custom-call | bytes 6000000 | tf_op jit(solution)/shard_map/plan/pallas_call | solution.py:456
  6.4 5.4 %collide.1.c1_ref = bf16[19,16,32,128]{3,2,1,0:T(8,128)(2,1)} custom-call(bf16[19,16,32,128]{3,2,1,0:T(8,128)(2,1)} %pop_ref.1, f32[3,48,128]{2,1,0:T(8,128)} %get-tuple-element.15.rate_ref), custom_call_target="tpu_custom_call" | custom-call | bytes 15000000 | tf_op jit(solution)/shard_map/collide/pallas_call | solution.py:466
  11.8 0.0 collective-permute-done.low_ref
  11.8 0.0 copy-start.3
  11.8 0.0 collective-permute-done.1.high_ref
  11.8 0.7 copy-done.3
  12.4 0.0 copy-start.4
  12.4 0.7 copy-done.4
  13.1 3.6 %faces.1 = (bf16[19,8,16,128]{3,2,1,0:T(8,128)(2,1)}, bf16[19,4,40,128]{3,2,1,0:T(8,128)(2,1)}, bf16[21,40,128]{2,1,0:T(8,128)(2,1)}, bf16[21,40,128]{2,1,0:T(8,128)(2,1)}) custom-call(bf16[19,16,32,128]{3,2,1,0:T(8,128)(2,1)} %collide.1.c1_ref, bf16[19,2,16,128]{3,2,1,0:T(8,128)(2,1)} %copy-done.3, bf16[19,2,16,128]{3,2,1,0:T(8,128)(2,1)} %copy-done.4, ...), custom_call_target="tpu_custom_call" | custom-call | bytes 6000000 | tf_op jit(solution)/shard_map/faces/pallas_call | solution.py:475
  16.7 1.4 %collective-permute-start.2 = (bf16[21,40,128]{2,1,0:T(8,128)(2,1)}, bf16[21,40,128]{2,1,0:T(8,128)(2,1)S(1)}, u32[]{:S(2)}, u32[]{:S(2)}) collective-permute-start(bf16[21,40,128]{2,1,0:T(8,128)(2,1)} %get-tuple-element.18), channel_id=1, source_target_pairs={{0,8},{8,16},{16,24},{24,32},{32,40},{40,48},{48,56},{56,64},{64,7... | collective-permute-start | bytes 645128 | tf_op jit(solution)/shard_map/ppermute | solution.py:494
  18.0 3.7 %collective-permute-start.3 = (bf16[21,40,128]{2,1,0:T(8,128)(2,1)}, bf16[21,40,128]{2,1,0:T(8,128)(2,1)S(1)}, u32[]{:S(2)}, u32[]{:S(2)}) collective-permute-start(bf16[21,40,128]{2,1,0:T(8,128)(2,1)} %get-tuple-element.19), channel_id=1, source_target_pairs={{0,120},{8,0},{16,8},{24,16},{32,24},{40,32},{48,40},{56,48},{64,5... | collective-permute-start | bytes 645128 | tf_op jit(solution)/shard_map/ppermute | solution.py:495
  21.8 7.0 %inner.1.c2_ref = f32[19,672,128]{2,1,0:T(8,128)} custom-call(bf16[19,16,32,128]{3,2,1,0:T(8,128)(2,1)} %collide.1.c1_ref, bf16[19,8,16,128]{3,2,1,0:T(8,128)(2,1)} %get-tuple-element.16.cy_ref, f32[3,48,128]{2,1,0:T(8,128)} %get-tuple-element.15.rate_ref), custom_call_target="tpu_custom_call" | custom-call | bytes 18000000 | tf_op jit(solution)/shard_map/inner/pallas_call | solution.py:497
  28.8 0.0 collective-permute-done.2.gl_ref
  28.8 0.0 copy-start.1
  28.8 0.0 collective-permute-done.3.gr_ref
  28.8 0.0 copy-start.2
  28.8 0.7 copy-done.1
  29.5 0.1 copy-done.2
  29.6 9.8 %step.1 = (bf16[4,608,512]{2,1,0:T(8,128)(2,1)}, bf16[128,80,128]{2,1,0:T(8,128)(2,1)}) custom-call(s32[2048]{0:T(1024)} %flags_ref.5, s32[2048]{0:T(1024)} %owner_ref.1, f32[19,672,128]{2,1,0:T(8,128)} %inner.1.c2_ref, bf16[19,4,40,128]{3,2,1,0:T(8,128)(2,1)} %get-tuple-element.17.rim_ref, bf16[21,40,128]{2,1,0:T(8,128)(2,1)} %copy-done.1, ...), custom_call_target="tpu_custom_call" | custom-call | bytes 18000000 | tf_op jit(solution)/shard_map/step/pallas_call | solution.py:511
  39.4 8.3 %all-to-all-start = ((bf16[128,80,128]{2,1,0:T(8,128)(2,1)}), bf16[128,80,128]{2,1,0:T(8,128)(2,1)S(1)}, u32[]{:S(2)}, u32[]{:S(2)}) async-start(bf16[128,80,128]{2,1,0:T(8,128)(2,1)} %get-tuple-element.20), calls=%async_computation | async-start | bytes 5242880 | tf_op jit(solution)/shard_map/all_to_all | solution.py:534
  47.7 17.1 %keep.1.half_ref = bf16[19,24,4096]{2,1,0:T(8,128)(2,1)} custom-call(s32[2048]{0:T(1024)} %flags_ref.5, s32[32,128]{1,0:T(8,128)} %get-tuple-element.14.owned_ref, bf16[4,608,512]{2,1,0:T(8,128)(2,1)} %get-tuple-element.22.state_ref), custom_call_target="tpu_custom_call" | custom-call | bytes 30000000 | tf_op jit(solution)/shard_map/keep/pallas_call | solution.py:536
  64.9 18.9 %all-to-all-done.recv_ref = bf16[128,80,128]{2,1,0:T(8,128)(2,1)S(1)} async-done(((bf16[128,80,128]{2,1,0:T(8,128)(2,1)}), bf16[128,80,128]{2,1,0:T(8,128)(2,1)S(1)}, u32[]{:S(2)}, u32[]{:S(2)}) %all-to-all-start) | async-done | bytes 2621472 | tf_op jit(solution)/shard_map/all_to_all | solution.py:534
  83.8 0.0 copy-start
  83.8 1.5 %copy-done = bf16[128,80,128]{2,1,0:T(8,128)(2,1)} copy-done((bf16[128,80,128]{2,1,0:T(8,128)(2,1)}, bf16[128,80,128]{2,1,0:T(8,128)(2,1)S(1)}, u32[]{:S(2)}) %copy-start) | copy-done | bytes 2621464
  85.3 5.4 %refine.1 = bf16[19,24,4096]{2,1,0:T(8,128)(2,1)} custom-call(s32[2048]{0:T(1024)} %flags_ref.5, s32[32,128]{1,0:T(8,128)} %get-tuple-element.14.owned_ref, bf16[128,80,128]{2,1,0:T(8,128)(2,1)} %copy-done, f32[32,128]{1,0:T(8,128)} %get-tuple-element.21.kind_ref, bf16[256,512]{1,0:T(8,128)(2,1)} %constant.5.clone.expand_ref, bf16[19,24,4096]{2,1,0:T(8,128)(2,1)} %keep.1.half_ref), custom_call_target="tpu_custom_call" | custom-call | bytes 15000000 | tf_op jit(solution)/shard_map/refine/pallas_call | solution.py:550
  (2 shorter events, 0.0 us)
Async XLA Ops:
  1.6 10.2 %collective-permute-start = (bf16[19,2,16,128]{3,2,1,0:T(8,128)(2,1)S(1)}, bf16[19,2,16,128]{3,2,1,0:T(8,128)(2,1)S(1)}, u32[]{:S(2)}, u32[]{:S(2)}) collective-permute-start(bf16[19,2,16,128]{3,2,1,0:T(8,128)(2,1)S(1)} %bitcast.9), channel_id=1, source_target_pairs={{0,1},{1,2},{2,3},{3,4},{4,5},{5,6},{6,7},{7,0},{8,9},{9,10},{10,1... | collective-permute-start | bytes 466952 | tf_op jit(solution)/shard_map/ppermute | solution.py:453
  4.6 7.2 %collective-permute-start.1 = (bf16[19,2,16,128]{3,2,1,0:T(8,128)(2,1)S(1)}, bf16[19,2,16,128]{3,2,1,0:T(8,128)(2,1)S(1)}, u32[]{:S(2)}, u32[]{:S(2)}) collective-permute-start(bf16[19,2,16,128]{3,2,1,0:T(8,128)(2,1)S(1)} %bitcast.10), channel_id=1, source_target_pairs={{0,7},{1,0},{2,1},{3,2},{4,3},{5,4},{6,5},{7,6},{8,15},{9,8},{10,9... | collective-permute-start | bytes 466952 | tf_op jit(solution)/shard_map/ppermute | solution.py:454
  11.8 0.7 copy-start.3
  12.4 0.7 copy-start.4
  16.7 12.1 %collective-permute-start.2 = (bf16[21,40,128]{2,1,0:T(8,128)(2,1)}, bf16[21,40,128]{2,1,0:T(8,128)(2,1)S(1)}, u32[]{:S(2)}, u32[]{:S(2)}) collective-permute-start(bf16[21,40,128]{2,1,0:T(8,128)(2,1)} %get-tuple-element.18), channel_id=1, source_target_pairs={{0,8},{8,16},{16,24},{24,32},{32,40},{40,48},{48,56},{56,64},{64,7... | collective-permute-start | bytes 645128 | tf_op jit(solution)/shard_map/ppermute | solution.py:494
  18.0 10.8 %collective-permute-start.3 = (bf16[21,40,128]{2,1,0:T(8,128)(2,1)}, bf16[21,40,128]{2,1,0:T(8,128)(2,1)S(1)}, u32[]{:S(2)}, u32[]{:S(2)}) collective-permute-start(bf16[21,40,128]{2,1,0:T(8,128)(2,1)} %get-tuple-element.19), channel_id=1, source_target_pairs={{0,120},{8,0},{16,8},{24,16},{32,24},{40,32},{48,40},{56,48},{64,5... | collective-permute-start | bytes 645128 | tf_op jit(solution)/shard_map/ppermute | solution.py:495
  28.8 0.7 copy-start.1
  28.8 0.7 copy-start.2
  39.4 44.4 %all-to-all-start = ((bf16[128,80,128]{2,1,0:T(8,128)(2,1)}), bf16[128,80,128]{2,1,0:T(8,128)(2,1)S(1)}, u32[]{:S(2)}, u32[]{:S(2)}) async-start(bf16[128,80,128]{2,1,0:T(8,128)(2,1)} %get-tuple-element.20), calls=%async_computation | async-start | bytes 5242880 | tf_op jit(solution)/shard_map/all_to_all | solution.py:534
  83.8 1.5 %copy-start = (bf16[128,80,128]{2,1,0:T(8,128)(2,1)}, bf16[128,80,128]{2,1,0:T(8,128)(2,1)S(1)}, u32[]{:S(2)}) copy-start(bf16[128,80,128]{2,1,0:T(8,128)(2,1)S(1)} %all-to-all-done.recv_ref) | copy-start | bytes 7864324

commit v3 on v2

--- a/solution.py
+++ b/solution.py
@@ -63,11 +63,9 @@
     return out
 
 
-def plan_kernel(levels_ref, flags_ref, owner_ref, rate_ref, owned_ref, kind_ref, part, kinds):
+def rate_kernel(levels_ref, rate_ref):
     slab, column = lax.axis_index("gx"), lax.axis_index("yz")
     slabs, columns = lax.axis_size("gx"), lax.axis_size("yz")
-    me = slab * columns + column
-
     group = lax.broadcasted_iota(jnp.int32, (8, 128), 1) // BS
     for plane in range(3):
         row = lax.rem(slab + (plane + slabs - 1), slabs) * (2 * columns)
@@ -80,6 +78,10 @@
             for at in range(first, last, 8):
                 rate_ref[plane, at : at + 8, :] = rate
 
+
+def plan_kernel(flags_ref, owner_ref, after_ref, owned_ref, kind_ref, part, kinds):
+    del after_ref
+    me = lax.axis_index("gx") * lax.axis_size("yz") + lax.axis_index("yz")
     rows = owner_ref.shape[0]
     mine = owner_ref[...] == me
     mask = jnp.where(mine, 1.0, 0.0)
@@ -103,15 +105,27 @@
     kind_ref[...] = jnp.broadcast_to(jnp.sum(kinds[...], axis=1, keepdims=True), kinds.shape)
 
 
-def collide_kernel(pop_ref, rate_ref, c1_ref):
-    @pl.loop(0, 16)
-    def _(x):
-        for t in range(4):
-            rows = slice(8 * t, 8 * t + 8)
-            h = [pop_ref[i, x, rows, :].astype(F32) for i in range(19)]
-            out = collide(h, rate_ref[1, 8 + 8 * t : 16 + 8 * t, :])
-            for i in range(19):
-                c1_ref[i, x, rows, :] = out[i].astype(BF16)
+def collide_kernel(pop_ref, rate_ref, c1_ref, planes, sem):
+    def fetch(part):
+        at = pl.ds(part * 4, 4)
+        return pltpu.make_async_copy(pop_ref.at[:, at], planes.at[:, at], sem.at[part])
+
+    for part in range(4):
+        fetch(part).start()
+
+    @pl.loop(0, 4)
+    def _(part):
+        fetch(part).wait()
+
+        @pl.loop(0, 4)
+        def _(step):
+            x = part * 4 + step
+            for t in range(4):
+                rows = slice(8 * t, 8 * t + 8)
+                h = [planes[i, x, rows, :].astype(F32) for i in range(19)]
+                out = collide(h, rate_ref[1, 8 + 8 * t : 16 + 8 * t, :])
+                for i in range(19):
+                    c1_ref[i, x, rows, :] = out[i].astype(BF16)
 
 
 def face_kernel(c1_ref, low_ref, high_ref, rate_ref, cy_ref, rim_ref, right_ref, left_ref, planes, edge, sem):
@@ -165,13 +179,22 @@
 
 
 def advance(source, at, rate, target, row, lane):
-    h = shifted(source, at, lane)
-    out = collide([v.astype(BF16).astype(F32) for v in h], rate)
+    out = collide(shifted(source, at, lane), rate)
     for i in range(19):
-        target[i, pl.ds(row, 8), :] = out[i].astype(BF16).astype(F32)
-
-
-def inner_kernel(c1_ref, cy_ref, rate_ref, c2_ref, first, second, sem):
+        target[i, pl.ds(row, 8), :] = out[i]
+
+
+def settle(source, base, target, part, lanes, lane):
+    for yh in range(4):
+        def at(dx, dy, yh=yh):
+            return base + ((dx + 1) * ROWS + 8 + 8 * yh + dy)
+
+        h = shifted(source, at, lane)
+        for i in range(19):
+            target[part, 32 * i + 8 * yh : 32 * i + 8 * yh + 8, lanes] = h[i].astype(BF16)
+
+
+def inner_kernel(c1_ref, cy_ref, rate_ref, rest_ref, state_ref, first, second, sem):
     lane = lax.broadcasted_iota(jnp.int32, (8, 128), 1)
 
     @pl.loop(0, 16)
@@ -194,12 +217,23 @@
                 return base + ((dx + 1) * ROWS + 7 + 8 * t + dy)
 
             advance(first, at, rate_ref[1, 7 + 8 * t : 15 + 8 * t, :], second, base + (7 + 8 * t), lane)
-        pltpu.make_async_copy(second.at[:, pl.ds(base, ROWS)], c2_ref.at[:, pl.ds(base, ROWS)], sem.at[p]).start()
-
-    @pl.loop(0, 14)
+
+    copies = [
+        pltpu.make_async_copy(
+            second.at[:, a * ROWS : (a + 2) * ROWS], rest_ref.at[:, b * ROWS : (b + 2) * ROWS], sem.at[n]
+        )
+        for n, (a, b) in enumerate(((0, 0), (12, 2)))
+    ]
+    for copy in copies:
+        copy.start()
+
+    @pl.loop(0, 12)
     def _(p):
-        base = pl.multiple_of(p * ROWS, 8)
-        pltpu.make_async_copy(second.at[:, pl.ds(base, ROWS)], c2_ref.at[:, pl.ds(base, ROWS)], sem.at[p]).wait()
+        lanes = pl.ds(pl.multiple_of((p % 2) * 128, 128), 128)
+        settle(second, pl.multiple_of(p * ROWS, 8), state_ref, p // 2, lanes, lane)
+
+    for copy in copies:
+        copy.wait()
 
 
 def butterfly(a, lane, unit):
@@ -218,14 +252,14 @@
 
 
 def step_kernel(
-    flags_ref, owner_ref, c2_ref, rim_ref, gl_ref, gr_ref, rate_ref, reduce_ref,
-    state_ref, send_ref,
-    first, second, state, mean, pack, stage, in_sem, out_sem, send_sem,
+    flags_ref, owner_ref, rest_ref, rim_ref, gl_ref, gr_ref, rate_ref, reduce_ref, inner_ref,
+    outer_ref, send_ref,
+    first, second, mean, mix, pack, stage, in_sem, send_sem,
 ):
     me = lax.axis_index("gx") * lax.axis_size("yz") + lax.axis_index("yz")
     lane = lax.broadcasted_iota(jnp.int32, (8, 128), 1)
-    inner = pltpu.make_async_copy(c2_ref, second.at[:, 2 * ROWS : 16 * ROWS], in_sem)
-    inner.start()
+    rest = pltpu.make_async_copy(rest_ref, second.at[:, 2 * ROWS : 6 * ROWS], in_sem)
+    rest.start()
 
     def place(i, at, rows):
         first[i, at * ROWS + 8 : at * ROWS + 40, :] = rows[0:32, :]
@@ -243,35 +277,38 @@
     def _(e):
         above = e // 2
         base = pl.multiple_of((e + 2 * above) * ROWS, 8)
-        row = pl.multiple_of((e + 14 * above) * ROWS, 8)
+        row = pl.multiple_of((e + 4 * above) * ROWS, 8)
         for t in range(5):
             def at(dx, dy, t=t):
                 return base + ((dx + 1) * ROWS + 7 + 8 * t + dy)
 
             advance(first, at, rate_ref[(e + 1) // 2, 7 + 8 * t : 15 + 8 * t, :], second, row + (7 + 8 * t), lane)
 
-    inner.wait()
+    rest.wait()
+
+    @pl.loop(0, 4)
+    def _(e):
+        above = e // 2
+        lanes = pl.ds(pl.multiple_of((e % 2) * 128, 128), 128)
+        settle(second, pl.multiple_of((e + 2 * above) * ROWS, 8), outer_ref, above, lanes, lane)
 
     for q in range(4):
-        @pl.loop(0, 4)
-        def _(part):
-            base = pl.multiple_of((4 * q + part) * ROWS, 8)
-            for yh in range(4):
-                def at(dx, dy, yh=yh):
-                    return base + ((dx + 1) * ROWS + 8 + 8 * yh + dy)
-
-                h = shifted(second, at, lane)
-                for i in range(19):
-                    state[q, 32 * i + 8 * yh : 32 * i + 8 * yh + 8, pl.ds(pl.multiple_of(part * 128, 128), 128)] = h[
-                        i
-                    ].astype(BF16)
-
-        pltpu.make_async_copy(state.at[q], state_ref.at[q], out_sem.at[q]).start()
-        mean[0:608, :] = jnp.dot(state[q, :, :], reduce_ref[...], preferred_element_type=F32)
+        total = None
+        for par in range(2):
+            c = 2 * q + par
+            pair = outer_ref[c // 7, :, :] if c in (0, 7) else inner_ref[c - 1, :, :]
+            term = jnp.dot(pair, reduce_ref[par, :, :], preferred_element_type=F32)
+            total = term if total is None else total + term
+        mean[q, :, :] = total
+        for i in range(19):
+            for by in range(2):
+                at = 32 * i + 16 * by
+                mix[q, by, 8 * i : 8 * i + 8, :] = (
+                    mean[q, pl.ds(at, 8, stride=2), :] + mean[q, pl.ds(at + 1, 8, stride=2), :]
+                )
         for by in range(2):
             for g in range(3):
-                rows = [256 * g + 16 * by + 2 * y for y in range(8)]
-                a = [mean[pl.ds(r, 8, stride=32), :] + mean[pl.ds(r + 1, 8, stride=32), :] for r in rows]
+                a = [mix[q, by, pl.ds(64 * g + y, 8, stride=8), :] for y in range(8)]
                 a = butterfly(a, lane, 8)
                 for z in range(8):
                     pack[8 * by + z, 20 * q + 8 * g : 20 * q + 8 * g + 8, :] = a[z]
@@ -289,11 +326,8 @@
         def _():
             pltpu.make_async_copy(stage.at[k], send_ref.at[0], send_sem.at[k]).wait()
 
-    for q in range(4):
-        pltpu.make_async_copy(state.at[q], state_ref.at[q], out_sem.at[q]).wait()
-
-
-def keep_kernel(flags_ref, owned_ref, state_ref, half_ref, mix, slots, place):
+
+def keep_kernel(flags_ref, owned_ref, inner_ref, outer_ref, half_ref, mix, slots, place):
     me = lax.axis_index("gx") * lax.axis_size("yz") + lax.axis_index("yz")
     lane = lax.broadcasted_iota(jnp.int32, (8, 128), 1)
 
@@ -314,20 +348,26 @@
         for r in range(CAP * 3):
             slots[c, 8 * r : 8 * r + 8, :] = jnp.zeros((8, 128), F32)
 
-    @pl.loop(0, 16)
-    def _(x):
-        lanes = pl.ds(pl.multiple_of((x % 4) * 128, 128), 128)
+    def spread(state_ref, pair, x):
+        lanes = pl.ds(pl.multiple_of((x % 2) * 128, 128), 128)
         for yh in range(4):
             for i in range(19):
-                mix[yh, 8 * i : 8 * i + 8, :] = state_ref[x // 4, 32 * i + 8 * yh : 32 * i + 8 * yh + 8, lanes].astype(
-                    F32
-                )
+                tile = state_ref[pair, 32 * i + 8 * yh : 32 * i + 8 * yh + 8, lanes]
+                mix[yh, 8 * i : 8 * i + 8, :] = tile.astype(F32)
             for g in range(3):
                 a = [mix[yh, pl.ds(64 * g + y, 8, stride=8), :] for y in range(8)]
                 a = butterfly(a, lane, 16)
                 for z in range(8):
                     row = pl.multiple_of(place[(yh // 2) * 8 + z] * 24 + 8 * g, 8)
                     slots[2 * x + yh % 2, pl.ds(row, 8), :] = a[z]
+
+    @pl.loop(2, 14)
+    def _(x):
+        spread(inner_ref, x // 2 - 1, x)
+
+    @pl.loop(0, 4)
+    def _(e):
+        spread(outer_ref, e // 2, e + 12 * (e // 2))
 
     @pl.loop(0, 32)
     def _(c):
@@ -356,7 +396,8 @@
 
     def widen(s, device):
         pltpu.make_async_copy(recv_ref.at[device], taken.at[s], in_sem.at[s]).wait()
-        rows[pl.ds(pl.multiple_of(s * 80, 8), 80), :] = taken[s, :, :].astype(F32)
+        for r in range(10):
+            rows[pl.ds(192 * r + s, 8, stride=24), :] = taken[s, 8 * r : 8 * r + 8, :].astype(F32)
 
     each_arrival(fetch)
 
@@ -371,7 +412,8 @@
         for i in range(19):
             ones, twos = [], []
             for g in range(3):
-                v = rows[pl.ds(640 * g + 20 * q + i, 8, stride=80), :]
+                start = 24 * (20 * q + i) + 8 * g
+                v = rows[start : start + 8, :]
                 ones.append(jnp.where(kinds[g] == 1.0, v, 0.0))
                 twos.append(jnp.where(kinds[g] == 2.0, v, 0.0))
             for start, v in ((0, ones), (128, twos)):
@@ -396,8 +438,7 @@
             for odd in range(2):
                 other = max(c - 1, 0) if odd == 0 else min(c + 1, 7)
                 x = slice((2 * c + odd) * 256, (2 * c + odd) * 256 + 256)
-                value = (mid + plane(other) * far) + half[i, :, x].astype(F32)
-                result[i, :, x] = value.astype(BF16)
+                result[i, :, x] = (mid + plane(other) * far).astype(BF16) + half[i, :, x]
         pltpu.make_async_copy(result.at[i], out_ref.at[i], out_sem.at[i]).start()
 
     @pl.loop(0, 19)
@@ -408,9 +449,9 @@
 def mean_matrix():
     half = np.zeros((128, 64), np.float32)
     half[np.arange(128), np.arange(128) // 2] = 0.125
-    pair = np.zeros((4, 2), np.float32)
-    pair[np.arange(4), np.arange(4) // 2] = 1.0
-    return np.kron(pair, half)
+    both = np.concatenate([half, half], axis=0)
+    none = np.zeros_like(both)
+    return np.stack([np.concatenate([both, none], axis=1), np.concatenate([none, both], axis=1)])
 
 
 def expand_matrix():
@@ -432,14 +473,23 @@
 VM = pl.BlockSpec(memory_space=pltpu.VMEM)
 SM = pl.BlockSpec(memory_space=pltpu.SMEM)
 ANY = pl.BlockSpec(memory_space=pl.ANY)
+HBM = pl.BlockSpec(memory_space=pltpu.HBM)
 
 
 def struct(shape, dtype):
     return jax.ShapeDtypeStruct(shape, dtype)
 
 
+def in_hbm(array):
+    return pltpu.with_memory_space_constraint(array, pltpu.HBM)
+
+
 def cost(microseconds):
     return pl.CostEstimate(flops=0, bytes_accessed=int(microseconds * 3.0e6), transcendentals=0)
+
+
+def limit(mebibytes):
+    return pltpu.CompilerParams(vmem_limit_bytes=mebibytes << 20)
 
 
 def body(populations, levels, refine_flags, new_owner):
@@ -453,24 +503,26 @@
     low = lax.ppermute(top, "yz", ring(columns, 1))
     high = lax.ppermute(bottom, "yz", ring(columns, -1))
 
-    rate, owned, kind = pl.pallas_call(
-        plan_kernel,
-        out_shape=(struct((3, ROWS, 128), F32), struct((32, 128), jnp.int32), struct((32, 128), F32)),
-        in_specs=[SM, VM, VM],
-        out_specs=(VM, VM, VM),
-        scratch_shapes=[pltpu.VMEM((32, 128), F32), pltpu.VMEM((32, 128), F32)],
-        cost_estimate=cost(2),
-        name="plan",
-    )(levels, refine_flags.reshape(total // 128, 128), new_owner.reshape(total // 128, 128))
+    rate = pl.pallas_call(
+        rate_kernel,
+        out_shape=struct((3, ROWS, 128), F32),
+        in_specs=[SM],
+        out_specs=VM,
+        compiler_params=limit(4),
+        cost_estimate=cost(1),
+        name="rates",
+    )(in_hbm(levels))
 
     c1 = pl.pallas_call(
         collide_kernel,
         out_shape=struct((19, 16, 32, 128), BF16),
-        in_specs=[VM, VM],
+        in_specs=[HBM, VM],
         out_specs=VM,
+        scratch_shapes=[pltpu.VMEM((19, 16, 32, 128), BF16), pltpu.SemaphoreType.DMA((4,))],
+        compiler_params=limit(8),
         cost_estimate=cost(5),
         name="collide",
-    )(populations, rate)
+    )(in_hbm(populations), rate)
 
     cy, rim, right, left = pl.pallas_call(
         face_kernel,
@@ -487,6 +539,7 @@
             pltpu.VMEM((19 * 128 + 128, 128), F32),
             pltpu.SemaphoreType.DMA((2,)),
         ],
+        compiler_params=limit(8),
         cost_estimate=cost(2),
         name="faces",
     )(c1, low, high, rate)
@@ -494,63 +547,76 @@
     from_left = lax.ppermute(right, "gx", ring(slabs, 1))
     from_right = lax.ppermute(left, "gx", ring(slabs, -1))
 
-    c2 = pl.pallas_call(
+    rest, inner = pl.pallas_call(
         inner_kernel,
-        out_shape=struct((19, 14 * ROWS, 128), F32),
+        out_shape=(struct((19, 4 * ROWS, 128), F32), struct((6, 608, 256), BF16)),
         in_specs=[VM, VM, VM],
-        out_specs=ANY,
+        out_specs=(ANY, VM),
         scratch_shapes=[
             pltpu.VMEM((19, 16 * ROWS, 128), F32),
             pltpu.VMEM((19, 14 * ROWS, 128), F32),
-            pltpu.SemaphoreType.DMA((14,)),
+            pltpu.SemaphoreType.DMA((2,)),
         ],
+        compiler_params=limit(20),
         cost_estimate=cost(6),
         name="inner",
     )(c1, cy, rate)
 
-    state, send = pl.pallas_call(
+    outer, send = pl.pallas_call(
         step_kernel,
-        out_shape=(struct((4, 608, 512), BF16), struct((devices, 80, 128), BF16)),
-        in_specs=[SM, SM, ANY] + [VM] * 5,
-        out_specs=(ANY, ANY),
+        out_shape=(struct((2, 608, 256), BF16), pltpu.HBM((devices, 80, 128), BF16)),
+        in_specs=[SM, SM, ANY] + [VM] * 6,
+        out_specs=(VM, HBM),
         scratch_shapes=[
             pltpu.VMEM((19, 8 * ROWS, 128), F32),
-            pltpu.VMEM((19, 18 * ROWS, 128), F32),
-            pltpu.VMEM((4, 608, 512), BF16),
-            pltpu.VMEM((768, 128), F32),
+            pltpu.VMEM((19, 8 * ROWS, 128), F32),
+            pltpu.VMEM((4, 608, 128), F32),
+            pltpu.VMEM((4, 2, 192, 128), F32),
             pltpu.VMEM((BLK, 88, 128), F32),
             pltpu.VMEM((BLK, 80, 128), BF16),
             pltpu.SemaphoreType.DMA,
-            pltpu.SemaphoreType.DMA((4,)),
             pltpu.SemaphoreType.DMA((BLK,)),
         ],
+        compiler_params=limit(18),
         cost_estimate=cost(6),
         name="step",
     )(
-        refine_flags, new_owner, c2, rim, from_left, from_right, rate,
-        jnp.asarray(mean_matrix(), BF16),
+        refine_flags, new_owner, rest, rim, from_left, from_right, rate,
+        jnp.asarray(mean_matrix(), BF16), inner,
     )
 
     recv = lax.all_to_all(send, ("gx", "yz"), split_axis=0, concat_axis=0, tiled=True)
+
+    owned, kind = pl.pallas_call(
+        plan_kernel,
+        out_shape=(struct((32, 128), jnp.int32), struct((32, 128), F32)),
+        in_specs=[VM, VM, ANY],
+        out_specs=(VM, VM),
+        scratch_shapes=[pltpu.VMEM((32, 128), F32), pltpu.VMEM((32, 128), F32)],
+        compiler_params=limit(4),
+        cost_estimate=cost(2),
+        name="plan",
+    )(refine_flags.reshape(total // 128, 128), new_owner.reshape(total // 128, 128), outer)
 
     half = pl.pallas_call(
         keep_kernel,
-        out_shape=struct((19, CAP, 4096), BF16),
-        in_specs=[SM, SM, VM],
+        out_shape=pltpu.HBM((19, CAP, 4096), BF16),
+        in_specs=[SM, SM, VM, VM],
         out_specs=VM,
         scratch_shapes=[
             pltpu.VMEM((4, 192, 128), F32),
             pltpu.VMEM((32, (CAP + 1) * 24, 128), F32),
             pltpu.SMEM((BLK,), jnp.int32),
         ],
+        compiler_params=limit(20),
         cost_estimate=cost(10),
         name="keep",
-    )(refine_flags, owned, state)
+    )(refine_flags, owned, inner, outer)
 
     migrated = pl.pallas_call(
         refine_kernel,
         out_shape=struct((19, CAP, 4096), BF16),
-        in_specs=[SM, SM, ANY, VM, VM, ANY],
+        in_specs=[SM, SM, ANY, VM, VM, HBM],
         out_specs=ANY,
         scratch_shapes=[
             pltpu.VMEM((CAP, 80, 128), BF16),
@@ -563,9 +629,10 @@
             pltpu.SemaphoreType.DMA((19,)),
             pltpu.SemaphoreType.DMA((19,)),
         ],
+        compiler_params=limit(18),
         cost_estimate=cost(5),
         name="refine",
-    )(refine_flags, owned, recv, kind, jnp.asarray(expand_matrix(), BF16), half)
+    )(refine_flags, owned, recv, kind, jnp.asarray(expand_matrix(), BF16), in_hbm(half))
     return jnp.transpose(migrated, (1, 0, 2))
 
 

time: 91.2 us -> 76.6 us (0.84)
  Pallas kernels: 50.1 us -> 35.9 us
  local copies, waits for them, and re-layouts: 5.13 us -> 3.11 us
  starting transfers between devices: 16.4 us -> 18.4 us
    pallas_call x4 -> x5, Pallas kernels: 35.8 us -> 26.6 us  [the longest x1 15.8 us: body(): pl.pallas_call(keep_kernel, out_shape=pltpu.HBM((19, CAP, 4096), BF16), i...]
    pallas_call x1, Pallas kernels: 3.57 us -> 0.63 us  [body(): pl.pallas_call(face_kernel, out_shape=(struct((19, 8, 16, 128), BF16), st...]
    pallas_call x1, Pallas kernels: 5.36 us -> 3.31 us  [body(): pl.pallas_call(collide_kernel, out_shape=struct((19, 16, 32, 128), BF16),...]
    unnamed x12 -> x14, local copies, waits for them, and re-layouts: 3.6 us -> 1.59 us
    all_to_all x1, starting transfers between devices: 8.32 us -> 10.3 us  [body(): lax.all_to_all(send, ('gx', 'yz'), split_axis=0, concat_axis=0, tiled=True)]
  transfers between devices with their start and end apart: 5 -> 5, of which waited for: 1 -> 2; matrix products, arithmetic and copies ran while one was open for 0% -> 0% of each run, Pallas kernels for 35% -> 33%
where the time goes in v3:
time: 76.6 us; the launch traced here: 76.4 us
  Pallas kernels  35.9 us (47%)
  waiting for transfers between devices  18.8 us (25%)
  starting transfers between devices  18.4 us (24%)
  local copies, waits for them, and re-layouts  3.11 us (4%)
    all_to_all x1, waiting for transfers between devices, body(): lax.all_to_all(send, ('gx', 'yz'), split_axis=0, concat_axis=0, tiled=True)  18.4 us
    pallas_call x1, Pallas kernels, body(): pl.pallas_call(keep_kernel, out_shape=pltpu.HBM((19, CAP, 4096), BF16), i...  15.8 us
    all_to_all x1, starting transfers between devices, body(): lax.all_to_all(send, ('gx', 'yz'), split_axis=0, concat_axis=0, tiled=True)  10.3 us
    pallas_call x1, Pallas kernels, body(): pl.pallas_call(refine_kernel, out_shape=struct((19, CAP, 4096), BF16), in...  5.42 us
    pallas_call x1, Pallas kernels, body(): pl.pallas_call(inner_kernel, out_shape=(struct((19, 4 * ROWS, 128), F32),...  4.92 us
    pallas_call x1, Pallas kernels, body(): pl.pallas_call(step_kernel, out_shape=(struct((2, 608, 256), BF16), pltpu...  4.61 us
    ppermute x1, starting transfers between devices, body(): from_right = lax.ppermute(left, 'gx', ring(slabs, -1))  3.71 us
    pallas_call x1, Pallas kernels, body(): pl.pallas_call(collide_kernel, out_shape=struct((19, 16, 32, 128), BF16),...  3.31 us
  transfers between devices with their start and end apart: 5, of which 2 were waited for; matrix products, arithmetic and copies ran while one was open for 0% of the time, Pallas kernels for 33%

profile of v3, /device:TPU:1, one launch (start us, length us, event | category | flops | bytes accessed | tf_op | source)
XLA Modules:
  0.0 76.4 jit_solution(10009080231130286114)
XLA Ops:
  0.0 1.5 %fusion = (bf16[19,16,2,128]{3,2,1,0:T(2,128)(2,1)S(1)}, bf16[19,16,2,128]{3,2,1,0:T(2,128)(2,1)S(1)}) fusion(bf16[19,16,32,128]{3,2,1,0:T(8,128)(2,1)} %pop_ref.1), kind=kLoop, calls=%fused_computation.2 | loop fusion | bytes 622592 | tf_op jit(solution)/shard_map/slice | solution.py:502
  1.6 3.0 %collective-permute-start = (bf16[19,2,16,128]{3,2,1,0:T(8,128)(2,1)S(1)}, bf16[19,2,16,128]{3,2,1,0:T(8,128)(2,1)S(1)}, u32[]{:S(2)}, u32[]{:S(2)}) collective-permute-start(bf16[19,2,16,128]{3,2,1,0:T(8,128)(2,1)S(1)} %bitcast.11), channel_id=1, source_target_pairs={{0,1},{1,2},{2,3},{3,4},{4,5},{5,6},{6,7},{7,0},{8,9},{9,10},{10,1... | collective-permute-start | bytes 466952 | tf_op jit(solution)/shard_map/ppermute | solution.py:503
  4.6 0.0 collective-permute-start.1
  4.6 0.9 %rates.1.rate_ref = f32[3,48,128]{2,1,0:T(8,128)S(1)} custom-call(s32[2048]{0:T(1024)} %levels_ref.1), custom_call_target="tpu_custom_call" | custom-call | bytes 3000000 | tf_op jit(solution)/shard_map/rates/pallas_call | solution.py:506
  5.6 3.3 %collide.1.c1_ref = bf16[19,16,32,128]{3,2,1,0:T(8,128)(2,1)S(1)} custom-call(bf16[19,16,32,128]{3,2,1,0:T(8,128)(2,1)} %pop_ref.1, f32[3,48,128]{2,1,0:T(8,128)S(1)} %rates.1.rate_ref), custom_call_target="tpu_custom_call" | custom-call | bytes 15000000 | tf_op jit(solution)/shard_map/collide/pallas_call | solution.py:516
  8.9 0.0 copy-start.3
  8.9 0.0 copy-start.4
  8.9 0.0 copy-start.5
  8.9 0.0 collective-permute-done.low_ref
  8.9 0.4 collective-permute-done.1.high_ref
  9.3 0.6 faces.1
  9.9 1.4 %collective-permute-start.2 = (bf16[21,40,128]{2,1,0:T(8,128)(2,1)S(1)}, bf16[21,40,128]{2,1,0:T(8,128)(2,1)S(1)}, u32[]{:S(2)}, u32[]{:S(2)}) collective-permute-start(bf16[21,40,128]{2,1,0:T(8,128)(2,1)S(1)} %get-tuple-element.18), channel_id=1, source_target_pairs={{0,8},{8,16},{16,24},{24,32},{32,40},{40,48},{48,56},{56,64},{64,7... | collective-permute-start | bytes 645128 | tf_op jit(solution)/shard_map/ppermute | solution.py:547
  11.3 3.7 %collective-permute-start.3 = (bf16[21,40,128]{2,1,0:T(8,128)(2,1)S(1)}, bf16[21,40,128]{2,1,0:T(8,128)(2,1)S(1)}, u32[]{:S(2)}, u32[]{:S(2)}) collective-permute-start(bf16[21,40,128]{2,1,0:T(8,128)(2,1)S(1)} %get-tuple-element.19), channel_id=1, source_target_pairs={{0,120},{8,0},{16,8},{24,16},{32,24},{40,32},{48,40},{56,48},{64,5... | collective-permute-start | bytes 645128 | tf_op jit(solution)/shard_map/ppermute | solution.py:548
  15.0 4.9 %inner.1 = (f32[19,192,128]{2,1,0:T(8,128)S(1)}, bf16[6,608,256]{2,1,0:T(8,128)(2,1)S(1)}) custom-call(bf16[19,16,32,128]{3,2,1,0:T(8,128)(2,1)S(1)} %collide.1.c1_ref, bf16[19,8,16,128]{3,2,1,0:T(8,128)(2,1)S(1)} %get-tuple-element.15.cy_ref, f32[3,48,128]{2,1,0:T(8,128)S(1)} %rates.1.rate_ref), custom_call_target="tpu_custom_call" | custom-call | bytes 18000000 | tf_op jit(solution)/shard_map/inner/pallas_call | solution.py:550
  19.9 0.0 copy-start
  19.9 0.0 collective-permute-done.2.gl_ref
  20.0 0.0 collective-permute-done.3.gr_ref
  20.0 0.0 copy-done.3
  20.0 0.0 copy-done.4
  20.0 0.0 copy-done.5
  20.0 4.6 %step.1 = (bf16[2,608,256]{2,1,0:T(8,128)(2,1)S(1)}, bf16[128,80,128]{2,1,0:T(8,128)(2,1)}) custom-call(s32[2048]{0:T(1024)S(1)} %copy-done.4, s32[2048]{0:T(1024)S(1)} %copy-done.5, f32[19,192,128]{2,1,0:T(8,128)S(1)} %get-tuple-element.16.rest_ref, bf16[19,4,40,128]{3,2,1,0:T(8,128)(2,1)S(1)} %get-tuple-element.17.rim_ref, ...), custom_call_target="tpu_custom_call" | custom-call | bytes 18000000 | tf_op jit(solution)/shard_map/step/pallas_call | solution.py:565
  24.6 0.0 copy-done
  24.6 10.3 %all-to-all-start = ((bf16[128,80,128]{2,1,0:T(8,128)(2,1)}), bf16[128,80,128]{2,1,0:T(8,128)(2,1)S(1)}, u32[]{:S(2)}, u32[]{:S(2)}) async-start(bf16[128,80,128]{2,1,0:T(8,128)(2,1)} %get-tuple-element.23), calls=%async_computation | async-start | bytes 5242880 | tf_op jit(solution)/shard_map/all_to_all | solution.py:588
  34.9 0.4 plan.1
  35.2 0.0 copy-start.1
  35.2 1.5 %copy-done.1 = bf16[6,608,256]{2,1,0:T(8,128)(2,1)S(1)} copy-done((bf16[6,608,256]{2,1,0:T(8,128)(2,1)S(1)}, bf16[6,608,256]{2,1,0:T(8,128)(2,1)}, u32[]{:S(2)}) %copy-start.1) | copy-done | bytes 1867800
  36.8 0.0 copy-start.2
  36.8 15.8 %keep.1.half_ref = bf16[19,24,4096]{2,1,0:T(8,128)(2,1)} custom-call(s32[2048]{0:T(1024)S(1)} %copy-done.4, s32[32,128]{1,0:T(8,128)S(1)} %get-tuple-element.22.owned_ref, bf16[6,608,256]{2,1,0:T(8,128)(2,1)S(1)} %copy-done.1, bf16[2,608,256]{2,1,0:T(8,128)(2,1)S(1)} %get-tuple-element.21.after_ref.outer_ref), custom_call_target="tpu_custom_call" | custom-call | bytes 30000000 | tf_op jit(solution)/shard_map/keep/pallas_call | solution.py:601
  52.5 18.4 %all-to-all-done.recv_ref = bf16[128,80,128]{2,1,0:T(8,128)(2,1)S(1)} async-done(((bf16[128,80,128]{2,1,0:T(8,128)(2,1)}), bf16[128,80,128]{2,1,0:T(8,128)(2,1)S(1)}, u32[]{:S(2)}, u32[]{:S(2)}) %all-to-all-start) | async-done | bytes 2621472 | tf_op jit(solution)/shard_map/all_to_all | solution.py:588
  71.0 0.0 copy-done.2
  71.0 5.4 %refine.1 = bf16[19,24,4096]{2,1,0:T(8,128)(2,1)} custom-call(s32[2048]{0:T(1024)S(1)} %copy-done.4, s32[32,128]{1,0:T(8,128)S(1)} %get-tuple-element.22.owned_ref, bf16[128,80,128]{2,1,0:T(8,128)(2,1)S(1)} %all-to-all-done.recv_ref, f32[32,128]{1,0:T(8,128)S(1)} %get-tuple-element.24.kind_ref, bf16[256,512]{1,0:T(8,128)(2,1)S(1)} %copy-done.2, ...), custom_call_target="tpu_custom_call" | custom-call | bytes 15000000 | tf_op jit(solution)/shard_map/refine/pallas_call | solution.py:616
  (2 shorter events, 0.0 us)
Async XLA Ops:
  1.6 7.3 %collective-permute-start = (bf16[19,2,16,128]{3,2,1,0:T(8,128)(2,1)S(1)}, bf16[19,2,16,128]{3,2,1,0:T(8,128)(2,1)S(1)}, u32[]{:S(2)}, u32[]{:S(2)}) collective-permute-start(bf16[19,2,16,128]{3,2,1,0:T(8,128)(2,1)S(1)} %bitcast.11), channel_id=1, source_target_pairs={{0,1},{1,2},{2,3},{3,4},{4,5},{5,6},{6,7},{7,0},{8,9},{9,10},{10,1... | collective-permute-start | bytes 466952 | tf_op jit(solution)/shard_map/ppermute | solution.py:503
  4.6 4.7 %collective-permute-start.1 = (bf16[19,2,16,128]{3,2,1,0:T(8,128)(2,1)S(1)}, bf16[19,2,16,128]{3,2,1,0:T(8,128)(2,1)S(1)}, u32[]{:S(2)}, u32[]{:S(2)}) collective-permute-start(bf16[19,2,16,128]{3,2,1,0:T(8,128)(2,1)S(1)} %bitcast.12), channel_id=1, source_target_pairs={{0,7},{1,0},{2,1},{3,2},{4,3},{5,4},{6,5},{7,6},{8,15},{9,8},{10,9... | collective-permute-start | bytes 466952 | tf_op jit(solution)/shard_map/ppermute | solution.py:504
  8.9 11.1 %copy-start.3 = (bf16[2,256,128]{2,1,0:T(8,128)(2,1)S(1)}, bf16[2,256,128]{2,1,0:T(8,128)(2,1)}, u32[]{:S(2)}) copy-start(bf16[2,256,128]{2,1,0:T(8,128)(2,1)} %constant.4.clone.reduce_ref) | copy-start | bytes 393220
  8.9 11.1 %copy-start.4 = (s32[2048]{0:T(1024)S(1)}, s32[2048]{0:T(1024)}, u32[]{:S(2)}) copy-start(s32[2048]{0:T(1024)} %flags_ref.5) | copy-start | bytes 24580
  8.9 11.1 %copy-start.5 = (s32[2048]{0:T(1024)S(1)}, s32[2048]{0:T(1024)}, u32[]{:S(2)}) copy-start(s32[2048]{0:T(1024)} %owner_ref.1) | copy-start | bytes 24580
  9.9 10.0 %collective-permute-start.2 = (bf16[21,40,128]{2,1,0:T(8,128)(2,1)S(1)}, bf16[21,40,128]{2,1,0:T(8,128)(2,1)S(1)}, u32[]{:S(2)}, u32[]{:S(2)}) collective-permute-start(bf16[21,40,128]{2,1,0:T(8,128)(2,1)S(1)} %get-tuple-element.18), channel_id=1, source_target_pairs={{0,8},{8,16},{16,24},{24,32},{32,40},{40,48},{48,56},{56,64},{64,7... | collective-permute-start | bytes 645128 | tf_op jit(solution)/shard_map/ppermute | solution.py:547
  11.3 8.7 %collective-permute-start.3 = (bf16[21,40,128]{2,1,0:T(8,128)(2,1)S(1)}, bf16[21,40,128]{2,1,0:T(8,128)(2,1)S(1)}, u32[]{:S(2)}, u32[]{:S(2)}) collective-permute-start(bf16[21,40,128]{2,1,0:T(8,128)(2,1)S(1)} %get-tuple-element.19), channel_id=1, source_target_pairs={{0,120},{8,0},{16,8},{24,16},{32,24},{40,32},{48,40},{56,48},{64,5... | collective-permute-start | bytes 645128 | tf_op jit(solution)/shard_map/ppermute | solution.py:548
  19.9 4.7 %copy-start = (bf16[6,608,256]{2,1,0:T(8,128)(2,1)}, bf16[6,608,256]{2,1,0:T(8,128)(2,1)S(1)}, u32[]{:S(2)}) copy-start(bf16[6,608,256]{2,1,0:T(8,128)(2,1)S(1)} %get-tuple-element.20.inner_ref) | copy-start | bytes 5603332
  24.6 46.3 %all-to-all-start = ((bf16[128,80,128]{2,1,0:T(8,128)(2,1)}), bf16[128,80,128]{2,1,0:T(8,128)(2,1)S(1)}, u32[]{:S(2)}, u32[]{:S(2)}) async-start(bf16[128,80,128]{2,1,0:T(8,128)(2,1)} %get-tuple-element.23), calls=%async_computation | async-start | bytes 5242880 | tf_op jit(solution)/shard_map/all_to_all | solution.py:588
  35.2 1.5 %copy-start.1 = (bf16[6,608,256]{2,1,0:T(8,128)(2,1)S(1)}, bf16[6,608,256]{2,1,0:T(8,128)(2,1)}, u32[]{:S(2)}) copy-start(bf16[6,608,256]{2,1,0:T(8,128)(2,1)} %copy-done) | copy-start | bytes 5603332
  36.8 34.2 %copy-start.2 = (bf16[256,512]{1,0:T(8,128)(2,1)S(1)}, bf16[256,512]{1,0:T(8,128)(2,1)}, u32[]{:S(2)}) copy-start(bf16[256,512]{1,0:T(8,128)(2,1)} %constant.5.clone.expand_ref) | copy-start | bytes 786436

commit v4 on v3

--- a/solution.py
+++ b/solution.py
@@ -194,7 +194,9 @@
             target[part, 32 * i + 8 * yh : 32 * i + 8 * yh + 8, lanes] = h[i].astype(BF16)
 
 
-def inner_kernel(c1_ref, cy_ref, rate_ref, rest_ref, state_ref, first, second, sem):
+def inner_kernel(
+    c1_ref, cy_ref, rate_ref, reduce_ref, rest_ref, state_ref, middle_ref, first, second, mean, mix, sem
+):
     lane = lax.broadcasted_iota(jnp.int32, (8, 128), 1)
 
     @pl.loop(0, 16)
@@ -232,6 +234,9 @@
         lanes = pl.ds(pl.multiple_of((p % 2) * 128, 128), 128)
         settle(second, pl.multiple_of(p * ROWS, 8), state_ref, p // 2, lanes, lane)
 
+    means(
+        [(q, state_ref.at[2 * q - 1], state_ref.at[2 * q]) for q in (1, 2)], reduce_ref, mean, mix, middle_ref, lane
+    )
     for copy in copies:
         copy.wait()
 
@@ -251,8 +256,27 @@
     return a
 
 
+def means(quarters, reduce_ref, mean, mix, pack, lane):
+    for n, (q, left, right) in enumerate(quarters):
+        mean[n, :, :] = jnp.dot(left[...], reduce_ref[0, :, :], preferred_element_type=F32) + jnp.dot(
+            right[...], reduce_ref[1, :, :], preferred_element_type=F32
+        )
+        for i in range(19):
+            for by in range(2):
+                at = 32 * i + 16 * by
+                mix[n, by, 8 * i : 8 * i + 8, :] = (
+                    mean[n, pl.ds(at, 8, stride=2), :] + mean[n, pl.ds(at + 1, 8, stride=2), :]
+                )
+        for by in range(2):
+            for g in range(3):
+                a = [mix[n, by, pl.ds(64 * g + y, 8, stride=8), :] for y in range(8)]
+                a = butterfly(a, lane, 8)
+                for z in range(8):
+                    pack[8 * by + z, pl.ds(32 * g + q, 8, stride=4), :] = a[z]
+
+
 def step_kernel(
-    flags_ref, owner_ref, rest_ref, rim_ref, gl_ref, gr_ref, rate_ref, reduce_ref, inner_ref,
+    flags_ref, owner_ref, rest_ref, rim_ref, gl_ref, gr_ref, rate_ref, reduce_ref, inner_ref, middle_ref,
     outer_ref, send_ref,
     first, second, mean, mix, pack, stage, in_sem, send_sem,
 ):
@@ -292,32 +316,21 @@
         lanes = pl.ds(pl.multiple_of((e % 2) * 128, 128), 128)
         settle(second, pl.multiple_of((e + 2 * above) * ROWS, 8), outer_ref, above, lanes, lane)
 
-    for q in range(4):
-        total = None
-        for par in range(2):
-            c = 2 * q + par
-            pair = outer_ref[c // 7, :, :] if c in (0, 7) else inner_ref[c - 1, :, :]
-            term = jnp.dot(pair, reduce_ref[par, :, :], preferred_element_type=F32)
-            total = term if total is None else total + term
-        mean[q, :, :] = total
-        for i in range(19):
-            for by in range(2):
-                at = 32 * i + 16 * by
-                mix[q, by, 8 * i : 8 * i + 8, :] = (
-                    mean[q, pl.ds(at, 8, stride=2), :] + mean[q, pl.ds(at + 1, 8, stride=2), :]
-                )
-        for by in range(2):
-            for g in range(3):
-                a = [mix[q, by, pl.ds(64 * g + y, 8, stride=8), :] for y in range(8)]
-                a = butterfly(a, lane, 8)
-                for z in range(8):
-                    pack[8 * by + z, 20 * q + 8 * g : 20 * q + 8 * g + 8, :] = a[z]
+    means(
+        [(0, outer_ref.at[0], inner_ref.at[0]), (3, inner_ref.at[5], outer_ref.at[1])],
+        reduce_ref, mean, mix, pack, lane,
+    )
+
+    quarter = lax.broadcasted_iota(jnp.int32, (4, 128), 0)
+    middle = (quarter == 1) | (quarter == 2)
 
     @pl.loop(0, BLK)
     def _(k):
         @pl.when(flags_ref[me * BLK + k] != 0)
         def _():
-            stage[k, :, :] = pack[k, 0:80, :].astype(BF16)
+            for i in range(19):
+                rows = slice(4 * i, 4 * i + 4)
+                stage[k, i, :, :] = jnp.where(middle, middle_ref[k, rows, :], pack[k, rows, :]).astype(BF16)
             pltpu.make_async_copy(stage.at[k], send_ref.at[owner_ref[me * BLK + k]], send_sem.at[k]).start()
 
     @pl.loop(0, BLK)
@@ -396,8 +409,8 @@
 
     def widen(s, device):
         pltpu.make_async_copy(recv_ref.at[device], taken.at[s], in_sem.at[s]).wait()
-        for r in range(10):
-            rows[pl.ds(192 * r + s, 8, stride=24), :] = taken[s, 8 * r : 8 * r + 8, :].astype(F32)
+        for i in range(19):
+            rows[pl.ds(96 * i + s, 4, stride=24), :] = taken[s, i, :, :].astype(F32)
 
     each_arrival(fetch)
 
@@ -412,7 +425,7 @@
         for i in range(19):
             ones, twos = [], []
             for g in range(3):
-                start = 24 * (20 * q + i) + 8 * g
+                start = 24 * (4 * i + q) + 8 * g
                 v = rows[start : start + 8, :]
                 ones.append(jnp.where(kinds[g] == 1.0, v, 0.0))
                 twos.append(jnp.where(kinds[g] == 2.0, v, 0.0))
@@ -547,33 +560,40 @@
     from_left = lax.ppermute(right, "gx", ring(slabs, 1))
     from_right = lax.ppermute(left, "gx", ring(slabs, -1))
 
-    rest, inner = pl.pallas_call(
+    reduce = jnp.asarray(mean_matrix(), BF16)
+    rest, inner, middle = pl.pallas_call(
         inner_kernel,
-        out_shape=(struct((19, 4 * ROWS, 128), F32), struct((6, 608, 256), BF16)),
-        in_specs=[VM, VM, VM],
-        out_specs=(ANY, VM),
+        out_shape=(
+            struct((19, 4 * ROWS, 128), F32),
+            struct((6, 608, 256), BF16),
+            struct((BLK, 96, 128), F32),
+        ),
+        in_specs=[VM] * 4,
+        out_specs=(ANY, VM, VM),
         scratch_shapes=[
             pltpu.VMEM((19, 16 * ROWS, 128), F32),
             pltpu.VMEM((19, 14 * ROWS, 128), F32),
+            pltpu.VMEM((2, 608, 128), F32),
+            pltpu.VMEM((2, 2, 192, 128), F32),
             pltpu.SemaphoreType.DMA((2,)),
         ],
-        compiler_params=limit(20),
+        compiler_params=limit(22),
         cost_estimate=cost(6),
         name="inner",
-    )(c1, cy, rate)
+    )(c1, cy, rate, reduce)
 
     outer, send = pl.pallas_call(
         step_kernel,
-        out_shape=(struct((2, 608, 256), BF16), pltpu.HBM((devices, 80, 128), BF16)),
-        in_specs=[SM, SM, ANY] + [VM] * 6,
+        out_shape=(struct((2, 608, 256), BF16), pltpu.HBM((devices, 19, 4, 128), BF16)),
+        in_specs=[SM, SM, ANY] + [VM] * 7,
         out_specs=(VM, HBM),
         scratch_shapes=[
             pltpu.VMEM((19, 8 * ROWS, 128), F32),
             pltpu.VMEM((19, 8 * ROWS, 128), F32),
-            pltpu.VMEM((4, 608, 128), F32),
-            pltpu.VMEM((4, 2, 192, 128), F32),
-            pltpu.VMEM((BLK, 88, 128), F32),
-            pltpu.VMEM((BLK, 80, 128), BF16),
+            pltpu.VMEM((2, 608, 128), F32),
+            pltpu.VMEM((2, 2, 192, 128), F32),
+            pltpu.VMEM((BLK, 96, 128), F32),
+            pltpu.VMEM((BLK, 19, 4, 128), BF16),
             pltpu.SemaphoreType.DMA,
             pltpu.SemaphoreType.DMA((BLK,)),
         ],
@@ -581,8 +601,7 @@
         cost_estimate=cost(6),
         name="step",
     )(
-        refine_flags, new_owner, rest, rim, from_left, from_right, rate,
-        jnp.asarray(mean_matrix(), BF16), inner,
+        refine_flags, new_owner, rest, rim, from_left, from_right, rate, reduce, inner, middle,
     )
 
     recv = lax.all_to_all(send, ("gx", "yz"), split_axis=0, concat_axis=0, tiled=True)
@@ -619,8 +638,8 @@
         in_specs=[SM, SM, ANY, VM, VM, HBM],
         out_specs=ANY,
         scratch_shapes=[
-            pltpu.VMEM((CAP, 80, 128), BF16),
-            pltpu.VMEM((CAP * 80, 128), F32),
+            pltpu.VMEM((CAP, 19, 4, 128), BF16),
+            pltpu.VMEM((CAP * 76, 128), F32),
             pltpu.VMEM((4, 456, 256), BF16),
             pltpu.VMEM((4, 456, 512), F32),
             pltpu.VMEM((19, CAP, 4096), BF16),
@@ -632,7 +651,7 @@
         compiler_params=limit(18),
         cost_estimate=cost(5),
         name="refine",
-    )(refine_flags, owned, recv, kind, jnp.asarray(expand_matrix(), BF16), in_hbm(half))
+    )(refine_flags, owned, in_hbm(recv), kind, jnp.asarray(expand_matrix(), BF16), in_hbm(half))
     return jnp.transpose(migrated, (1, 0, 2))
 
 

time: 76.6 us -> 74.8 us (0.977)
  local copies, waits for them, and re-layouts: 3.11 us -> 1.59 us
    unnamed x14 -> x10, local copies, waits for them, and re-layouts: 1.59 us -> 0.07 us
    pallas_call x1, Pallas kernels: 4.92 us -> 5.79 us  [body(): pl.pallas_call(inner_kernel, out_shape=(struct((19, 4 * ROWS, 128), F32),...]
  transfers between devices with their start and end apart: 5 -> 5, of which waited for: 2 -> 2; matrix products, arithmetic and copies ran while one was open for 0% -> 0% of each run, Pallas kernels for 33% -> 35%
where the time goes in v4:
time: 74.8 us; the launch traced here: 74.5 us
  Pallas kernels  36.3 us (49%)
  waiting for transfers between devices  18.6 us (25%)
  starting transfers between devices  17.9 us (24%)
  local copies, waits for them, and re-layouts  1.59 us (2%)
    all_to_all x1, waiting for transfers between devices, body(): lax.all_to_all(send, ('gx', 'yz'), split_axis=0, concat_axis=0, tiled=True)  18.2 us
    pallas_call x1, Pallas kernels, body(): pl.pallas_call(keep_kernel, out_shape=pltpu.HBM((19, CAP, 4096), BF16), i...  15.8 us
    all_to_all x1, starting transfers between devices, body(): lax.all_to_all(send, ('gx', 'yz'), split_axis=0, concat_axis=0, tiled=True)  9.78 us
    pallas_call x1, Pallas kernels, body(): pl.pallas_call(inner_kernel, out_shape=(struct((19, 4 * ROWS, 128), F32),...  5.79 us
    pallas_call x1, Pallas kernels, body(): pl.pallas_call(refine_kernel, out_shape=struct((19, CAP, 4096), BF16), in...  5.23 us
    pallas_call x1, Pallas kernels, body(): pl.pallas_call(step_kernel, out_shape=(struct((2, 608, 256), BF16), pltpu...  4.29 us
    ppermute x1, starting transfers between devices, body(): from_right = lax.ppermute(left, 'gx', ring(slabs, -1))  3.71 us
    pallas_call x1, Pallas kernels, body(): pl.pallas_call(collide_kernel, out_shape=struct((19, 16, 32, 128), BF16),...  3.31 us
  transfers between devices with their start and end apart: 5, of which 2 were waited for; matrix products, arithmetic and copies ran while one was open for 0% of the time, Pallas kernels for 35%

profile of v4, /device:TPU:1, one launch (start us, length us, event | category | flops | bytes accessed | tf_op | source)
XLA Modules:
  0.0 74.5 jit_solution(6916761641068071007)
XLA Ops:
  0.0 1.5 %fusion = (bf16[19,16,2,128]{3,2,1,0:T(2,128)(2,1)S(1)}, bf16[19,16,2,128]{3,2,1,0:T(2,128)(2,1)S(1)}) fusion(bf16[19,16,32,128]{3,2,1,0:T(8,128)(2,1)} %pop_ref.1), kind=kLoop, calls=%fused_computation.2 | loop fusion | bytes 622592 | tf_op jit(solution)/shard_map/slice | solution.py:515
  1.6 3.0 %collective-permute-start = (bf16[19,2,16,128]{3,2,1,0:T(8,128)(2,1)S(1)}, bf16[19,2,16,128]{3,2,1,0:T(8,128)(2,1)S(1)}, u32[]{:S(2)}, u32[]{:S(2)}) collective-permute-start(bf16[19,2,16,128]{3,2,1,0:T(8,128)(2,1)S(1)} %bitcast.11), channel_id=1, source_target_pairs={{0,1},{1,2},{2,3},{3,4},{4,5},{5,6},{6,7},{7,0},{8,9},{9,10},{10,1... | collective-permute-start | bytes 466952 | tf_op jit(solution)/shard_map/ppermute | solution.py:516
  4.6 0.0 collective-permute-start.1
  4.6 0.9 %rates.1.rate_ref = f32[3,48,128]{2,1,0:T(8,128)S(1)} custom-call(s32[2048]{0:T(1024)} %levels_ref.1), custom_call_target="tpu_custom_call" | custom-call | bytes 3000000 | tf_op jit(solution)/shard_map/rates/pallas_call | solution.py:519
  5.6 3.3 %collide.1.c1_ref = bf16[19,16,32,128]{3,2,1,0:T(8,128)(2,1)S(1)} custom-call(bf16[19,16,32,128]{3,2,1,0:T(8,128)(2,1)} %pop_ref.1, f32[3,48,128]{2,1,0:T(8,128)S(1)} %rates.1.rate_ref), custom_call_target="tpu_custom_call" | custom-call | bytes 15000000 | tf_op jit(solution)/shard_map/collide/pallas_call | solution.py:529
  8.9 0.0 copy-start
  8.9 0.0 copy-start.2
  8.9 0.0 copy-start.3
  8.9 0.0 collective-permute-done.low_ref
  8.9 0.4 collective-permute-done.1.high_ref
  9.3 0.6 faces.1
  9.9 1.4 %collective-permute-start.2 = (bf16[21,40,128]{2,1,0:T(8,128)(2,1)S(1)}, bf16[21,40,128]{2,1,0:T(8,128)(2,1)S(1)}, u32[]{:S(2)}, u32[]{:S(2)}) collective-permute-start(bf16[21,40,128]{2,1,0:T(8,128)(2,1)S(1)} %get-tuple-element.19), channel_id=1, source_target_pairs={{0,8},{8,16},{16,24},{24,32},{32,40},{40,48},{48,56},{56,64},{64,7... | collective-permute-start | bytes 645128 | tf_op jit(solution)/shard_map/ppermute | solution.py:560
  11.3 3.7 %collective-permute-start.3 = (bf16[21,40,128]{2,1,0:T(8,128)(2,1)S(1)}, bf16[21,40,128]{2,1,0:T(8,128)(2,1)S(1)}, u32[]{:S(2)}, u32[]{:S(2)}) collective-permute-start(bf16[21,40,128]{2,1,0:T(8,128)(2,1)S(1)} %get-tuple-element.20), channel_id=1, source_target_pairs={{0,120},{8,0},{16,8},{24,16},{32,24},{40,32},{48,40},{56,48},{64,5... | collective-permute-start | bytes 645128 | tf_op jit(solution)/shard_map/ppermute | solution.py:561
  15.0 0.0 copy-done
  15.0 5.8 %inner.1 = (f32[19,192,128]{2,1,0:T(8,128)S(1)}, bf16[6,608,256]{2,1,0:T(8,128)(2,1)S(1)}, f32[16,96,128]{2,1,0:T(8,128)S(1)}) custom-call(bf16[19,16,32,128]{3,2,1,0:T(8,128)(2,1)S(1)} %collide.1.c1_ref, bf16[19,8,16,128]{3,2,1,0:T(8,128)(2,1)S(1)} %get-tuple-element.16.cy_ref, f32[3,48,128]{2,1,0:T(8,128)S(1)} %rates.1.rate_ref, ...), custom_call_target="tpu_custom_call" | custom-call | bytes 18000000 | tf_op jit(solution)/shard_map/inner/pallas_call | solution.py:564
  20.8 0.0 collective-permute-done.2.gl_ref
  20.8 0.0 collective-permute-done.3.gr_ref
  20.8 0.0 copy-done.2
  20.8 0.0 copy-done.3
  20.8 4.3 %step.1 = (bf16[2,608,256]{2,1,0:T(8,128)(2,1)S(1)}, bf16[128,19,4,128]{3,2,1,0:T(4,128)(2,1)}) custom-call(s32[2048]{0:T(1024)S(1)} %copy-done.2, s32[2048]{0:T(1024)S(1)} %copy-done.3, f32[19,192,128]{2,1,0:T(8,128)S(1)} %get-tuple-element.17.rest_ref, bf16[19,4,40,128]{3,2,1,0:T(8,128)(2,1)S(1)} %get-tuple-element.18.rim_ref, ...), custom_call_target="tpu_custom_call" | custom-call | bytes 18000000 | tf_op jit(solution)/shard_map/step/pallas_call | solution.py:585
  25.1 9.8 %all-to-all-start = ((bf16[128,19,4,128]{3,2,1,0:T(4,128)(2,1)}), bf16[128,19,4,128]{3,2,1,0:T(4,128)(2,1)}, u32[]{:S(2)}, u32[]{:S(2)}) async-start(bf16[128,19,4,128]{3,2,1,0:T(4,128)(2,1)} %get-tuple-element.25), calls=%async_computation | async-start | bytes 4980736 | tf_op jit(solution)/shard_map/all_to_all | solution.py:607
  34.9 0.4 plan.1
  35.3 0.0 copy-start.1
  35.3 15.8 %keep.1.half_ref = bf16[19,24,4096]{2,1,0:T(8,128)(2,1)} custom-call(s32[2048]{0:T(1024)S(1)} %copy-done.2, s32[32,128]{1,0:T(8,128)S(1)} %get-tuple-element.24.owned_ref, bf16[6,608,256]{2,1,0:T(8,128)(2,1)S(1)} %get-tuple-element.21.inner_ref, bf16[2,608,256]{2,1,0:T(8,128)(2,1)S(1)} %get-tuple-element.23.after_ref.outer_ref), custom_call_target="tpu_custom_call" | custom-call | bytes 30000000 | tf_op jit(solution)/shard_map/keep/pallas_call | solution.py:620
  51.1 18.2 %all-to-all-done.recv_ref = bf16[128,19,4,128]{3,2,1,0:T(4,128)(2,1)} async-done(((bf16[128,19,4,128]{3,2,1,0:T(4,128)(2,1)}), bf16[128,19,4,128]{3,2,1,0:T(4,128)(2,1)}, u32[]{:S(2)}, u32[]{:S(2)}) %all-to-all-start) | async-done | bytes 2490400 | tf_op jit(solution)/shard_map/all_to_all | solution.py:607
  69.3 0.0 copy-done.1
  69.3 5.2 %refine.1 = bf16[19,24,4096]{2,1,0:T(8,128)(2,1)} custom-call(s32[2048]{0:T(1024)S(1)} %copy-done.2, s32[32,128]{1,0:T(8,128)S(1)} %get-tuple-element.24.owned_ref, bf16[128,19,4,128]{3,2,1,0:T(4,128)(2,1)} %all-to-all-done.recv_ref, f32[32,128]{1,0:T(8,128)S(1)} %get-tuple-element.26.kind_ref, bf16[256,512]{1,0:T(8,128)(2,1)S(1)} %copy-done.1, ...), custom_call_target="tpu_custom_call" | custom-call | bytes 15000000 | tf_op jit(solution)/shard_map/refine/pallas_call | solution.py:635
  (2 shorter events, 0.0 us)
Async XLA Ops:
  1.6 7.3 %collective-permute-start = (bf16[19,2,16,128]{3,2,1,0:T(8,128)(2,1)S(1)}, bf16[19,2,16,128]{3,2,1,0:T(8,128)(2,1)S(1)}, u32[]{:S(2)}, u32[]{:S(2)}) collective-permute-start(bf16[19,2,16,128]{3,2,1,0:T(8,128)(2,1)S(1)} %bitcast.11), channel_id=1, source_target_pairs={{0,1},{1,2},{2,3},{3,4},{4,5},{5,6},{6,7},{7,0},{8,9},{9,10},{10,1... | collective-permute-start | bytes 466952 | tf_op jit(solution)/shard_map/ppermute | solution.py:516
  4.6 4.7 %collective-permute-start.1 = (bf16[19,2,16,128]{3,2,1,0:T(8,128)(2,1)S(1)}, bf16[19,2,16,128]{3,2,1,0:T(8,128)(2,1)S(1)}, u32[]{:S(2)}, u32[]{:S(2)}) collective-permute-start(bf16[19,2,16,128]{3,2,1,0:T(8,128)(2,1)S(1)} %bitcast.12), channel_id=1, source_target_pairs={{0,7},{1,0},{2,1},{3,2},{4,3},{5,4},{6,5},{7,6},{8,15},{9,8},{10,9... | collective-permute-start | bytes 466952 | tf_op jit(solution)/shard_map/ppermute | solution.py:517
  8.9 6.1 %copy-start = (bf16[2,256,128]{2,1,0:T(8,128)(2,1)S(1)}, bf16[2,256,128]{2,1,0:T(8,128)(2,1)}, u32[]{:S(2)}) copy-start(bf16[2,256,128]{2,1,0:T(8,128)(2,1)} %constant.4.clone.reduce_ref) | copy-start | bytes 393220
  8.9 11.9 %copy-start.2 = (s32[2048]{0:T(1024)S(1)}, s32[2048]{0:T(1024)}, u32[]{:S(2)}) copy-start(s32[2048]{0:T(1024)} %flags_ref.5) | copy-start | bytes 24580
  8.9 11.9 %copy-start.3 = (s32[2048]{0:T(1024)S(1)}, s32[2048]{0:T(1024)}, u32[]{:S(2)}) copy-start(s32[2048]{0:T(1024)} %owner_ref.1) | copy-start | bytes 24580
  9.9 10.9 %collective-permute-start.2 = (bf16[21,40,128]{2,1,0:T(8,128)(2,1)S(1)}, bf16[21,40,128]{2,1,0:T(8,128)(2,1)S(1)}, u32[]{:S(2)}, u32[]{:S(2)}) collective-permute-start(bf16[21,40,128]{2,1,0:T(8,128)(2,1)S(1)} %get-tuple-element.19), channel_id=1, source_target_pairs={{0,8},{8,16},{16,24},{24,32},{32,40},{40,48},{48,56},{56,64},{64,7... | collective-permute-start | bytes 645128 | tf_op jit(solution)/shard_map/ppermute | solution.py:560
  11.3 9.5 %collective-permute-start.3 = (bf16[21,40,128]{2,1,0:T(8,128)(2,1)S(1)}, bf16[21,40,128]{2,1,0:T(8,128)(2,1)S(1)}, u32[]{:S(2)}, u32[]{:S(2)}) collective-permute-start(bf16[21,40,128]{2,1,0:T(8,128)(2,1)S(1)} %get-tuple-element.20), channel_id=1, source_target_pairs={{0,120},{8,0},{16,8},{24,16},{32,24},{40,32},{48,40},{56,48},{64,5... | collective-permute-start | bytes 645128 | tf_op jit(solution)/shard_map/ppermute | solution.py:561
  25.1 44.2 %all-to-all-start = ((bf16[128,19,4,128]{3,2,1,0:T(4,128)(2,1)}), bf16[128,19,4,128]{3,2,1,0:T(4,128)(2,1)}, u32[]{:S(2)}, u32[]{:S(2)}) async-start(bf16[128,19,4,128]{3,2,1,0:T(4,128)(2,1)} %get-tuple-element.25), calls=%async_computation | async-start | bytes 4980736 | tf_op jit(solution)/shard_map/all_to_all | solution.py:607
  35.3 34.0 %copy-start.1 = (bf16[256,512]{1,0:T(8,128)(2,1)S(1)}, bf16[256,512]{1,0:T(8,128)(2,1)}, u32[]{:S(2)}) copy-start(bf16[256,512]{1,0:T(8,128)(2,1)} %constant.5.clone.expand_ref) | copy-start | bytes 786436

commit v5 on v4

--- a/solution.py
+++ b/solution.py
@@ -25,8 +25,8 @@
 PLUS = [i for i in range(19) if VEL[i][0] == 1]
 MINUS = [i for i in range(19) if VEL[i][0] == -1]
 FLAT = [i for i in range(19) if VEL[i][0] == 0]
-RIGHTWARD = [(i, 2) for i in PLUS] + [(i, 1) for i in PLUS + FLAT + [12, 14]]
-LEFTWARD = [(i, 2) for i in MINUS] + [(i, 1) for i in MINUS + FLAT + [11, 13]]
+RIGHTWARD = [(i, 2) for i in PLUS] + [(i, 1) for i in PLUS + FLAT]
+LEFTWARD = [(i, 2) for i in MINUS] + [(i, 1) for i in MINUS + FLAT]
 FACES = len(RIGHTWARD)
 FROWS = 40
 HALO_Y = ((0, 32), (1, 33), (6, -2), (7, -1))
@@ -128,6 +128,15 @@
                     c1_ref[i, x, rows, :] = out[i].astype(BF16)
 
 
+def turn(rows, turned, dz):
+    lane = lax.broadcasted_iota(jnp.int32, rows.shape, 1)
+    if dz == 1:
+        rows = jnp.where(lane == 127, pltpu.roll(turned, 127, axis=1), rows)
+    else:
+        rows = jnp.where(lane == 0, pltpu.roll(turned, 1, axis=1), rows)
+    return rows.astype(BF16)
+
+
 def face_kernel(c1_ref, low_ref, high_ref, rate_ref, cy_ref, rim_ref, right_ref, left_ref, planes, edge, sem):
     copies = [
         pltpu.make_async_copy(c1_ref.at[:, a : a + 2], planes.at[:, b : b + 2], sem.at[n])
@@ -158,11 +167,19 @@
             ends = edge[pl.ds(i * 128 + plane, 8, stride=16), :].astype(BF16)
             rim_ref[i, n, 0:32, :] = body_rows
             rim_ref[i, n, 32:40, :] = ends
-            for ref, faces, depth in ((right_ref, RIGHTWARD, 16 - plane), (left_ref, LEFTWARD, plane + 1)):
-                if (i, depth) in faces:
-                    at = faces.index((i, depth))
+            for ref, faces, depth, outermost in ((right_ref, RIGHTWARD, 16 - plane, 3), (left_ref, LEFTWARD, plane + 1, 0)):
+                if (i, depth) not in faces:
+                    continue
+                at = faces.index((i, depth))
+                dz = VEL[i][2]
+                if depth == 1 or dz == 0:
                     ref[at, 0:32, :] = body_rows
                     ref[at, 32:40, :] = ends
+                else:
+                    last = (0, 1, 14, 15)[outermost]
+                    turned = edge[pl.ds(OPP[i] * 128 + last, 8, stride=16), :]
+                    ref[at, 0:32, :] = turn(body_rows.astype(F32), planes[OPP[i], outermost, :, :].astype(F32), dz)
+                    ref[at, 32:40, :] = turn(ends.astype(F32), turned, dz)
 
 
 def shifted(ref, at, lane):
@@ -295,7 +312,10 @@
             place(i, at, rim_ref[i, n, :, :].astype(F32))
     for ref, faces, places in ((gl_ref, RIGHTWARD, (None, 1, 0)), (gr_ref, LEFTWARD, (None, 6, 7))):
         for n, (i, depth) in enumerate(faces):
-            place(i, places[depth], ref[n, :, :].astype(F32))
+            rows = ref[n, :, :].astype(F32)
+            place(i, places[depth], rows)
+            if depth == 2 and VEL[i][2] != 0:
+                place(OPP[i], places[1], pltpu.roll(rows, 1 if VEL[i][2] == 1 else 127, axis=1))
 
     @pl.loop(0, 4)
     def _(e):
@@ -393,32 +413,20 @@
 
 def refine_kernel(
     flags_ref, owned_ref, recv_ref, kind_ref, expand_ref, half_ref, out_ref,
-    taken, rows, wide, product, half, result, in_sem, half_sem, out_sem,
+    rows, wide, product, half, result, half_sem, out_sem,
 ):
-    def each_arrival(act):
-        @pl.loop(0, CAP)
-        def _(s):
-            b = owned_ref[s, 0]
-
-            @pl.when((b >= 0) & (flags_ref[jnp.maximum(b, 0)] != 0))
-            def _():
-                act(s, b // BLK)
-
-    def fetch(s, device):
-        pltpu.make_async_copy(recv_ref.at[device], taken.at[s], in_sem.at[s]).start()
-
-    def widen(s, device):
-        pltpu.make_async_copy(recv_ref.at[device], taken.at[s], in_sem.at[s]).wait()
-        for i in range(19):
-            rows[pl.ds(96 * i + s, 4, stride=24), :] = taken[s, i, :, :].astype(F32)
-
-    each_arrival(fetch)
-
     @pl.loop(0, 19)
     def _(i):
         pltpu.make_async_copy(half_ref.at[i], half.at[i], half_sem.at[i]).start()
 
-    each_arrival(widen)
+    @pl.loop(0, CAP)
+    def _(s):
+        b = owned_ref[s, 0]
+
+        @pl.when((b >= 0) & (flags_ref[jnp.maximum(b, 0)] != 0))
+        def _():
+            for i in range(19):
+                rows[pl.ds(96 * i + s, 4, stride=24), :] = recv_ref[b // BLK, i, :, :].astype(F32)
 
     kinds = [kind_ref[8 * g : 8 * g + 8, :] for g in range(3)]
     for q in range(4):
@@ -635,23 +643,21 @@
     migrated = pl.pallas_call(
         refine_kernel,
         out_shape=struct((19, CAP, 4096), BF16),
-        in_specs=[SM, SM, ANY, VM, VM, HBM],
+        in_specs=[SM, SM, VM, VM, VM, HBM],
         out_specs=ANY,
         scratch_shapes=[
-            pltpu.VMEM((CAP, 19, 4, 128), BF16),
             pltpu.VMEM((CAP * 76, 128), F32),
             pltpu.VMEM((4, 456, 256), BF16),
             pltpu.VMEM((4, 456, 512), F32),
             pltpu.VMEM((19, CAP, 4096), BF16),
             pltpu.VMEM((19, CAP, 4096), BF16),
-            pltpu.SemaphoreType.DMA((CAP,)),
             pltpu.SemaphoreType.DMA((19,)),
             pltpu.SemaphoreType.DMA((19,)),
         ],
         compiler_params=limit(18),
         cost_estimate=cost(5),
         name="refine",
-    )(refine_flags, owned, in_hbm(recv), kind, jnp.asarray(expand_matrix(), BF16), in_hbm(half))
+    )(refine_flags, owned, recv, kind, jnp.asarray(expand_matrix(), BF16), in_hbm(half))
     return jnp.transpose(migrated, (1, 0, 2))
 
 

time: 74.8 us -> 73.7 us (0.985)
  local copies, waits for them, and re-layouts: 1.59 us -> 3.11 us
  waiting for transfers between devices: 18.6 us -> 17.4 us
  starting transfers between devices: 17.9 us -> 17 us
    unnamed x10 -> x14, local copies, waits for them, and re-layouts: 0.07 us -> 1.59 us
    all_to_all x1, waiting for transfers between devices: 18.2 us -> 17 us  [body(): lax.all_to_all(send, ('gx', 'yz'), split_axis=0, concat_axis=0, tiled=True)]
    all_to_all x1, starting transfers between devices: 9.78 us -> 8.91 us  [body(): lax.all_to_all(send, ('gx', 'yz'), split_axis=0, concat_axis=0, tiled=True)]
  transfers between devices with their start and end apart: 5 -> 5, of which waited for: 2 -> 2; matrix products, arithmetic and copies ran while one was open for 0% -> 0% of each run, Pallas kernels for 35% -> 36%
where the time goes in v5:
time: 73.7 us; the launch traced here: 73.4 us
  Pallas kernels  35.7 us (48%)
  waiting for transfers between devices  17.4 us (24%)
  starting transfers between devices  17 us (23%)
  local copies, waits for them, and re-layouts  3.11 us (4%)
    all_to_all x1, waiting for transfers between devices, body(): lax.all_to_all(send, ('gx', 'yz'), split_axis=0, concat_axis=0, tiled=True)  17 us
    pallas_call x1, Pallas kernels, body(): pl.pallas_call(keep_kernel, out_shape=pltpu.HBM((19, CAP, 4096), BF16), i...  15.8 us
    all_to_all x1, starting transfers between devices, body(): lax.all_to_all(send, ('gx', 'yz'), split_axis=0, concat_axis=0, tiled=True)  8.91 us
    pallas_call x1, Pallas kernels, body(): pl.pallas_call(inner_kernel, out_shape=(struct((19, 4 * ROWS, 128), F32),...  5.79 us
    pallas_call x1, Pallas kernels, body(): pl.pallas_call(refine_kernel, out_shape=struct((19, CAP, 4096), BF16), in...  4.64 us
    pallas_call x1, Pallas kernels, body(): pl.pallas_call(step_kernel, out_shape=(struct((2, 608, 256), BF16), pltpu...  4.3 us
    ppermute x1, starting transfers between devices, body(): from_right = lax.ppermute(left, 'gx', ring(slabs, -1))  3.71 us
    pallas_call x1, Pallas kernels, body(): pl.pallas_call(collide_kernel, out_shape=struct((19, 16, 32, 128), BF16),...  3.31 us
  transfers between devices with their start and end apart: 5, of which 2 were waited for; matrix products, arithmetic and copies ran while one was open for 0% of the time, Pallas kernels for 36%

profile of v5, /device:TPU:1, one launch (start us, length us, event | category | flops | bytes accessed | tf_op | source)
XLA Modules:
  0.0 73.4 jit_solution(9392990333831594515)
XLA Ops:
  0.0 1.5 %fusion = (bf16[19,16,2,128]{3,2,1,0:T(2,128)(2,1)S(1)}, bf16[19,16,2,128]{3,2,1,0:T(2,128)(2,1)S(1)}) fusion(bf16[19,16,32,128]{3,2,1,0:T(8,128)(2,1)} %pop_ref.1), kind=kLoop, calls=%fused_computation.2 | loop fusion | bytes 622592 | tf_op jit(solution)/shard_map/slice | solution.py:523
  1.6 3.0 %collective-permute-start = (bf16[19,2,16,128]{3,2,1,0:T(8,128)(2,1)S(1)}, bf16[19,2,16,128]{3,2,1,0:T(8,128)(2,1)S(1)}, u32[]{:S(2)}, u32[]{:S(2)}) collective-permute-start(bf16[19,2,16,128]{3,2,1,0:T(8,128)(2,1)S(1)} %bitcast.11), channel_id=1, source_target_pairs={{0,1},{1,2},{2,3},{3,4},{4,5},{5,6},{6,7},{7,0},{8,9},{9,10},{10,1... | collective-permute-start | bytes 466952 | tf_op jit(solution)/shard_map/ppermute | solution.py:524
  4.6 0.0 collective-permute-start.1
  4.6 0.9 %rates.1.rate_ref = f32[3,48,128]{2,1,0:T(8,128)S(1)} custom-call(s32[2048]{0:T(1024)} %levels_ref.1), custom_call_target="tpu_custom_call" | custom-call | bytes 3000000 | tf_op jit(solution)/shard_map/rates/pallas_call | solution.py:527
  5.6 3.3 %collide.1.c1_ref = bf16[19,16,32,128]{3,2,1,0:T(8,128)(2,1)S(1)} custom-call(bf16[19,16,32,128]{3,2,1,0:T(8,128)(2,1)} %pop_ref.1, f32[3,48,128]{2,1,0:T(8,128)S(1)} %rates.1.rate_ref), custom_call_target="tpu_custom_call" | custom-call | bytes 15000000 | tf_op jit(solution)/shard_map/collide/pallas_call | solution.py:537
  8.9 0.0 copy-start.2
  8.9 0.0 copy-start.4
  8.9 0.0 copy-start.5
  8.9 0.0 collective-permute-done.low_ref
  8.9 0.4 collective-permute-done.1.high_ref
  9.3 0.6 faces.1
  9.9 1.4 %collective-permute-start.2 = (bf16[19,40,128]{2,1,0:T(8,128)(2,1)S(1)}, bf16[19,40,128]{2,1,0:T(8,128)(2,1)S(1)}, u32[]{:S(2)}, u32[]{:S(2)}) collective-permute-start(bf16[19,40,128]{2,1,0:T(8,128)(2,1)S(1)} %get-tuple-element.19), channel_id=1, source_target_pairs={{0,8},{8,16},{16,24},{24,32},{32,40},{40,48},{48,56},{56,64},{64,7... | collective-permute-start | bytes 583688 | tf_op jit(solution)/shard_map/ppermute | solution.py:568
  11.3 3.7 %collective-permute-start.3 = (bf16[19,40,128]{2,1,0:T(8,128)(2,1)S(1)}, bf16[19,40,128]{2,1,0:T(8,128)(2,1)S(1)}, u32[]{:S(2)}, u32[]{:S(2)}) collective-permute-start(bf16[19,40,128]{2,1,0:T(8,128)(2,1)S(1)} %get-tuple-element.20), channel_id=1, source_target_pairs={{0,120},{8,0},{16,8},{24,16},{32,24},{40,32},{48,40},{56,48},{64,5... | collective-permute-start | bytes 583688 | tf_op jit(solution)/shard_map/ppermute | solution.py:569
  15.0 0.0 copy-done.2
  15.0 5.8 %inner.1 = (f32[19,192,128]{2,1,0:T(8,128)S(1)}, bf16[6,608,256]{2,1,0:T(8,128)(2,1)S(1)}, f32[16,96,128]{2,1,0:T(8,128)S(1)}) custom-call(bf16[19,16,32,128]{3,2,1,0:T(8,128)(2,1)S(1)} %collide.1.c1_ref, bf16[19,8,16,128]{3,2,1,0:T(8,128)(2,1)S(1)} %get-tuple-element.16.cy_ref, f32[3,48,128]{2,1,0:T(8,128)S(1)} %rates.1.rate_ref, ...), custom_call_target="tpu_custom_call" | custom-call | bytes 18000000 | tf_op jit(solution)/shard_map/inner/pallas_call | solution.py:572
  20.8 0.0 copy-start
  20.8 0.0 collective-permute-done.2.gl_ref
  20.8 0.0 collective-permute-done.3.gr_ref
  20.8 0.0 copy-done.4
  20.8 0.0 copy-done.5
  20.8 4.3 %step.1 = (bf16[2,608,256]{2,1,0:T(8,128)(2,1)S(1)}, bf16[128,19,4,128]{3,2,1,0:T(4,128)(2,1)}) custom-call(s32[2048]{0:T(1024)S(1)} %copy-done.4, s32[2048]{0:T(1024)S(1)} %copy-done.5, f32[19,192,128]{2,1,0:T(8,128)S(1)} %get-tuple-element.17.rest_ref, bf16[19,4,40,128]{3,2,1,0:T(8,128)(2,1)S(1)} %get-tuple-element.18.rim_ref, ...), custom_call_target="tpu_custom_call" | custom-call | bytes 18000000 | tf_op jit(solution)/shard_map/step/pallas_call | solution.py:593
  25.2 0.0 copy-done
  25.2 8.9 %all-to-all-start = ((bf16[128,19,4,128]{3,2,1,0:T(4,128)(2,1)}), bf16[128,19,4,128]{3,2,1,0:T(4,128)(2,1)S(1)}, u32[]{:S(2)}, u32[]{:S(2)}) async-start(bf16[128,19,4,128]{3,2,1,0:T(4,128)(2,1)} %get-tuple-element.25), calls=%async_computation | async-start | bytes 4980736 | tf_op jit(solution)/shard_map/all_to_all | solution.py:615
  34.1 0.4 plan.1
  34.4 0.0 copy-start.1
  34.5 1.5 %copy-done.1 = bf16[6,608,256]{2,1,0:T(8,128)(2,1)S(1)} copy-done((bf16[6,608,256]{2,1,0:T(8,128)(2,1)S(1)}, bf16[6,608,256]{2,1,0:T(8,128)(2,1)}, u32[]{:S(2)}) %copy-start.1) | copy-done | bytes 1867800
  36.0 0.0 copy-start.3
  36.0 15.8 %keep.1.half_ref = bf16[19,24,4096]{2,1,0:T(8,128)(2,1)} custom-call(s32[2048]{0:T(1024)S(1)} %copy-done.4, s32[32,128]{1,0:T(8,128)S(1)} %get-tuple-element.24.owned_ref, bf16[6,608,256]{2,1,0:T(8,128)(2,1)S(1)} %copy-done.1, bf16[2,608,256]{2,1,0:T(8,128)(2,1)S(1)} %get-tuple-element.23.after_ref.outer_ref), custom_call_target="tpu_custom_call" | custom-call | bytes 30000000 | tf_op jit(solution)/shard_map/keep/pallas_call | solution.py:628
  51.7 17.0 %all-to-all-done.recv_ref = bf16[128,19,4,128]{3,2,1,0:T(4,128)(2,1)S(1)} async-done(((bf16[128,19,4,128]{3,2,1,0:T(4,128)(2,1)}), bf16[128,19,4,128]{3,2,1,0:T(4,128)(2,1)S(1)}, u32[]{:S(2)}, u32[]{:S(2)}) %all-to-all-start) | async-done | bytes 2490400 | tf_op jit(solution)/shard_map/all_to_all | solution.py:615
  68.7 0.0 copy-done.3
  68.7 4.6 %refine.1 = bf16[19,24,4096]{2,1,0:T(8,128)(2,1)} custom-call(s32[2048]{0:T(1024)S(1)} %copy-done.4, s32[32,128]{1,0:T(8,128)S(1)} %get-tuple-element.24.owned_ref, bf16[128,19,4,128]{3,2,1,0:T(4,128)(2,1)S(1)} %all-to-all-done.recv_ref, f32[32,128]{1,0:T(8,128)S(1)} %get-tuple-element.26.kind_ref, bf16[256,512]{1,0:T(8,128)(2,1)S(1)} %copy-done.3, ...), custom_call_target="tpu_custom_call" | custom-call | bytes 15000000 | tf_op jit(solution)/shard_map/refine/pallas_call | solution.py:643
  (2 shorter events, 0.0 us)
Async XLA Ops:
  1.6 7.3 %collective-permute-start = (bf16[19,2,16,128]{3,2,1,0:T(8,128)(2,1)S(1)}, bf16[19,2,16,128]{3,2,1,0:T(8,128)(2,1)S(1)}, u32[]{:S(2)}, u32[]{:S(2)}) collective-permute-start(bf16[19,2,16,128]{3,2,1,0:T(8,128)(2,1)S(1)} %bitcast.11), channel_id=1, source_target_pairs={{0,1},{1,2},{2,3},{3,4},{4,5},{5,6},{6,7},{7,0},{8,9},{9,10},{10,1... | collective-permute-start | bytes 466952 | tf_op jit(solution)/shard_map/ppermute | solution.py:524
  4.6 4.7 %collective-permute-start.1 = (bf16[19,2,16,128]{3,2,1,0:T(8,128)(2,1)S(1)}, bf16[19,2,16,128]{3,2,1,0:T(8,128)(2,1)S(1)}, u32[]{:S(2)}, u32[]{:S(2)}) collective-permute-start(bf16[19,2,16,128]{3,2,1,0:T(8,128)(2,1)S(1)} %bitcast.12), channel_id=1, source_target_pairs={{0,7},{1,0},{2,1},{3,2},{4,3},{5,4},{6,5},{7,6},{8,15},{9,8},{10,9... | collective-permute-start | bytes 466952 | tf_op jit(solution)/shard_map/ppermute | solution.py:525
  8.9 6.1 %copy-start.2 = (bf16[2,256,128]{2,1,0:T(8,128)(2,1)S(1)}, bf16[2,256,128]{2,1,0:T(8,128)(2,1)}, u32[]{:S(2)}) copy-start(bf16[2,256,128]{2,1,0:T(8,128)(2,1)} %constant.4.clone.reduce_ref) | copy-start | bytes 393220
  8.9 11.9 %copy-start.4 = (s32[2048]{0:T(1024)S(1)}, s32[2048]{0:T(1024)}, u32[]{:S(2)}) copy-start(s32[2048]{0:T(1024)} %flags_ref.5) | copy-start | bytes 24580
  8.9 11.9 %copy-start.5 = (s32[2048]{0:T(1024)S(1)}, s32[2048]{0:T(1024)}, u32[]{:S(2)}) copy-start(s32[2048]{0:T(1024)} %owner_ref.1) | copy-start | bytes 24580
  9.9 10.9 %collective-permute-start.2 = (bf16[19,40,128]{2,1,0:T(8,128)(2,1)S(1)}, bf16[19,40,128]{2,1,0:T(8,128)(2,1)S(1)}, u32[]{:S(2)}, u32[]{:S(2)}) collective-permute-start(bf16[19,40,128]{2,1,0:T(8,128)(2,1)S(1)} %get-tuple-element.19), channel_id=1, source_target_pairs={{0,8},{8,16},{16,24},{24,32},{32,40},{40,48},{48,56},{56,64},{64,7... | collective-permute-start | bytes 583688 | tf_op jit(solution)/shard_map/ppermute | solution.py:568
  11.3 9.5 %collective-permute-start.3 = (bf16[19,40,128]{2,1,0:T(8,128)(2,1)S(1)}, bf16[19,40,128]{2,1,0:T(8,128)(2,1)S(1)}, u32[]{:S(2)}, u32[]{:S(2)}) collective-permute-start(bf16[19,40,128]{2,1,0:T(8,128)(2,1)S(1)} %get-tuple-element.20), channel_id=1, source_target_pairs={{0,120},{8,0},{16,8},{24,16},{32,24},{40,32},{48,40},{56,48},{64,5... | collective-permute-start | bytes 583688 | tf_op jit(solution)/shard_map/ppermute | solution.py:569
  20.8 4.4 %copy-start = (bf16[6,608,256]{2,1,0:T(8,128)(2,1)}, bf16[6,608,256]{2,1,0:T(8,128)(2,1)S(1)}, u32[]{:S(2)}) copy-start(bf16[6,608,256]{2,1,0:T(8,128)(2,1)S(1)} %get-tuple-element.21.inner_ref) | copy-start | bytes 5603332
  25.2 43.6 %all-to-all-start = ((bf16[128,19,4,128]{3,2,1,0:T(4,128)(2,1)}), bf16[128,19,4,128]{3,2,1,0:T(4,128)(2,1)S(1)}, u32[]{:S(2)}, u32[]{:S(2)}) async-start(bf16[128,19,4,128]{3,2,1,0:T(4,128)(2,1)} %get-tuple-element.25), calls=%async_computation | async-start | bytes 4980736 | tf_op jit(solution)/shard_map/all_to_all | solution.py:615
  34.4 1.5 %copy-start.1 = (bf16[6,608,256]{2,1,0:T(8,128)(2,1)S(1)}, bf16[6,608,256]{2,1,0:T(8,128)(2,1)}, u32[]{:S(2)}) copy-start(bf16[6,608,256]{2,1,0:T(8,128)(2,1)} %copy-done) | copy-start | bytes 5603332
  36.0 32.8 %copy-start.3 = (bf16[256,512]{1,0:T(8,128)(2,1)S(1)}, bf16[256,512]{1,0:T(8,128)(2,1)}, u32[]{:S(2)}) copy-start(bf16[256,512]{1,0:T(8,128)(2,1)} %constant.5.clone.expand_ref) | copy-start | bytes 786436

commit v6 on v5

--- a/solution.py
+++ b/solution.py
@@ -100,9 +100,15 @@
         hit = rank == float(slot + 1)
         part[slot : slot + 1, :] = jnp.sum(jnp.where(hit, marked, 0.0), axis=0, keepdims=True)
         kinds[slot : slot + 1, :] = jnp.sum(jnp.where(hit, flagged, 0.0), axis=0, keepdims=True)
-    found = jnp.sum(part[...], axis=1, keepdims=True) - 1.0
-    owned_ref[...] = jnp.broadcast_to(found, part.shape).astype(jnp.int32)
-    kind_ref[...] = jnp.broadcast_to(jnp.sum(kinds[...], axis=1, keepdims=True), kinds.shape)
+    found = jnp.broadcast_to(jnp.sum(part[...], axis=1, keepdims=True) - 1.0, part.shape)
+    kind = jnp.broadcast_to(jnp.sum(kinds[...], axis=1, keepdims=True), kinds.shape)
+    kind_ref[...] = kind
+
+    own = lax.broadcasted_iota(jnp.int32, part.shape, 0) == lax.broadcasted_iota(jnp.int32, part.shape, 1)
+    found = jnp.sum(jnp.where(own, found, 0.0), axis=0, keepdims=True)
+    kind = jnp.sum(jnp.where(own, kind, 0.0), axis=0, keepdims=True)
+    row = lax.broadcasted_iota(jnp.int32, owned_ref.shape, 0)
+    owned_ref[...] = jnp.where(row == 0, found, kind).astype(jnp.int32)
 
 
 def collide_kernel(pop_ref, rate_ref, c1_ref, planes, sem):
@@ -228,14 +234,15 @@
                     i, slot, 8 * half : 8 * half + 8, :
                 ].astype(F32)
 
-    @pl.loop(0, 14)
-    def _(p):
-        base = pl.multiple_of(p * ROWS, 8)
-        for t in range(5):
-            def at(dx, dy, t=t):
-                return base + ((dx + 1) * ROWS + 7 + 8 * t + dy)
-
-            advance(first, at, rate_ref[1, 7 + 8 * t : 15 + 8 * t, :], second, base + (7 + 8 * t), lane)
+    @pl.loop(0, 7)
+    def _(w):
+        for v in range(2):
+            base = pl.multiple_of((2 * w + v) * ROWS, 8)
+            for t in range(5):
+                def at(dx, dy, t=t, base=base):
+                    return base + ((dx + 1) * ROWS + 7 + 8 * t + dy)
+
+                advance(first, at, rate_ref[1, 7 + 8 * t : 15 + 8 * t, :], second, base + (7 + 8 * t), lane)
 
     copies = [
         pltpu.make_async_copy(
@@ -317,16 +324,17 @@
             if depth == 2 and VEL[i][2] != 0:
                 place(OPP[i], places[1], pltpu.roll(rows, 1 if VEL[i][2] == 1 else 127, axis=1))
 
-    @pl.loop(0, 4)
-    def _(e):
-        above = e // 2
-        base = pl.multiple_of((e + 2 * above) * ROWS, 8)
-        row = pl.multiple_of((e + 4 * above) * ROWS, 8)
-        for t in range(5):
-            def at(dx, dy, t=t):
-                return base + ((dx + 1) * ROWS + 7 + 8 * t + dy)
-
-            advance(first, at, rate_ref[(e + 1) // 2, 7 + 8 * t : 15 + 8 * t, :], second, row + (7 + 8 * t), lane)
+    @pl.loop(0, 2)
+    def _(above):
+        for v in range(2):
+            base = pl.multiple_of((v + 4 * above) * ROWS, 8)
+            row = pl.multiple_of((v + 6 * above) * ROWS, 8)
+            for t in range(5):
+                def at(dx, dy, t=t, base=base):
+                    return base + ((dx + 1) * ROWS + 7 + 8 * t + dy)
+
+                rate = rate_ref[above + v, 7 + 8 * t : 15 + 8 * t, :]
+                advance(first, at, rate, second, row + (7 + 8 * t), lane)
 
     rest.wait()
 
@@ -360,7 +368,7 @@
             pltpu.make_async_copy(stage.at[k], send_ref.at[0], send_sem.at[k]).wait()
 
 
-def keep_kernel(flags_ref, owned_ref, inner_ref, outer_ref, half_ref, mix, slots, place):
+def keep_kernel(owned_ref, inner_ref, outer_ref, half_ref, mix, slots, place):
     me = lax.axis_index("gx") * lax.axis_size("yz") + lax.axis_index("yz")
     lane = lax.broadcasted_iota(jnp.int32, (8, 128), 1)
 
@@ -370,9 +378,9 @@
 
     @pl.loop(0, CAP)
     def _(s):
-        b = owned_ref[s, 0]
-
-        @pl.when((b >= 0) & (flags_ref[jnp.maximum(b, 0)] == 0))
+        b = owned_ref[0, s]
+
+        @pl.when((b >= 0) & (owned_ref[1, s] == 0))
         def _():
             place[b - me * BLK] = s
 
@@ -412,7 +420,7 @@
 
 
 def refine_kernel(
-    flags_ref, owned_ref, recv_ref, kind_ref, expand_ref, half_ref, out_ref,
+    owned_ref, recv_ref, kind_ref, expand_ref, half_ref, out_ref,
     rows, wide, product, half, result, half_sem, out_sem,
 ):
     @pl.loop(0, 19)
@@ -421,9 +429,9 @@
 
     @pl.loop(0, CAP)
     def _(s):
-        b = owned_ref[s, 0]
-
-        @pl.when((b >= 0) & (flags_ref[jnp.maximum(b, 0)] != 0))
+        b = owned_ref[0, s]
+
+        @pl.when(owned_ref[1, s] != 0)
         def _():
             for i in range(19):
                 rows[pl.ds(96 * i + s, 4, stride=24), :] = recv_ref[b // BLK, i, :, :].astype(F32)
@@ -616,7 +624,7 @@
 
     owned, kind = pl.pallas_call(
         plan_kernel,
-        out_shape=(struct((32, 128), jnp.int32), struct((32, 128), F32)),
+        out_shape=(struct((8, 128), jnp.int32), struct((32, 128), F32)),
         in_specs=[VM, VM, ANY],
         out_specs=(VM, VM),
         scratch_shapes=[pltpu.VMEM((32, 128), F32), pltpu.VMEM((32, 128), F32)],
@@ -628,7 +636,7 @@
     half = pl.pallas_call(
         keep_kernel,
         out_shape=pltpu.HBM((19, CAP, 4096), BF16),
-        in_specs=[SM, SM, VM, VM],
+        in_specs=[SM, VM, VM],
         out_specs=VM,
         scratch_shapes=[
             pltpu.VMEM((4, 192, 128), F32),
@@ -638,12 +646,12 @@
         compiler_params=limit(20),
         cost_estimate=cost(10),
         name="keep",
-    )(refine_flags, owned, inner, outer)
+    )(owned, inner, outer)
 
     migrated = pl.pallas_call(
         refine_kernel,
         out_shape=struct((19, CAP, 4096), BF16),
-        in_specs=[SM, SM, VM, VM, VM, HBM],
+        in_specs=[SM, VM, VM, VM, HBM],
         out_specs=ANY,
         scratch_shapes=[
             pltpu.VMEM((CAP * 76, 128), F32),
@@ -657,7 +665,7 @@
         compiler_params=limit(18),
         cost_estimate=cost(5),
         name="refine",
-    )(refine_flags, owned, recv, kind, jnp.asarray(expand_matrix(), BF16), in_hbm(half))
+    )(owned, recv, kind, jnp.asarray(expand_matrix(), BF16), in_hbm(half))
     return jnp.transpose(migrated, (1, 0, 2))
 
 

time: 73.7 us -> 73 us (level)
  Pallas kernels: 35.7 us -> 34.2 us
  transfers between devices with their start and end apart: 5 -> 5, of which waited for: 2 -> 2; matrix products, arithmetic and copies ran while one was open for 0% -> 0% of each run, Pallas kernels for 36% -> 35%
where the time goes in v6:
time: 73 us; the launch traced here: 72.8 us
  Pallas kernels  34.2 us (47%)
  waiting for transfers between devices  17.8 us (24%)
  starting transfers between devices  17.5 us (24%)
  local copies, waits for them, and re-layouts  3.11 us (4%)
    all_to_all x1, waiting for transfers between devices, body(): lax.all_to_all(send, ('gx', 'yz'), split_axis=0, concat_axis=0, tiled=True)  17.4 us
    pallas_call x1, Pallas kernels, body(): pl.pallas_call(keep_kernel, out_shape=pltpu.HBM((19, CAP, 4096), BF16), i...  15.3 us
    all_to_all x1, starting transfers between devices, body(): lax.all_to_all(send, ('gx', 'yz'), split_axis=0, concat_axis=0, tiled=True)  9.4 us
    pallas_call x1, Pallas kernels, body(): pl.pallas_call(inner_kernel, out_shape=(struct((19, 4 * ROWS, 128), F32),...  5.26 us
    pallas_call x1, Pallas kernels, body(): pl.pallas_call(refine_kernel, out_shape=struct((19, CAP, 4096), BF16), in...  4.24 us
    pallas_call x1, Pallas kernels, body(): pl.pallas_call(step_kernel, out_shape=(struct((2, 608, 256), BF16), pltpu...  4.14 us
    ppermute x1, starting transfers between devices, body(): from_right = lax.ppermute(left, 'gx', ring(slabs, -1))  3.71 us
    pallas_call x1, Pallas kernels, body(): pl.pallas_call(collide_kernel, out_shape=struct((19, 16, 32, 128), BF16),...  3.31 us
  transfers between devices with their start and end apart: 5, of which 2 were waited for; matrix products, arithmetic and copies ran while one was open for 0% of the time, Pallas kernels for 35%

profile of v6, /device:TPU:1, one launch (start us, length us, event | category | flops | bytes accessed | tf_op | source)
XLA Modules:
  0.0 72.8 jit_solution(14573468860272241425)
XLA Ops:
  0.0 1.5 %fusion = (bf16[19,16,2,128]{3,2,1,0:T(2,128)(2,1)S(1)}, bf16[19,16,2,128]{3,2,1,0:T(2,128)(2,1)S(1)}) fusion(bf16[19,16,32,128]{3,2,1,0:T(8,128)(2,1)} %pop_ref.1), kind=kLoop, calls=%fused_computation.2 | loop fusion | bytes 622592 | tf_op jit(solution)/shard_map/slice | solution.py:531
  1.6 3.0 %collective-permute-start = (bf16[19,2,16,128]{3,2,1,0:T(8,128)(2,1)S(1)}, bf16[19,2,16,128]{3,2,1,0:T(8,128)(2,1)S(1)}, u32[]{:S(2)}, u32[]{:S(2)}) collective-permute-start(bf16[19,2,16,128]{3,2,1,0:T(8,128)(2,1)S(1)} %bitcast.11), channel_id=1, source_target_pairs={{0,1},{1,2},{2,3},{3,4},{4,5},{5,6},{6,7},{7,0},{8,9},{9,10},{10,1... | collective-permute-start | bytes 466952 | tf_op jit(solution)/shard_map/ppermute | solution.py:532
  4.6 0.0 collective-permute-start.1
  4.6 0.9 %rates.1.rate_ref = f32[3,48,128]{2,1,0:T(8,128)S(1)} custom-call(s32[2048]{0:T(1024)} %levels_ref.1), custom_call_target="tpu_custom_call" | custom-call | bytes 3000000 | tf_op jit(solution)/shard_map/rates/pallas_call | solution.py:535
  5.6 3.3 %collide.1.c1_ref = bf16[19,16,32,128]{3,2,1,0:T(8,128)(2,1)S(1)} custom-call(bf16[19,16,32,128]{3,2,1,0:T(8,128)(2,1)} %pop_ref.1, f32[3,48,128]{2,1,0:T(8,128)S(1)} %rates.1.rate_ref), custom_call_target="tpu_custom_call" | custom-call | bytes 15000000 | tf_op jit(solution)/shard_map/collide/pallas_call | solution.py:545
  8.9 0.0 copy-start.2
  8.9 0.0 copy-start.4
  8.9 0.0 copy-start.5
  8.9 0.0 collective-permute-done.low_ref
  8.9 0.4 collective-permute-done.1.high_ref
  9.3 0.6 faces.1
  9.9 1.4 %collective-permute-start.2 = (bf16[19,40,128]{2,1,0:T(8,128)(2,1)S(1)}, bf16[19,40,128]{2,1,0:T(8,128)(2,1)S(1)}, u32[]{:S(2)}, u32[]{:S(2)}) collective-permute-start(bf16[19,40,128]{2,1,0:T(8,128)(2,1)S(1)} %get-tuple-element.19), channel_id=1, source_target_pairs={{0,8},{8,16},{16,24},{24,32},{32,40},{40,48},{48,56},{56,64},{64,7... | collective-permute-start | bytes 583688 | tf_op jit(solution)/shard_map/ppermute | solution.py:576
  11.3 3.7 %collective-permute-start.3 = (bf16[19,40,128]{2,1,0:T(8,128)(2,1)S(1)}, bf16[19,40,128]{2,1,0:T(8,128)(2,1)S(1)}, u32[]{:S(2)}, u32[]{:S(2)}) collective-permute-start(bf16[19,40,128]{2,1,0:T(8,128)(2,1)S(1)} %get-tuple-element.20), channel_id=1, source_target_pairs={{0,120},{8,0},{16,8},{24,16},{32,24},{40,32},{48,40},{56,48},{64,5... | collective-permute-start | bytes 583688 | tf_op jit(solution)/shard_map/ppermute | solution.py:577
  15.0 0.0 copy-done.2
  15.0 5.3 %inner.1 = (f32[19,192,128]{2,1,0:T(8,128)S(1)}, bf16[6,608,256]{2,1,0:T(8,128)(2,1)S(1)}, f32[16,96,128]{2,1,0:T(8,128)S(1)}) custom-call(bf16[19,16,32,128]{3,2,1,0:T(8,128)(2,1)S(1)} %collide.1.c1_ref, bf16[19,8,16,128]{3,2,1,0:T(8,128)(2,1)S(1)} %get-tuple-element.16.cy_ref, f32[3,48,128]{2,1,0:T(8,128)S(1)} %rates.1.rate_ref, ...), custom_call_target="tpu_custom_call" | custom-call | bytes 18000000 | tf_op jit(solution)/shard_map/inner/pallas_call | solution.py:580
  20.3 0.0 copy-start
  20.3 0.0 collective-permute-done.2.gl_ref
  20.3 0.0 collective-permute-done.3.gr_ref
  20.3 0.0 copy-done.4
  20.3 0.0 copy-done.5
  20.3 4.1 %step.1 = (bf16[2,608,256]{2,1,0:T(8,128)(2,1)S(1)}, bf16[128,19,4,128]{3,2,1,0:T(4,128)(2,1)}) custom-call(s32[2048]{0:T(1024)S(1)} %copy-done.4, s32[2048]{0:T(1024)S(1)} %copy-done.5, f32[19,192,128]{2,1,0:T(8,128)S(1)} %get-tuple-element.17.rest_ref, bf16[19,4,40,128]{3,2,1,0:T(8,128)(2,1)S(1)} %get-tuple-element.18.rim_ref, ...), custom_call_target="tpu_custom_call" | custom-call | bytes 18000000 | tf_op jit(solution)/shard_map/step/pallas_call | solution.py:601
  24.5 0.0 copy-done
  24.5 9.4 %all-to-all-start = ((bf16[128,19,4,128]{3,2,1,0:T(4,128)(2,1)}), bf16[128,19,4,128]{3,2,1,0:T(4,128)(2,1)S(1)}, u32[]{:S(2)}, u32[]{:S(2)}) async-start(bf16[128,19,4,128]{3,2,1,0:T(4,128)(2,1)} %get-tuple-element.25), calls=%async_computation | async-start | bytes 4980736 | tf_op jit(solution)/shard_map/all_to_all | solution.py:623
  33.9 0.4 plan.1
  34.3 0.0 copy-start.1
  34.3 1.5 %copy-done.1 = bf16[6,608,256]{2,1,0:T(8,128)(2,1)S(1)} copy-done((bf16[6,608,256]{2,1,0:T(8,128)(2,1)S(1)}, bf16[6,608,256]{2,1,0:T(8,128)(2,1)}, u32[]{:S(2)}) %copy-start.1) | copy-done | bytes 1867800
  35.8 0.0 copy-start.3
  35.8 15.3 %keep.1.half_ref = bf16[19,24,4096]{2,1,0:T(8,128)(2,1)} custom-call(s32[8,128]{1,0:T(8,128)S(1)} %get-tuple-element.24.owned_ref, bf16[6,608,256]{2,1,0:T(8,128)(2,1)S(1)} %copy-done.1, bf16[2,608,256]{2,1,0:T(8,128)(2,1)S(1)} %get-tuple-element.23.after_ref.outer_ref), custom_call_target="tpu_custom_call" | custom-call | bytes 30000000 | tf_op jit(solution)/shard_map/keep/pallas_call | solution.py:636
  51.1 17.4 %all-to-all-done.recv_ref = bf16[128,19,4,128]{3,2,1,0:T(4,128)(2,1)S(1)} async-done(((bf16[128,19,4,128]{3,2,1,0:T(4,128)(2,1)}), bf16[128,19,4,128]{3,2,1,0:T(4,128)(2,1)S(1)}, u32[]{:S(2)}, u32[]{:S(2)}) %all-to-all-start) | async-done | bytes 2490400 | tf_op jit(solution)/shard_map/all_to_all | solution.py:623
  68.5 0.0 copy-done.3
  68.5 4.2 %refine.1 = bf16[19,24,4096]{2,1,0:T(8,128)(2,1)} custom-call(s32[8,128]{1,0:T(8,128)S(1)} %get-tuple-element.24.owned_ref, bf16[128,19,4,128]{3,2,1,0:T(4,128)(2,1)S(1)} %all-to-all-done.recv_ref, f32[32,128]{1,0:T(8,128)S(1)} %get-tuple-element.26.kind_ref, bf16[256,512]{1,0:T(8,128)(2,1)S(1)} %copy-done.3, bf16[19,24,4096]{2,1,0:T(8,128)(2,1)} %keep.1.half_ref), custom_call_target="tpu_custom_call" | custom-call | bytes 15000000 | tf_op jit(solution)/shard_map/refine/pallas_call | solution.py:651
  (2 shorter events, 0.0 us)
Async XLA Ops:
  1.6 7.3 %collective-permute-start = (bf16[19,2,16,128]{3,2,1,0:T(8,128)(2,1)S(1)}, bf16[19,2,16,128]{3,2,1,0:T(8,128)(2,1)S(1)}, u32[]{:S(2)}, u32[]{:S(2)}) collective-permute-start(bf16[19,2,16,128]{3,2,1,0:T(8,128)(2,1)S(1)} %bitcast.11), channel_id=1, source_target_pairs={{0,1},{1,2},{2,3},{3,4},{4,5},{5,6},{6,7},{7,0},{8,9},{9,10},{10,1... | collective-permute-start | bytes 466952 | tf_op jit(solution)/shard_map/ppermute | solution.py:532
  4.6 4.7 %collective-permute-start.1 = (bf16[19,2,16,128]{3,2,1,0:T(8,128)(2,1)S(1)}, bf16[19,2,16,128]{3,2,1,0:T(8,128)(2,1)S(1)}, u32[]{:S(2)}, u32[]{:S(2)}) collective-permute-start(bf16[19,2,16,128]{3,2,1,0:T(8,128)(2,1)S(1)} %bitcast.12), channel_id=1, source_target_pairs={{0,7},{1,0},{2,1},{3,2},{4,3},{5,4},{6,5},{7,6},{8,15},{9,8},{10,9... | collective-permute-start | bytes 466952 | tf_op jit(solution)/shard_map/ppermute | solution.py:533
  8.9 6.1 %copy-start.2 = (bf16[2,256,128]{2,1,0:T(8,128)(2,1)S(1)}, bf16[2,256,128]{2,1,0:T(8,128)(2,1)}, u32[]{:S(2)}) copy-start(bf16[2,256,128]{2,1,0:T(8,128)(2,1)} %constant.4.clone.reduce_ref) | copy-start | bytes 393220
  8.9 11.4 %copy-start.4 = (s32[2048]{0:T(1024)S(1)}, s32[2048]{0:T(1024)}, u32[]{:S(2)}) copy-start(s32[2048]{0:T(1024)} %flags_ref.1) | copy-start | bytes 24580
  8.9 11.4 %copy-start.5 = (s32[2048]{0:T(1024)S(1)}, s32[2048]{0:T(1024)}, u32[]{:S(2)}) copy-start(s32[2048]{0:T(1024)} %owner_ref.1) | copy-start | bytes 24580
  9.9 10.4 %collective-permute-start.2 = (bf16[19,40,128]{2,1,0:T(8,128)(2,1)S(1)}, bf16[19,40,128]{2,1,0:T(8,128)(2,1)S(1)}, u32[]{:S(2)}, u32[]{:S(2)}) collective-permute-start(bf16[19,40,128]{2,1,0:T(8,128)(2,1)S(1)} %get-tuple-element.19), channel_id=1, source_target_pairs={{0,8},{8,16},{16,24},{24,32},{32,40},{40,48},{48,56},{56,64},{64,7... | collective-permute-start | bytes 583688 | tf_op jit(solution)/shard_map/ppermute | solution.py:576
  11.3 9.0 %collective-permute-start.3 = (bf16[19,40,128]{2,1,0:T(8,128)(2,1)S(1)}, bf16[19,40,128]{2,1,0:T(8,128)(2,1)S(1)}, u32[]{:S(2)}, u32[]{:S(2)}) collective-permute-start(bf16[19,40,128]{2,1,0:T(8,128)(2,1)S(1)} %get-tuple-element.20), channel_id=1, source_target_pairs={{0,120},{8,0},{16,8},{24,16},{32,24},{40,32},{48,40},{56,48},{64,5... | collective-permute-start | bytes 583688 | tf_op jit(solution)/shard_map/ppermute | solution.py:577
  20.3 4.2 %copy-start = (bf16[6,608,256]{2,1,0:T(8,128)(2,1)}, bf16[6,608,256]{2,1,0:T(8,128)(2,1)S(1)}, u32[]{:S(2)}) copy-start(bf16[6,608,256]{2,1,0:T(8,128)(2,1)S(1)} %get-tuple-element.21.inner_ref) | copy-start | bytes 5603332
  24.5 44.1 %all-to-all-start = ((bf16[128,19,4,128]{3,2,1,0:T(4,128)(2,1)}), bf16[128,19,4,128]{3,2,1,0:T(4,128)(2,1)S(1)}, u32[]{:S(2)}, u32[]{:S(2)}) async-start(bf16[128,19,4,128]{3,2,1,0:T(4,128)(2,1)} %get-tuple-element.25), calls=%async_computation | async-start | bytes 4980736 | tf_op jit(solution)/shard_map/all_to_all | solution.py:623
  34.3 1.5 %copy-start.1 = (bf16[6,608,256]{2,1,0:T(8,128)(2,1)S(1)}, bf16[6,608,256]{2,1,0:T(8,128)(2,1)}, u32[]{:S(2)}) copy-start(bf16[6,608,256]{2,1,0:T(8,128)(2,1)} %copy-done) | copy-start | bytes 5603332
  35.8 32.8 %copy-start.3 = (bf16[256,512]{1,0:T(8,128)(2,1)S(1)}, bf16[256,512]{1,0:T(8,128)(2,1)}, u32[]{:S(2)}) copy-start(bf16[256,512]{1,0:T(8,128)(2,1)} %constant.5.clone.expand_ref) | copy-start | bytes 786436

commit v7 on v6

--- a/solution.py
+++ b/solution.py
@@ -218,9 +218,17 @@
 
 
 def inner_kernel(
-    c1_ref, cy_ref, rate_ref, reduce_ref, rest_ref, state_ref, middle_ref, first, second, mean, mix, sem
+    c1_ref, cy_ref, rate_ref, reduce_ref, flags_ref, owner_ref, rest_ref, state_ref, middle_ref, target_ref,
+    first, second, mean, mix, sem,
 ):
     lane = lax.broadcasted_iota(jnp.int32, (8, 128), 1)
+
+    me = lax.axis_index("gx") * lax.axis_size("yz") + lax.axis_index("yz")
+    mine = lax.broadcasted_iota(jnp.int32, owner_ref.shape, 0) == me // 8
+    goes = jnp.where(flags_ref[...] != 0, owner_ref[...], -1).astype(F32)
+    goes = jnp.broadcast_to(jnp.sum(jnp.where(mine, goes, 0.0), axis=0, keepdims=True), (8, 128))
+    goes = pltpu.roll(goes, lax.rem(128 - lax.rem(me, 8) * BLK, 128), axis=1)
+    target_ref[...] = goes.astype(jnp.int32)
 
     @pl.loop(0, 16)
     def _(x):
@@ -300,11 +308,10 @@
 
 
 def step_kernel(
-    flags_ref, owner_ref, rest_ref, rim_ref, gl_ref, gr_ref, rate_ref, reduce_ref, inner_ref, middle_ref,
+    target_ref, rest_ref, rim_ref, gl_ref, gr_ref, rate_ref, reduce_ref, inner_ref, middle_ref,
     outer_ref, send_ref,
     first, second, mean, mix, pack, stage, in_sem, send_sem,
 ):
-    me = lax.axis_index("gx") * lax.axis_size("yz") + lax.axis_index("yz")
     lane = lax.broadcasted_iota(jnp.int32, (8, 128), 1)
     rest = pltpu.make_async_copy(rest_ref, second.at[:, 2 * ROWS : 6 * ROWS], in_sem)
     rest.start()
@@ -354,16 +361,16 @@
 
     @pl.loop(0, BLK)
     def _(k):
-        @pl.when(flags_ref[me * BLK + k] != 0)
+        @pl.when(target_ref[0, k] >= 0)
         def _():
             for i in range(19):
                 rows = slice(4 * i, 4 * i + 4)
                 stage[k, i, :, :] = jnp.where(middle, middle_ref[k, rows, :], pack[k, rows, :]).astype(BF16)
-            pltpu.make_async_copy(stage.at[k], send_ref.at[owner_ref[me * BLK + k]], send_sem.at[k]).start()
+            pltpu.make_async_copy(stage.at[k], send_ref.at[target_ref[0, k]], send_sem.at[k]).start()
 
     @pl.loop(0, BLK)
     def _(k):
-        @pl.when(flags_ref[me * BLK + k] != 0)
+        @pl.when(target_ref[0, k] >= 0)
         def _():
             pltpu.make_async_copy(stage.at[k], send_ref.at[0], send_sem.at[k]).wait()
 
@@ -577,15 +584,18 @@
     from_right = lax.ppermute(left, "gx", ring(slabs, -1))
 
     reduce = jnp.asarray(mean_matrix(), BF16)
-    rest, inner, middle = pl.pallas_call(
+    flag_rows = refine_flags.reshape(total // 128, 128)
+    owner_rows = new_owner.reshape(total // 128, 128)
+    rest, inner, middle, target = pl.pallas_call(
         inner_kernel,
         out_shape=(
             struct((19, 4 * ROWS, 128), F32),
             struct((6, 608, 256), BF16),
             struct((BLK, 96, 128), F32),
+            struct((8, 128), jnp.int32),
         ),
-        in_specs=[VM] * 4,
-        out_specs=(ANY, VM, VM),
+        in_specs=[VM] * 6,
+        out_specs=(ANY, VM, VM, VM),
         scratch_shapes=[
             pltpu.VMEM((19, 16 * ROWS, 128), F32),
             pltpu.VMEM((19, 14 * ROWS, 128), F32),
@@ -596,12 +606,12 @@
         compiler_params=limit(22),
         cost_estimate=cost(6),
         name="inner",
-    )(c1, cy, rate, reduce)
+    )(c1, cy, rate, reduce, flag_rows, owner_rows)
 
     outer, send = pl.pallas_call(
         step_kernel,
         out_shape=(struct((2, 608, 256), BF16), pltpu.HBM((devices, 19, 4, 128), BF16)),
-        in_specs=[SM, SM, ANY] + [VM] * 7,
+        in_specs=[SM, ANY] + [VM] * 7,
         out_specs=(VM, HBM),
         scratch_shapes=[
             pltpu.VMEM((19, 8 * ROWS, 128), F32),
@@ -617,7 +627,7 @@
         cost_estimate=cost(6),
         name="step",
     )(
-        refine_flags, new_owner, rest, rim, from_left, from_right, rate, reduce, inner, middle,
+        target, rest, rim, from_left, from_right, rate, reduce, inner, middle,
     )
 
     recv = lax.all_to_all(send, ("gx", "yz"), split_axis=0, concat_axis=0, tiled=True)

time: 73 us -> 72.8 us (level)
  no operation moved by 1% of the time
where the time goes in v7:
time: 72.8 us; the launch traced here: 72.5 us
  Pallas kernels  34 us (47%)
  waiting for transfers between devices  17.8 us (24%)
  starting transfers between devices  17.5 us (24%)
  local copies, waits for them, and re-layouts  3.11 us (4%)
    all_to_all x1, waiting for transfers between devices, body(): lax.all_to_all(send, ('gx', 'yz'), split_axis=0, concat_axis=0, tiled=True)  17.4 us
    pallas_call x1, Pallas kernels, body(): pl.pallas_call(keep_kernel, out_shape=pltpu.HBM((19, CAP, 4096), BF16), i...  15.3 us
    all_to_all x1, starting transfers between devices, body(): lax.all_to_all(send, ('gx', 'yz'), split_axis=0, concat_axis=0, tiled=True)  9.36 us
    pallas_call x1, Pallas kernels, body(): pl.pallas_call(inner_kernel, out_shape=(struct((19, 4 * ROWS, 128), F32),...  5.35 us
    pallas_call x1, Pallas kernels, body(): pl.pallas_call(refine_kernel, out_shape=struct((19, CAP, 4096), BF16), in...  4.14 us
    pallas_call x1, Pallas kernels, body(): pl.pallas_call(step_kernel, out_shape=(struct((2, 608, 256), BF16), pltpu...  3.92 us
    ppermute x1, starting transfers between devices, body(): from_right = lax.ppermute(left, 'gx', ring(slabs, -1))  3.71 us
    pallas_call x1, Pallas kernels, body(): pl.pallas_call(collide_kernel, out_shape=struct((19, 16, 32, 128), BF16),...  3.31 us
  transfers between devices with their start and end apart: 5, of which 2 were waited for; matrix products, arithmetic and copies ran while one was open for 0% of the time, Pallas kernels for 35%

profile of v7, /device:TPU:1, one launch (start us, length us, event | category | flops | bytes accessed | tf_op | source)
XLA Modules:
  0.0 72.5 jit_solution(3826657673461327396)
XLA Ops:
  0.0 1.5 %fusion = (bf16[19,16,2,128]{3,2,1,0:T(2,128)(2,1)S(1)}, bf16[19,16,2,128]{3,2,1,0:T(2,128)(2,1)S(1)}) fusion(bf16[19,16,32,128]{3,2,1,0:T(8,128)(2,1)} %pop_ref.1), kind=kLoop, calls=%fused_computation.2 | loop fusion | bytes 622592 | tf_op jit(solution)/shard_map/slice | solution.py:538
  1.6 3.0 %collective-permute-start = (bf16[19,2,16,128]{3,2,1,0:T(8,128)(2,1)S(1)}, bf16[19,2,16,128]{3,2,1,0:T(8,128)(2,1)S(1)}, u32[]{:S(2)}, u32[]{:S(2)}) collective-permute-start(bf16[19,2,16,128]{3,2,1,0:T(8,128)(2,1)S(1)} %bitcast.13), channel_id=1, source_target_pairs={{0,1},{1,2},{2,3},{3,4},{4,5},{5,6},{6,7},{7,0},{8,9},{9,10},{10,1... | collective-permute-start | bytes 466952 | tf_op jit(solution)/shard_map/ppermute | solution.py:539
  4.6 0.0 collective-permute-start.1
  4.6 0.9 %rates.1.rate_ref = f32[3,48,128]{2,1,0:T(8,128)S(1)} custom-call(s32[2048]{0:T(1024)} %levels_ref.1), custom_call_target="tpu_custom_call" | custom-call | bytes 3000000 | tf_op jit(solution)/shard_map/rates/pallas_call | solution.py:542
  5.6 3.3 %collide.1.c1_ref = bf16[19,16,32,128]{3,2,1,0:T(8,128)(2,1)S(1)} custom-call(bf16[19,16,32,128]{3,2,1,0:T(8,128)(2,1)} %pop_ref.1, f32[3,48,128]{2,1,0:T(8,128)S(1)} %rates.1.rate_ref), custom_call_target="tpu_custom_call" | custom-call | bytes 15000000 | tf_op jit(solution)/shard_map/collide/pallas_call | solution.py:552
  8.9 0.0 copy-start.2
  8.9 0.0 copy-start.4
  8.9 0.0 copy-start.5
  8.9 0.0 collective-permute-done.low_ref
  8.9 0.4 collective-permute-done.1.high_ref
  9.3 0.6 faces.1
  9.9 1.4 %collective-permute-start.2 = (bf16[19,40,128]{2,1,0:T(8,128)(2,1)S(1)}, bf16[19,40,128]{2,1,0:T(8,128)(2,1)S(1)}, u32[]{:S(2)}, u32[]{:S(2)}) collective-permute-start(bf16[19,40,128]{2,1,0:T(8,128)(2,1)S(1)} %get-tuple-element.21), channel_id=1, source_target_pairs={{0,8},{8,16},{16,24},{24,32},{32,40},{40,48},{48,56},{56,64},{64,7... | collective-permute-start | bytes 583688 | tf_op jit(solution)/shard_map/ppermute | solution.py:583
  11.3 3.7 %collective-permute-start.3 = (bf16[19,40,128]{2,1,0:T(8,128)(2,1)S(1)}, bf16[19,40,128]{2,1,0:T(8,128)(2,1)S(1)}, u32[]{:S(2)}, u32[]{:S(2)}) collective-permute-start(bf16[19,40,128]{2,1,0:T(8,128)(2,1)S(1)} %get-tuple-element.22), channel_id=1, source_target_pairs={{0,120},{8,0},{16,8},{24,16},{32,24},{40,32},{48,40},{56,48},{64,5... | collective-permute-start | bytes 583688 | tf_op jit(solution)/shard_map/ppermute | solution.py:584
  15.0 0.0 copy-done.2
  15.0 0.0 copy-done.4
  15.0 0.0 copy-done.5
  15.0 5.4 %inner.1 = (f32[19,192,128]{2,1,0:T(8,128)S(1)}, bf16[6,608,256]{2,1,0:T(8,128)(2,1)S(1)}, f32[16,96,128]{2,1,0:T(8,128)S(1)}, s32[8,128]{1,0:T(8,128)S(1)}) custom-call(bf16[19,16,32,128]{3,2,1,0:T(8,128)(2,1)S(1)} %collide.1.c1_ref, bf16[19,8,16,128]{3,2,1,0:T(8,128)(2,1)S(1)} %get-tuple-element.17.cy_ref, f32[3,48,128]{2,1,0:T(8,128)S(1)} %rates.1.rate_ref, ...), custom_call_target="tpu_custom_call" | custom-call | bytes 18000000 | tf_op jit(solution)/shard_map/inner/pallas_call | solution.py:589
  20.4 0.0 copy-start
  20.4 0.0 collective-permute-done.2.gl_ref
  20.4 0.0 collective-permute-done.3.gr_ref
  20.4 3.9 %step.1 = (bf16[2,608,256]{2,1,0:T(8,128)(2,1)S(1)}, bf16[128,19,4,128]{3,2,1,0:T(4,128)(2,1)}) custom-call(s32[8,128]{1,0:T(8,128)S(1)} %get-tuple-element.18.target_ref, f32[19,192,128]{2,1,0:T(8,128)S(1)} %get-tuple-element.19.rest_ref, bf16[19,4,40,128]{3,2,1,0:T(8,128)(2,1)S(1)} %get-tuple-element.20.rim_ref, ...), custom_call_target="tpu_custom_call" | custom-call | bytes 18000000 | tf_op jit(solution)/shard_map/step/pallas_call | solution.py:611
  24.3 0.0 copy-done
  24.3 9.4 %all-to-all-start = ((bf16[128,19,4,128]{3,2,1,0:T(4,128)(2,1)}), bf16[128,19,4,128]{3,2,1,0:T(4,128)(2,1)S(1)}, u32[]{:S(2)}, u32[]{:S(2)}) async-start(bf16[128,19,4,128]{3,2,1,0:T(4,128)(2,1)} %get-tuple-element.27), calls=%async_computation | async-start | bytes 4980736 | tf_op jit(solution)/shard_map/all_to_all | solution.py:633
  33.7 0.4 plan.1
  34.1 0.0 copy-start.1
  34.1 1.5 %copy-done.1 = bf16[6,608,256]{2,1,0:T(8,128)(2,1)S(1)} copy-done((bf16[6,608,256]{2,1,0:T(8,128)(2,1)S(1)}, bf16[6,608,256]{2,1,0:T(8,128)(2,1)}, u32[]{:S(2)}) %copy-start.1) | copy-done | bytes 1867800
  35.6 0.0 copy-start.3
  35.6 15.3 %keep.1.half_ref = bf16[19,24,4096]{2,1,0:T(8,128)(2,1)} custom-call(s32[8,128]{1,0:T(8,128)S(1)} %get-tuple-element.26.owned_ref, bf16[6,608,256]{2,1,0:T(8,128)(2,1)S(1)} %copy-done.1, bf16[2,608,256]{2,1,0:T(8,128)(2,1)S(1)} %get-tuple-element.25.after_ref.outer_ref), custom_call_target="tpu_custom_call" | custom-call | bytes 30000000 | tf_op jit(solution)/shard_map/keep/pallas_call | solution.py:646
  50.9 17.4 %all-to-all-done.recv_ref = bf16[128,19,4,128]{3,2,1,0:T(4,128)(2,1)S(1)} async-done(((bf16[128,19,4,128]{3,2,1,0:T(4,128)(2,1)}), bf16[128,19,4,128]{3,2,1,0:T(4,128)(2,1)S(1)}, u32[]{:S(2)}, u32[]{:S(2)}) %all-to-all-start) | async-done | bytes 2490400 | tf_op jit(solution)/shard_map/all_to_all | solution.py:633
  68.4 0.0 copy-done.3
  68.4 4.1 %refine.1 = bf16[19,24,4096]{2,1,0:T(8,128)(2,1)} custom-call(s32[8,128]{1,0:T(8,128)S(1)} %get-tuple-element.26.owned_ref, bf16[128,19,4,128]{3,2,1,0:T(4,128)(2,1)S(1)} %all-to-all-done.recv_ref, f32[32,128]{1,0:T(8,128)S(1)} %get-tuple-element.28.kind_ref, bf16[256,512]{1,0:T(8,128)(2,1)S(1)} %copy-done.3, bf16[19,24,4096]{2,1,0:T(8,128)(2,1)} %keep.1.half_ref), custom_call_target="tpu_custom_call" | custom-call | bytes 15000000 | tf_op jit(solution)/shard_map/refine/pallas_call | solution.py:661
  (2 shorter events, 0.0 us)
Async XLA Ops:
  1.6 7.3 %collective-permute-start = (bf16[19,2,16,128]{3,2,1,0:T(8,128)(2,1)S(1)}, bf16[19,2,16,128]{3,2,1,0:T(8,128)(2,1)S(1)}, u32[]{:S(2)}, u32[]{:S(2)}) collective-permute-start(bf16[19,2,16,128]{3,2,1,0:T(8,128)(2,1)S(1)} %bitcast.13), channel_id=1, source_target_pairs={{0,1},{1,2},{2,3},{3,4},{4,5},{5,6},{6,7},{7,0},{8,9},{9,10},{10,1... | collective-permute-start | bytes 466952 | tf_op jit(solution)/shard_map/ppermute | solution.py:539
  4.6 4.7 %collective-permute-start.1 = (bf16[19,2,16,128]{3,2,1,0:T(8,128)(2,1)S(1)}, bf16[19,2,16,128]{3,2,1,0:T(8,128)(2,1)S(1)}, u32[]{:S(2)}, u32[]{:S(2)}) collective-permute-start(bf16[19,2,16,128]{3,2,1,0:T(8,128)(2,1)S(1)} %bitcast.14), channel_id=1, source_target_pairs={{0,7},{1,0},{2,1},{3,2},{4,3},{5,4},{6,5},{7,6},{8,15},{9,8},{10,9... | collective-permute-start | bytes 466952 | tf_op jit(solution)/shard_map/ppermute | solution.py:540
  8.9 6.1 %copy-start.2 = (bf16[2,256,128]{2,1,0:T(8,128)(2,1)S(1)}, bf16[2,256,128]{2,1,0:T(8,128)(2,1)}, u32[]{:S(2)}) copy-start(bf16[2,256,128]{2,1,0:T(8,128)(2,1)} %constant.4.clone.reduce_ref) | copy-start | bytes 393220
  8.9 6.1 %copy-start.4 = (s32[2048]{0:T(1024)S(1)}, s32[2048]{0:T(1024)}, u32[]{:S(2)}) copy-start(s32[2048]{0:T(1024)} %param.8) | copy-start | bytes 24580
  8.9 6.1 %copy-start.5 = (s32[2048]{0:T(1024)S(1)}, s32[2048]{0:T(1024)}, u32[]{:S(2)}) copy-start(s32[2048]{0:T(1024)} %param.9) | copy-start | bytes 24580
  9.9 10.5 %collective-permute-start.2 = (bf16[19,40,128]{2,1,0:T(8,128)(2,1)S(1)}, bf16[19,40,128]{2,1,0:T(8,128)(2,1)S(1)}, u32[]{:S(2)}, u32[]{:S(2)}) collective-permute-start(bf16[19,40,128]{2,1,0:T(8,128)(2,1)S(1)} %get-tuple-element.21), channel_id=1, source_target_pairs={{0,8},{8,16},{16,24},{24,32},{32,40},{40,48},{48,56},{56,64},{64,7... | collective-permute-start | bytes 583688 | tf_op jit(solution)/shard_map/ppermute | solution.py:583
  11.3 9.1 %collective-permute-start.3 = (bf16[19,40,128]{2,1,0:T(8,128)(2,1)S(1)}, bf16[19,40,128]{2,1,0:T(8,128)(2,1)S(1)}, u32[]{:S(2)}, u32[]{:S(2)}) collective-permute-start(bf16[19,40,128]{2,1,0:T(8,128)(2,1)S(1)} %get-tuple-element.22), channel_id=1, source_target_pairs={{0,120},{8,0},{16,8},{24,16},{32,24},{40,32},{48,40},{56,48},{64,5... | collective-permute-start | bytes 583688 | tf_op jit(solution)/shard_map/ppermute | solution.py:584
  20.4 4.0 %copy-start = (bf16[6,608,256]{2,1,0:T(8,128)(2,1)}, bf16[6,608,256]{2,1,0:T(8,128)(2,1)S(1)}, u32[]{:S(2)}) copy-start(bf16[6,608,256]{2,1,0:T(8,128)(2,1)S(1)} %get-tuple-element.23.inner_ref) | copy-start | bytes 5603332
  24.3 44.0 %all-to-all-start = ((bf16[128,19,4,128]{3,2,1,0:T(4,128)(2,1)}), bf16[128,19,4,128]{3,2,1,0:T(4,128)(2,1)S(1)}, u32[]{:S(2)}, u32[]{:S(2)}) async-start(bf16[128,19,4,128]{3,2,1,0:T(4,128)(2,1)} %get-tuple-element.27), calls=%async_computation | async-start | bytes 4980736 | tf_op jit(solution)/shard_map/all_to_all | solution.py:633
  34.1 1.5 %copy-start.1 = (bf16[6,608,256]{2,1,0:T(8,128)(2,1)S(1)}, bf16[6,608,256]{2,1,0:T(8,128)(2,1)}, u32[]{:S(2)}) copy-start(bf16[6,608,256]{2,1,0:T(8,128)(2,1)} %copy-done) | copy-start | bytes 5603332
  35.6 32.8 %copy-start.3 = (bf16[256,512]{1,0:T(8,128)(2,1)S(1)}, bf16[256,512]{1,0:T(8,128)(2,1)}, u32[]{:S(2)}) copy-start(bf16[256,512]{1,0:T(8,128)(2,1)} %constant.5.clone.expand_ref) | copy-start | bytes 786436
